TPU v7x, 768 devices: a whole 4x8x12 slice. The times are simulated.
768 devices in a mesh: space: 64 (over x, y, core), chan: 12 (over z).
Axes of the slice: x: 4, y: 8, z: 12, core: 2. Of those that a mesh axis runs over, the one named last changes fastest.
Arguments:
- field: bfloat16 [288, 6144, 32], P('chan', 'space'), may hold values from -6 to 6
- grad_out: bfloat16 [288, 6144, 32], P('chan', 'space'), may hold values from -6 to 6
- filters: bfloat16 [9, 288, 288], replicated, may hold values from -0.125 to 0.125
Outputs:
- grad_field: float32 [288, 6144, 32], P('chan', 'space')
- grad_filters: float32 [9, 288, 288], P(None, 'chan')
All inputs are finite; a program needn't handle non-finite values.
Results may differ from a plain program's by a relative error of at most 0.0003.
Values may be sent and summed in bfloat16 or wider, within the bound.
No kernel may reach another device: no remote copies, remote signals or barrier semaphores. Data moves between devices by JAX's collectives and lax.ppermute only.
A program may use at most 64 MiB of HBM per device.

v0:
```python
import math

import jax
import jax.numpy as jnp
from jax import lax
from jax.sharding import PartitionSpec as P


def with_halo(cells, sides, width):
    for axis, dim in sides:
        count = lax.axis_size(axis)
        ends = count - 1
        head = lax.slice_in_dim(cells, 0, width, axis=dim)
        tail = lax.slice_in_dim(cells, cells.shape[dim] - width, cells.shape[dim], axis=dim)
        cells = jnp.concatenate(
            [
                lax.ppermute(tail, axis, [(i, (i + 1) % count) for i in range(ends)]),
                cells,
                lax.ppermute(head, axis, [((i + 1) % count, i) for i in range(ends)]),
            ],
            axis=dim,
        )
    return cells


def tap_terms(source, weights, padded, width, rows):
    result = jnp.zeros((weights.shape[1], width, rows), jnp.float32)
    parts = []
    for a in range(3):
        for b in range(3):
            k = a * 3 + b
            shifted = padded[:, 4 - 2 * a : 4 - 2 * a + width, 4 - 2 * b : 4 - 2 * b + rows]
            result = result + jnp.einsum(
                "io,owr->iwr", weights[k], shifted, preferred_element_type=jnp.float32
            )
            parts.append(
                jnp.einsum("iwr,owr->io", source, shifted, preferred_element_type=jnp.float32)
            )
    return (result, jnp.stack(parts))


def per_device(field, grad_out, filters):
    chan_dev = field.shape[0]
    width = field.shape[1]
    rows = field.shape[2]
    factor = 1.0 / math.sqrt(rows * width * lax.axis_size("space"))
    bordered = with_halo(grad_out, (("space", 1),), 2)
    first = lax.axis_index("chan") * chan_dev
    mine = lax.dynamic_slice_in_dim(filters, first, chan_dev, 1)
    padded = jnp.pad(lax.all_gather(bordered, "chan", axis=0, tiled=True), ((0, 0), (0, 0), (2, 2)))
    result, parts = tap_terms(field, mine, padded, width, rows)
    total = lax.psum(parts, "space")
    return (result, total * factor)


def solution(mesh):
    in_specs = (P("chan", "space", None), P("chan", "space", None), P())
    out_specs = (P("chan", "space", None), P(None, "chan", None))
    return jax.shard_map(
        per_device, mesh=mesh, in_specs=in_specs, out_specs=out_specs, check_vma=False
    )
```

profile of v0, /device:TPU:1, one launch (start us, length us, event | category | flops | bytes accessed | tf_op | source)
XLA Modules:
  0.0 307.8 jit_solution(16476392186810026551)
XLA Ops:
  7.2 0.0 all-gather.2.cloned.1.call-start
  7.2 1.1 copy.5
  8.4 0.1 fusion.156
  8.5 4.6 %collective-permute-start = (bf16[24,2,32]{1,0,2:T(8,128)(2,1)S(1)}, bf16[24,2,32]{1,0,2:T(8,128)(2,1)S(1)}, u32[]{:S(2)}, u32[]{:S(2)}) collective-permute-start(bf16[24,2,32]{1,0,2:T(8,128)(2,1)S(1)} %get-tuple-element.4), channel_id=1, source_target_pairs={{0,12},{12,24},{24,36},{36,48},{48,60},{60,72},{72,84},{84,96},{96... | collective-permute-start | bytes 9224 | tf_op jit(solution)/shard_map/ppermute | solution.py:17
  13.1 9.1 %collective-permute-start.1 = (bf16[24,2,32]{1,0,2:T(8,128)(2,1)S(1)}, bf16[24,2,32]{1,0,2:T(8,128)(2,1)S(1)}, u32[]{:S(2)}, u32[]{:S(2)}) collective-permute-start(bf16[24,2,32]{1,0,2:T(8,128)(2,1)S(1)} %get-tuple-element.5), channel_id=1, source_target_pairs={{12,0},{24,12},{36,24},{48,36},{60,48},{72,60},{84,72},{96,84},{10... | collective-permute-start | bytes 9224 | tf_op jit(solution)/shard_map/ppermute | solution.py:19
  22.2 1.0 collective-permute-done.1
  23.3 0.9 pad_maximum_fusion
  24.2 0.0 all-gather.2.cloned.1.call-update
  24.2 0.0 all-reduce.3.cloned.1.call-start
  24.3 59.5 %all-gather.2.cloned.1.call-done = bf16[288,100,32]{1,0,2:T(8,128)(2,1)} async-done(((bf16[24,100,32]{1,0,2:T(8,128)(2,1)}), bf16[288,100,32]{1,0,2:T(8,128)(2,1)}) %all-gather.2.cloned.1.call-update) | async-done | bytes 1843216 | tf_op jit(solution)/shard_map/all_gather | solution.py:50
  83.8 2.9 fusion.63
  86.7 1.1 fusion.99
  87.7 1.2 fusion.69
  88.9 1.1 fusion.75
  90.0 1.1 fusion.105
  91.1 1.2 fusion.81
  92.3 0.8 fusion.87
  93.0 0.8 fusion.111
  93.8 0.7 fusion.93
  94.6 0.7 copy-done.3
  95.3 2.6 fusion.10
  98.0 0.9 fusion.30
  98.9 0.9 fusion.22
  99.7 0.8 fusion.6
  100.5 0.5 fusion.2
  101.1 0.5 fusion.14
  101.6 0.9 fusion.57
  102.5 0.9 fusion.54
  103.4 0.5 fusion.48
  103.9 0.8 copy.17
  104.7 194.5 %all-reduce.3.cloned.1.call-done = f32[9,24,288]{2,1,0:T(8,128)} async-done(((f32[9,24,288]{2,1,0:T(8,128)}), f32[9,24,288]{2,1,0:T(8,128)}) %all-reduce.3.cloned.1.call-update) | async-done | bytes 248848 | tf_op jit(solution)/shard_map/psum | solution.py:52
  299.2 1.7 broadcast_multiply_fusion
  (11 shorter events, 0.1 us)
Async XLA Ops:
  7.2 88.2 %copy-start = (bf16[9,288,288]{2,1,0:T(8,128)(2,1)S(1)}, bf16[9,288,288]{2,1,0:T(8,128)(2,1)}, u32[]{:S(2)}) copy-start(bf16[9,288,288]{2,1,0:T(8,128)(2,1)} %param.5) | copy-start | bytes 4478980
  7.2 76.6 %all-gather.2.cloned.1.call-start = ((), (), s32[]{:S(2)}) async-start(), calls=%async_computation | async-start | bytes 2555904 | tf_op jit(solution)/shard_map/all_gather | solution.py:50
  8.5 13.7 %collective-permute-start = (bf16[24,2,32]{1,0,2:T(8,128)(2,1)S(1)}, bf16[24,2,32]{1,0,2:T(8,128)(2,1)S(1)}, u32[]{:S(2)}, u32[]{:S(2)}) collective-permute-start(bf16[24,2,32]{1,0,2:T(8,128)(2,1)S(1)} %get-tuple-element.4), channel_id=1, source_target_pairs={{0,12},{12,24},{24,36},{36,48},{48,60},{60,72},{72,84},{84,96},{96... | collective-permute-start | bytes 9224 | tf_op jit(solution)/shard_map/ppermute | solution.py:17
  13.1 10.2 %collective-permute-start.1 = (bf16[24,2,32]{1,0,2:T(8,128)(2,1)S(1)}, bf16[24,2,32]{1,0,2:T(8,128)(2,1)S(1)}, u32[]{:S(2)}, u32[]{:S(2)}) collective-permute-start(bf16[24,2,32]{1,0,2:T(8,128)(2,1)S(1)} %get-tuple-element.5), channel_id=1, source_target_pairs={{12,0},{24,12},{36,24},{48,36},{60,48},{72,60},{84,72},{96,84},{10... | collective-permute-start | bytes 9224 | tf_op jit(solution)/shard_map/ppermute | solution.py:19
  24.2 275.0 %all-reduce.3.cloned.1.call-start = ((), (), s32[]{:S(2)}) async-start(), calls=%async_computation.1 | async-start | bytes 663552 | tf_op jit(solution)/shard_map/psum | solution.py:52
  24.2 62.4 %copy-start.4 = (bf16[24,96,32]{1,2,0:T(8,128)(2,1)S(1)}, bf16[24,96,32]{1,2,0:T(8,128)(2,1)}, u32[]{:S(2)}) copy-start(bf16[24,96,32]{1,2,0:T(8,128)(2,1)} %param.3) | copy-start | bytes 442372
  83.8 2.9 copy-start.1
  94.6 0.7 copy-start.3
  95.3 2.6 copy-start.2
Sparse Core Ops, SparseCore 0:
  24.3 59.4 all-gather.1
  95.4 203.7 all-reduce.2
where the time goes:
time: 308 us
  waiting for transfers between devices  255 us (83%)
  matrix products  19.3 us (6%)
  between operations  14.2 us (5%)
  starting transfers between devices  13.8 us (4%)
    psum x1, waiting for transfers between devices, per_device(): total = lax.psum(parts, 'space')  195 us
    all_gather x1, waiting for transfers between devices, per_device(): lax.all_gather(bordered, 'chan', axis=0, tiled=True)  59.5 us
    dot_general x9, matrix products, tap_terms(): jnp.einsum('iwr,owr->io', source, shifted, preferred_element_type=jnp.flo...  10.8 us
    ppermute x1, starting transfers between devices, with_halo(): lax.ppermute(head, axis, [((i + 1) % count, i) for i in range(ends)])  9.13 us
    dot_general x9, matrix products, tap_terms(): jnp.einsum('io,owr->iwr', weights[k], shifted, preferred_element_type=jnp...  8.51 us
  transfers between devices with their start and end apart: 4, of which 3 were waited for; matrix products, arithmetic and copies ran while one was open for 3% of the time, Pallas kernels for 0%

commit v1 on v0

v1 whole, which is shorter than its diff:
```python
import math

import jax
import jax.numpy as jnp
from jax import lax
from jax.sharding import PartitionSpec as P

NX, NY, NCORE = 4, 8, 2


def group_lists():
    def at(x, y, core):
        return (x * NY + y) * NCORE + core

    across = [[at(x, y, c) for x in range(NX) for c in range(NCORE)] for y in range(NY)]
    along = [[at(x, y, c) for y in range(NY)] for x in range(NX) for c in range(NCORE)]
    return across, along


def per_device(field, grad_out, filters):
    across, along = group_lists()
    spaces = lax.axis_size("space")
    chans = lax.axis_size("chan")
    chan_dev, width, rows = field.shape
    factor = 1.0 / math.sqrt(rows * width * spaces)
    layer = lax.axis_index("chan")

    def move(cells, step):
        return lax.ppermute(cells, "chan", [(i, (i + step) % chans) for i in range(chans)])

    def spread(piece, groups):
        stacked = jnp.broadcast_to(piece[None], (8,) + piece.shape)
        return lax.all_to_all(stacked, "space", 0, 0, axis_index_groups=groups, tiled=True)

    source = field.transpose(0, 2, 1)
    cells = grad_out.transpose(0, 2, 1)
    left = lax.ppermute(cells[:, :, -2:], "space", [(i, i + 1) for i in range(spaces - 1)])
    right = lax.ppermute(cells[:, :, :2], "space", [(i + 1, i) for i in range(spaces - 1)])
    sources = [move(source, 1), source, move(source, -1), move(source, -2)]
    bordered = jnp.concatenate([left, cells, right], axis=2)
    grads = jnp.stack([move(bordered, 4), bordered, move(bordered, -4)])
    third = layer // 4
    grads = jnp.concatenate(
        [lax.dynamic_index_in_dim(grads, (m - third + 4) % 3, 0, False) for m in range(3)]
    )
    padded = jnp.pad(grads, ((0, 0), (2, 2), (0, 0)))
    window = jnp.concatenate(sources)

    first, last = filters[:, : 2 * chan_dev], filters[:, -chan_dev:]
    own = jnp.concatenate([last, filters, first], axis=1)
    own = lax.dynamic_slice_in_dim(own, layer * chan_dev, 4 * chan_dev, 1)
    lane = jnp.arange(3 * chan_dev)
    wanted = (4 * (lane // chan_dev) + layer % 4) * chan_dev + lane % chan_dev
    chosen = (jnp.arange(12 * chan_dev)[:, None] == wanted[None, :]).astype(filters.dtype)
    own = jnp.einsum("kio,op->kip", own, chosen, preferred_element_type=jnp.float32)
    own = own.astype(filters.dtype).reshape(3, 3, 4 * chan_dev, 3 * chan_dev)

    parts = []
    result = jnp.zeros((4 * chan_dev, rows, width), jnp.float32)
    for b in range(3):
        row = []
        for a in range(3):
            shifted = padded[:, 4 - 2 * b : 4 - 2 * b + rows, 4 - 2 * a : 4 - 2 * a + width]
            row.append(
                jnp.einsum("irw,orw->io", window, shifted, preferred_element_type=jnp.float32)
            )
            result = result + jnp.einsum(
                "io,orw->irw", own[a, b], shifted, preferred_element_type=jnp.float32
            )
        parts.append(jnp.pad(jnp.concatenate(row, axis=1), ((0, 0), (0, 40))))
    parts = jnp.stack(parts).reshape(3, 4, chan_dev, 2, 128)
    parts = parts.transpose(1, 3, 0, 2, 4).reshape(8, 3 * chan_dev, 128)

    piece = lax.all_to_all(parts, "space", 0, 0, axis_index_groups=across, tiled=True).sum(0)
    home = [
        (s * chans + c, s * chans + (c - 1 + s // (NY * NCORE)) % chans)
        for s in range(spaces)
        for c in range(chans)
    ]
    piece = lax.ppermute(piece, ("space", "chan"), home)
    piece = spread(piece, along).sum(0)
    whole = spread(piece, across).reshape(4, 2, 3, chan_dev, 128)
    whole = whole.transpose(0, 2, 3, 1, 4).reshape(4, 3, chan_dev, 256)[..., :216]
    whole = whole.reshape(4, 3, chan_dev, 3, 3, chan_dev)
    whole = jnp.stack(
        [lax.dynamic_index_in_dim(whole, (layer + 1 - v + 4) % 4, 0, False) for v in range(4)]
    )
    whole = whole.transpose(3, 1, 2, 4, 0, 5)
    grad_filters = whole.reshape(9, chan_dev, 12 * chan_dev) * factor

    blocks = result.reshape(4, chan_dev, rows, width)
    total = blocks[1] + move(blocks[0], -1) + move(blocks[2], 1) + move(blocks[3], 2)
    return (total.transpose(0, 2, 1), grad_filters)


def solution(mesh):
    in_specs = (P("chan", "space", None), P("chan", "space", None), P())
    out_specs = (P("chan", "space", None), P(None, "chan", None))
    return jax.shard_map(
        per_device, mesh=mesh, in_specs=in_specs, out_specs=out_specs, check_vma=False
    )
```

time: 308 us -> 154 us (0.50)
  waiting for transfers between devices: 255 us -> 35 us
  starting transfers between devices: 13.8 us -> 70.3 us
  matrix products: 19.3 us -> 33.4 us
  between operations: 14.2 us -> 1.26 us
  local copies, waits for them, and re-layouts: 2.85 us -> 9.47 us
    psum x1 -> x0, waiting for transfers between devices: 195 us -> none  [per_device(): total = lax.psum(parts, 'space')]
    all_gather x1 -> x0, waiting for transfers between devices: 59.5 us -> none  [per_device(): lax.all_gather(bordered, 'chan', axis=0, tiled=True)]
    ppermute x2 -> x11, starting transfers between devices: 13.7 us -> 54.5 us  [the longest x8 42.6 us: move(): lax.ppermute(cells, 'chan', [(i, (i + step) % chans) for i in range(chans)])]
    ppermute x2 -> x11, waiting for transfers between devices: 1.04 us -> 29.8 us  [the longest x8 27.4 us: move(): lax.ppermute(cells, 'chan', [(i, (i + step) % chans) for i in range(chans)])]
    all_to_all x0 -> x3, starting transfers between devices: none -> 15.8 us  [the longest x2 10 us: spread(): lax.all_to_all(stacked, 'space', 0, 0, axis_index_groups=groups, tiled=True)]
    dot_general x18 -> x19, matrix products: 19.3 us -> 33.4 us  [the longest x9 18.6 us: per_device(): jnp.einsum('io,orw->irw', own[a, b], shifted, preferred_element_type=jnp....]
    all_to_all x0 -> x3, waiting for transfers between devices: none -> 5.17 us  [the longest x1 5.16 us: per_device(): lax.all_to_all(parts, 'space', 0, 0, axis_index_groups=across, tiled=True)]
  transfers between devices with their start and end apart: 4 -> 14, of which waited for: 3 -> 6; matrix products, arithmetic and copies ran while one was open for 3% -> 16% of each run, Pallas kernels for 0% -> 0%
where the time goes in v1:
time: 154 us; the launch traced here: 153 us
  starting transfers between devices  70.3 us (46%)
  waiting for transfers between devices  35 us (23%)
  matrix products  33.4 us (22%)
  local copies, waits for them, and re-layouts  9.47 us (6%)
  other arithmetic  3.45 us (2%)
    ppermute x8, starting transfers between devices, move(): lax.ppermute(cells, 'chan', [(i, (i + step) % chans) for i in range(chans)])  42.6 us
    ppermute x8, waiting for transfers between devices, move(): lax.ppermute(cells, 'chan', [(i, (i + step) % chans) for i in range(chans)])  27.4 us
    dot_general x9, matrix products, per_device(): jnp.einsum('io,orw->irw', own[a, b], shifted, preferred_element_type=jnp....  18.6 us
    dot_general x9, matrix products, per_device(): jnp.einsum('irw,orw->io', window, shifted, preferred_element_type=jnp.flo...  14.3 us
    all_to_all x2, starting transfers between devices, spread(): lax.all_to_all(stacked, 'space', 0, 0, axis_index_groups=groups, tiled=True)  10 us
    all_to_all x1, starting transfers between devices, per_device(): lax.all_to_all(parts, 'space', 0, 0, axis_index_groups=across, tiled=True)  5.75 us
    ppermute x1, starting transfers between devices, per_device(): piece = lax.ppermute(piece, ('space', 'chan'), home)  5.34 us
    all_to_all x1, waiting for transfers between devices, per_device(): lax.all_to_all(parts, 'space', 0, 0, axis_index_groups=across, tiled=True)  5.16 us
  transfers between devices with their start and end apart: 14, of which 6 were waited for; matrix products, arithmetic and copies ran while one was open for 16% of the time, Pallas kernels for 0%

profile of v1, /device:TPU:1, one launch (start us, length us, event | category | flops | bytes accessed | tf_op | source)
XLA Modules:
  0.0 152.9 jit_solution(7075303452621359429)
XLA Ops:
  1.8 15.1 %collective-permute-start.9 = (bf16[24,32,96]{2,0,1:T(8,128)(2,1)S(1)}, bf16[24,32,96]{2,0,1:T(8,128)(2,1)}, u32[]{:S(2)}, u32[]{:S(2)}) collective-permute-start(bf16[24,32,96]{2,0,1:T(8,128)(2,1)S(1)} %bitcast.106), channel_id=1, source_target_pairs={{0,10},{1,11},{2,0},{3,1},{4,2},{5,3},{6,4},{7,5},{8,6},{9,7},{10,... | collective-permute-start | bytes 442376 | tf_op jit(solution)/shard_map/ppermute | solution.py:29
  17.0 2.2 %collective-permute-start.8 = (bf16[24,32,96]{2,0,1:T(8,128)(2,1)S(1)}, bf16[24,32,96]{2,0,1:T(8,128)(2,1)}, u32[]{:S(2)}, u32[]{:S(2)}) collective-permute-start(bf16[24,32,96]{2,0,1:T(8,128)(2,1)S(1)} %bitcast.107), channel_id=1, source_target_pairs={{0,11},{1,0},{2,1},{3,2},{4,3},{5,4},{6,5},{7,6},{8,7},{9,8},{10,9... | collective-permute-start | bytes 442376 | tf_op jit(solution)/shard_map/ppermute | solution.py:29
  19.2 3.1 %collective-permute-start.7 = (bf16[24,32,96]{2,0,1:T(8,128)(2,1)S(1)}, bf16[24,32,96]{2,0,1:T(8,128)(2,1)}, u32[]{:S(2)}, u32[]{:S(2)}) collective-permute-start(bf16[24,32,96]{2,0,1:T(8,128)(2,1)S(1)} %bitcast.108), channel_id=1, source_target_pairs={{0,1},{1,2},{2,3},{3,4},{4,5},{5,6},{6,7},{7,8},{8,9},{9,10},{10,1... | collective-permute-start | bytes 442376 | tf_op jit(solution)/shard_map/ppermute | solution.py:29
  23.4 3.4 %collective-permute-start.1 = (bf16[24,32,2]{2,1,0:T(8,128)(2,1)S(1)}, bf16[24,32,2]{2,1,0:T(8,128)(2,1)S(1)}, u32[]{:S(2)}, u32[]{:S(2)}) collective-permute-start(bf16[24,32,2]{2,1,0:T(8,128)(2,1)S(1)} %get-tuple-element.21), channel_id=1, source_target_pairs={{12,0},{24,12},{36,24},{48,36},{60,48},{72,60},{84,72},{96,84},{10... | collective-permute-start | bytes 9224 | tf_op jit(solution)/shard_map/ppermute | solution.py:38
  26.8 3.1 %collective-permute-start = (bf16[24,32,2]{2,1,0:T(8,128)(2,1)S(1)}, bf16[24,32,2]{2,1,0:T(8,128)(2,1)}, u32[]{:S(2)}, u32[]{:S(2)}) collective-permute-start(bf16[24,32,2]{2,1,0:T(8,128)(2,1)S(1)} %get-tuple-element.20), channel_id=1, source_target_pairs={{0,12},{12,24},{24,36},{36,48},{48,60},{60,72},{72,84},{84,96},{96... | collective-permute-start | bytes 9224 | tf_op jit(solution)/shard_map/ppermute | solution.py:37
  33.7 2.8 %collective-permute-start.3 = (bf16[24,32,100]{2,1,0:T(8,128)(2,1)S(1)}, bf16[24,32,100]{2,1,0:T(8,128)(2,1)S(1)}, u32[]{:S(2)}, u32[]{:S(2)}) collective-permute-start(bf16[24,32,100]{2,1,0:T(8,128)(2,1)S(1)} %pad_maximum_fusion.3), channel_id=1, source_target_pairs={{0,8},{1,9},{2,10},{3,11},{4,0},{5,1},{6,2},{7,3},{8,4},{9,5},{10,... | collective-permute-start | bytes 460808 | tf_op jit(solution)/shard_map/ppermute | solution.py:29
  36.5 6.4 %collective-permute-start.2 = (bf16[24,32,100]{2,1,0:T(8,128)(2,1)S(1)}, bf16[24,32,100]{2,1,0:T(8,128)(2,1)S(1)}, u32[]{:S(2)}, u32[]{:S(2)}) collective-permute-start(bf16[24,32,100]{2,1,0:T(8,128)(2,1)S(1)} %pad_maximum_fusion.3), channel_id=1, source_target_pairs={{0,4},{1,5},{2,6},{3,7},{4,8},{5,9},{6,10},{7,11},{8,0},{9,1},{10,... | collective-permute-start | bytes 460808 | tf_op jit(solution)/shard_map/ppermute | solution.py:29
  43.5 13.7 %collective-permute-done.3 = bf16[24,32,100]{2,1,0:T(8,128)(2,1)S(1)} collective-permute-done((bf16[24,32,100]{2,1,0:T(8,128)(2,1)S(1)}, bf16[24,32,100]{2,1,0:T(8,128)(2,1)S(1)}, u32[]{:S(2)}, u32[]{:S(2)}) %collective-permute-start.3) | collective-permute-done | bytes 153632 | tf_op jit(solution)/shard_map/ppermute | solution.py:29
  57.7 1.6 %fusion.16 = f32[96,32,96]{2,0,1:T(8,128)} fusion(bf16[72,32,100]{2,0,1:T(8,128)(2,1)S(1)} %pad_maximum_fusion.2, bf16[3,3,96,72]{2,3,1,0:T(8,128)(2,1)S(1)} %bitcast.118), kind=kOutput, calls=%fused_computation.33 | convolution fusion | flops 42467328 | bytes 1787904 | tf_op jit(solution)/shard_map/io,orw->irw/dot_general | solution.py:67
  59.3 1.6 %fusion.19 = f32[96,32,96]{2,0,1:T(8,128)} fusion(bf16[72,32,100]{2,0,1:T(8,128)(2,1)S(1)} %pad_maximum_fusion.2, bf16[3,3,96,72]{2,3,1,0:T(8,128)(2,1)S(1)} %bitcast.119), kind=kOutput, calls=%fused_computation.36 | convolution fusion | flops 42467328 | bytes 1787904 | tf_op jit(solution)/shard_map/io,orw->irw/dot_general | solution.py:67
  62.5 1.7 %fusion.8 = f32[96,32,96]{2,0,1:T(8,128)} fusion(bf16[72,32,100]{2,0,1:T(8,128)(2,1)S(1)} %pad_maximum_fusion.2, bf16[3,3,96,72]{2,3,1,0:T(8,128)(2,1)S(1)} %bitcast.121), kind=kOutput, calls=%fused_computation.25 | convolution fusion | flops 42467328 | bytes 1787904 | tf_op jit(solution)/shard_map/io,orw->irw/dot_general | solution.py:67
  64.2 1.7 %fusion.11 = f32[96,32,96]{2,0,1:T(8,128)} fusion(bf16[72,32,100]{2,0,1:T(8,128)(2,1)S(1)} %pad_maximum_fusion.2, bf16[3,3,96,72]{2,3,1,0:T(8,128)(2,1)S(1)} %bitcast.122), kind=kOutput, calls=%fused_computation.28 | convolution fusion | flops 42467328 | bytes 1787904 | tf_op jit(solution)/shard_map/io,orw->irw/dot_general | solution.py:67
  65.8 1.7 %fusion.22 = f32[96,32,96]{2,0,1:T(8,128)} fusion(bf16[72,32,100]{2,0,1:T(8,128)(2,1)S(1)} %pad_maximum_fusion.2, bf16[3,3,96,72]{2,3,1,0:T(8,128)(2,1)S(1)} %bitcast.123), kind=kOutput, calls=%fused_computation.39 | convolution fusion | flops 42467328 | bytes 1787904 | tf_op jit(solution)/shard_map/io,orw->irw/dot_general | solution.py:67
  67.5 1.6 %fusion.28 = f32[96,32,96]{2,0,1:T(8,128)} fusion(bf16[72,32,100]{2,0,1:T(8,128)(2,1)S(1)} %pad_maximum_fusion.2, bf16[3,3,96,72]{2,3,1,0:T(8,128)(2,1)S(1)} %bitcast.124), kind=kOutput, calls=%fused_computation.45 | convolution fusion | flops 42467328 | bytes 1787904 | tf_op jit(solution)/shard_map/io,orw->irw/dot_general | solution.py:67
  70.6 1.6 %convolution_bitcast_fusion.1 = f32[96,72]{0,1:T(8,128)S(1)} fusion(bf16[72,32,100]{2,0,1:T(8,128)(2,1)S(1)} %pad_maximum_fusion.2, bf16[24,32,96]{2,0,1:T(8,128)(2,1)} %collective-permute-done.9, bf16[24,32,96]{2,0,1:T(8,128)(2,1)} %collective-permute-done.8, bf16[24,32,96]{2,0,1:T(8,128)(2,1)S(1)} %bitcast.110, bf16[24,32,96]{2,0,1:T(8,128)(2,1)} %collective-permute-done.7), kind=kOutput, calls=%fused_computation.8 | convolution fusion | flops 44826624 | bytes 1078272 | tf_op jit(solution)/shard_map/irw,orw->io/dot_general | solution.py:65
  72.2 1.6 %convolution_bitcast_fusion.2 = f32[96,72]{0,1:T(8,128)S(1)} fusion(bf16[72,32,100]{2,0,1:T(8,128)(2,1)S(1)} %pad_maximum_fusion.2, bf16[24,32,96]{2,0,1:T(8,128)(2,1)} %collective-permute-done.9, bf16[24,32,96]{2,0,1:T(8,128)(2,1)} %collective-permute-done.8, bf16[24,32,96]{2,0,1:T(8,128)(2,1)S(1)} %bitcast.111, bf16[24,32,96]{2,0,1:T(8,128)(2,1)} %collective-permute-done.7), kind=kOutput, calls=%fused_computation.9 | convolution fusion | flops 44826624 | bytes 1078272 | tf_op jit(solution)/shard_map/irw,orw->io/dot_general | solution.py:65
  75.5 1.6 %convolution_bitcast_fusion.4 = f32[96,72]{0,1:T(8,128)S(1)} fusion(bf16[72,32,100]{2,0,1:T(8,128)(2,1)S(1)} %pad_maximum_fusion.2, bf16[24,32,96]{2,0,1:T(8,128)(2,1)} %collective-permute-done.9, bf16[24,32,96]{2,0,1:T(8,128)(2,1)} %collective-permute-done.8, bf16[24,32,96]{2,0,1:T(8,128)(2,1)S(1)} %bitcast.113, bf16[24,32,96]{2,0,1:T(8,128)(2,1)} %collective-permute-done.7), kind=kOutput, calls=%fused_computation.11 | convolution fusion | flops 44826624 | bytes 1078272 | tf_op jit(solution)/shard_map/irw,orw->io/dot_general | solution.py:65
  77.2 1.6 %convolution_bitcast_fusion.5 = f32[96,72]{0,1:T(8,128)S(1)} fusion(bf16[72,32,100]{2,0,1:T(8,128)(2,1)S(1)} %pad_maximum_fusion.2, bf16[24,32,96]{2,0,1:T(8,128)(2,1)} %collective-permute-done.9, bf16[24,32,96]{2,0,1:T(8,128)(2,1)} %collective-permute-done.8, bf16[24,32,96]{2,0,1:T(8,128)(2,1)S(1)} %bitcast.114, bf16[24,32,96]{2,0,1:T(8,128)(2,1)} %collective-permute-done.7), kind=kOutput, calls=%fused_computation.12 | convolution fusion | flops 44826624 | bytes 1078272 | tf_op jit(solution)/shard_map/irw,orw->io/dot_general | solution.py:65
  80.5 1.7 %convolution_bitcast_fusion.7 = f32[96,72]{0,1:T(8,128)S(1)} fusion(bf16[72,32,100]{2,0,1:T(8,128)(2,1)S(1)} %pad_maximum_fusion.2, bf16[24,32,96]{2,0,1:T(8,128)(2,1)} %collective-permute-done.9, bf16[24,32,96]{2,0,1:T(8,128)(2,1)} %collective-permute-done.8, bf16[24,32,96]{2,0,1:T(8,128)(2,1)S(1)} %bitcast.116, bf16[24,32,96]{2,0,1:T(8,128)(2,1)} %collective-permute-done.7), kind=kOutput, calls=%fused_computation.14 | convolution fusion | flops 44826624 | bytes 1078272 | tf_op jit(solution)/shard_map/irw,orw->io/dot_general | solution.py:65
  82.2 1.6 %convolution_bitcast_fusion.8 = f32[96,72]{0,1:T(8,128)S(1)} fusion(bf16[72,32,100]{2,0,1:T(8,128)(2,1)S(1)} %pad_maximum_fusion.2, bf16[24,32,96]{2,0,1:T(8,128)(2,1)} %collective-permute-done.9, bf16[24,32,96]{2,0,1:T(8,128)(2,1)} %collective-permute-done.8, bf16[24,32,96]{2,0,1:T(8,128)(2,1)S(1)} %bitcast.117, bf16[24,32,96]{2,0,1:T(8,128)(2,1)} %collective-permute-done.7), kind=kOutput, calls=%fused_computation.15 | convolution fusion | flops 44826624 | bytes 1078272 | tf_op jit(solution)/shard_map/irw,orw->io/dot_general | solution.py:65
  84.9 5.7 %all-to-all-start = ((f32[8,72,128]{2,1,0:T(8,128)}), f32[8,72,128]{2,1,0:T(8,128)S(1)}, u32[]{:S(2)}, u32[]{:S(2)}) async-start(f32[8,72,128]{2,1,0:T(8,128)} %bitcast.39), calls=%async_computation | async-start | bytes 589824 | tf_op jit(solution)/shard_map/all_to_all | solution.py:74
  90.6 1.6 %fusion.25 = f32[96,32,96]{2,0,1:T(8,128)} fusion(bf16[72,32,100]{2,0,1:T(8,128)(2,1)S(1)} %pad_maximum_fusion.2, bf16[3,3,96,72]{2,3,1,0:T(8,128)(2,1)S(1)} %bitcast.125), kind=kOutput, calls=%fused_computation.42 | convolution fusion | flops 42467328 | bytes 1787904 | tf_op jit(solution)/shard_map/io,orw->irw/dot_general | solution.py:67
  92.3 5.2 %all-to-all-done = f32[8,72,128]{2,1,0:T(8,128)S(1)} async-done(((f32[8,72,128]{2,1,0:T(8,128)}), f32[8,72,128]{2,1,0:T(8,128)S(1)}, u32[]{:S(2)}, u32[]{:S(2)}) %all-to-all-start) | async-done | bytes 294944 | tf_op jit(solution)/shard_map/all_to_all | solution.py:74
  97.5 5.3 %collective-permute-start.10 = (f32[72,128]{1,0:T(8,128)S(1)}, f32[72,128]{1,0:T(8,128)S(1)}, u32[]{:S(2)}, u32[]{:S(2)}) collective-permute-start(f32[72,128]{1,0:T(8,128)S(1)} %reduce_sum.18), channel_id=1, source_target_pairs={{0,11},{1,0},{2,1},{3,2},{4,3},{5,4},{6,5},{7,6},{8,7},{9,8},{10,9... | collective-permute-start | bytes 110600 | tf_op jit(solution)/shard_map/ppermute | solution.py:80
  102.8 5.5 %add_add_fusion = f32[96,32,96]{2,0,1:T(8,128)S(1)} fusion(f32[96,32,96]{2,0,1:T(8,128)} %fusion.16, f32[96,32,96]{2,0,1:T(8,128)} %fusion.19, f32[96,32,96]{2,0,1:T(8,128)} %fusion.5, f32[96,32,96]{2,0,1:T(8,128)} %fusion.8, f32[96,32,96]{2,0,1:T(8,128)} %fusion.11, f32[96,32,96]{2,0,1:T(8,128)} %fusion.22, f32[96,32,96]{2,0,1:T(8,128)} %fusion.28, ...), kind=kOutput, calls=%fused_computation.5 | convolution fusion | flops 44826624 | bytes 11225088 | tf_op jit(solution)/shard_map/io,orw->irw/dot_general | solution.py:67
  109.1 4.1 %all-to-all-start.1 = ((f32[8,72,128]{2,1,0:T(8,128)}), f32[8,72,128]{2,1,0:T(8,128)S(1)}, u32[]{:S(2)}, u32[]{:S(2)}) async-start(f32[8,72,128]{2,1,0:T(8,128)} %broadcast_in_dim.4), calls=%async_computation.1 | async-start | bytes 589824 | tf_op jit(solution)/shard_map/all_to_all | solution.py:33
  113.3 6.5 %collective-permute-start.6 = (f32[24,32,96]{2,0,1:T(8,128)S(1)}, f32[24,32,96]{2,0,1:T(8,128)S(1)}, u32[]{:S(2)}, u32[]{:S(2)}) collective-permute-start(f32[24,32,96]{2,0,1:T(8,128)S(1)} %get-tuple-element.15), channel_id=1, source_target_pairs={{0,2},{1,3},{2,4},{3,5},{4,6},{5,7},{6,8},{7,9},{8,10},{9,11},{10,... | collective-permute-start | bytes 884744 | tf_op jit(solution)/shard_map/ppermute | solution.py:29
  119.9 1.9 %collective-permute-start.5 = (f32[24,32,96]{2,0,1:T(8,128)S(1)}, f32[24,32,96]{2,0,1:T(8,128)}, u32[]{:S(2)}, u32[]{:S(2)}) collective-permute-start(f32[24,32,96]{2,0,1:T(8,128)S(1)} %get-tuple-element.16), channel_id=1, source_target_pairs={{0,1},{1,2},{2,3},{3,4},{4,5},{5,6},{6,7},{7,8},{8,9},{9,10},{10,1... | collective-permute-start | bytes 884744 | tf_op jit(solution)/shard_map/ppermute | solution.py:29
  121.8 4.6 %collective-permute-start.4 = (f32[24,32,96]{2,0,1:T(8,128)S(1)}, f32[24,32,96]{2,0,1:T(8,128)}, u32[]{:S(2)}, u32[]{:S(2)}) collective-permute-start(f32[24,32,96]{2,0,1:T(8,128)S(1)} %get-tuple-element.14), channel_id=1, source_target_pairs={{0,11},{1,0},{2,1},{3,2},{4,3},{5,4},{6,5},{7,6},{8,7},{9,8},{10,9... | collective-permute-start | bytes 884744 | tf_op jit(solution)/shard_map/ppermute | solution.py:29
  127.2 5.9 %all-to-all-start.2 = ((f32[8,72,128]{2,1,0:T(8,128)}), f32[8,72,128]{2,1,0:T(8,128)S(1)}, u32[]{:S(2)}, u32[]{:S(2)}) async-start(f32[8,72,128]{2,1,0:T(8,128)} %broadcast_in_dim.5), calls=%async_computation.2 | async-start | bytes 589824 | tf_op jit(solution)/shard_map/all_to_all | solution.py:33
  133.1 3.9 %collective-permute-done.6 = f32[24,32,96]{2,0,1:T(8,128)S(1)} collective-permute-done((f32[24,32,96]{2,0,1:T(8,128)S(1)}, f32[24,32,96]{2,0,1:T(8,128)S(1)}, u32[]{:S(2)}, u32[]{:S(2)}) %collective-permute-start.6) | collective-permute-done | bytes 294944 | tf_op jit(solution)/shard_map/ppermute | solution.py:29
  137.0 9.8 %collective-permute-done.5 = f32[24,32,96]{2,0,1:T(8,128)} collective-permute-done((f32[24,32,96]{2,0,1:T(8,128)S(1)}, f32[24,32,96]{2,0,1:T(8,128)}, u32[]{:S(2)}, u32[]{:S(2)}) %collective-permute-start.5) | collective-permute-done | bytes 294944 | tf_op jit(solution)/shard_map/ppermute | solution.py:29
  (59 shorter events, 22.1 us)
Async XLA Ops:
  0.6 31.9 %copy-start = (bf16[24,96,32]{1,2,0:T(8,128)(2,1)S(1)}, bf16[24,96,32]{1,2,0:T(8,128)(2,1)}, u32[]{:S(2)}) copy-start(bf16[24,96,32]{1,2,0:T(8,128)(2,1)} %param.4) | copy-start | bytes 442372
  0.6 42.2 %copy-start.1 = (bf16[9,288,288]{2,1,0:T(8,128)(2,1)S(1)}, bf16[9,288,288]{2,1,0:T(8,128)(2,1)}, u32[]{:S(2)}) copy-start(bf16[9,288,288]{2,1,0:T(8,128)(2,1)} %param.5) | copy-start | bytes 4478980
  0.7 42.2 %slice-start = ((bf16[9,288,288]{2,1,0:T(8,128)(2,1)}), bf16[9,24,288]{2,1,0:T(8,128)(2,1)S(1)}, s32[]{:S(2)}) async-start(bf16[9,288,288]{2,1,0:T(8,128)(2,1)} %param.5), calls=%async_computation.3 | async-start | bytes 331776 | tf_op jit(solution)/shard_map/slice | solution.py:49
  0.7 42.2 %slice-start.1 = ((bf16[9,288,288]{2,1,0:T(8,128)(2,1)}), bf16[9,48,288]{2,1,0:T(8,128)(2,1)S(1)}, s32[]{:S(2)}) async-start(bf16[9,288,288]{2,1,0:T(8,128)(2,1)} %param.5), calls=%async_computation.4 | async-start | bytes 663552 | tf_op jit(solution)/shard_map/slice | solution.py:49
  1.8 67.3 %collective-permute-start.9 = (bf16[24,32,96]{2,0,1:T(8,128)(2,1)S(1)}, bf16[24,32,96]{2,0,1:T(8,128)(2,1)}, u32[]{:S(2)}, u32[]{:S(2)}) collective-permute-start(bf16[24,32,96]{2,0,1:T(8,128)(2,1)S(1)} %bitcast.106), channel_id=1, source_target_pairs={{0,10},{1,11},{2,0},{3,1},{4,2},{5,3},{6,4},{7,5},{8,6},{9,7},{10,... | collective-permute-start | bytes 442376 | tf_op jit(solution)/shard_map/ppermute | solution.py:29
  17.0 52.1 %collective-permute-start.8 = (bf16[24,32,96]{2,0,1:T(8,128)(2,1)S(1)}, bf16[24,32,96]{2,0,1:T(8,128)(2,1)}, u32[]{:S(2)}, u32[]{:S(2)}) collective-permute-start(bf16[24,32,96]{2,0,1:T(8,128)(2,1)S(1)} %bitcast.107), channel_id=1, source_target_pairs={{0,11},{1,0},{2,1},{3,2},{4,3},{5,4},{6,5},{7,6},{8,7},{9,8},{10,9... | collective-permute-start | bytes 442376 | tf_op jit(solution)/shard_map/ppermute | solution.py:29
  19.2 49.9 %collective-permute-start.7 = (bf16[24,32,96]{2,0,1:T(8,128)(2,1)S(1)}, bf16[24,32,96]{2,0,1:T(8,128)(2,1)}, u32[]{:S(2)}, u32[]{:S(2)}) collective-permute-start(bf16[24,32,96]{2,0,1:T(8,128)(2,1)S(1)} %bitcast.108), channel_id=1, source_target_pairs={{0,1},{1,2},{2,3},{3,4},{4,5},{5,6},{6,7},{7,8},{8,9},{9,10},{10,1... | collective-permute-start | bytes 442376 | tf_op jit(solution)/shard_map/ppermute | solution.py:29
  23.4 8.0 %collective-permute-start.1 = (bf16[24,32,2]{2,1,0:T(8,128)(2,1)S(1)}, bf16[24,32,2]{2,1,0:T(8,128)(2,1)S(1)}, u32[]{:S(2)}, u32[]{:S(2)}) collective-permute-start(bf16[24,32,2]{2,1,0:T(8,128)(2,1)S(1)} %get-tuple-element.21), channel_id=1, source_target_pairs={{12,0},{24,12},{36,24},{48,36},{60,48},{72,60},{84,72},{96,84},{10... | collective-permute-start | bytes 9224 | tf_op jit(solution)/shard_map/ppermute | solution.py:38
  26.8 5.7 %collective-permute-start = (bf16[24,32,2]{2,1,0:T(8,128)(2,1)S(1)}, bf16[24,32,2]{2,1,0:T(8,128)(2,1)}, u32[]{:S(2)}, u32[]{:S(2)}) collective-permute-start(bf16[24,32,2]{2,1,0:T(8,128)(2,1)S(1)} %get-tuple-element.20), channel_id=1, source_target_pairs={{0,12},{12,24},{24,36},{36,48},{48,60},{60,72},{72,84},{84,96},{96... | collective-permute-start | bytes 9224 | tf_op jit(solution)/shard_map/ppermute | solution.py:37
  33.7 23.4 %collective-permute-start.3 = (bf16[24,32,100]{2,1,0:T(8,128)(2,1)S(1)}, bf16[24,32,100]{2,1,0:T(8,128)(2,1)S(1)}, u32[]{:S(2)}, u32[]{:S(2)}) collective-permute-start(bf16[24,32,100]{2,1,0:T(8,128)(2,1)S(1)} %pad_maximum_fusion.3), channel_id=1, source_target_pairs={{0,8},{1,9},{2,10},{3,11},{4,0},{5,1},{6,2},{7,3},{8,4},{9,5},{10,... | collective-permute-start | bytes 460808 | tf_op jit(solution)/shard_map/ppermute | solution.py:29
  36.5 20.6 %collective-permute-start.2 = (bf16[24,32,100]{2,1,0:T(8,128)(2,1)S(1)}, bf16[24,32,100]{2,1,0:T(8,128)(2,1)S(1)}, u32[]{:S(2)}, u32[]{:S(2)}) collective-permute-start(bf16[24,32,100]{2,1,0:T(8,128)(2,1)S(1)} %pad_maximum_fusion.3), channel_id=1, source_target_pairs={{0,4},{1,5},{2,6},{3,7},{4,8},{5,9},{6,10},{7,11},{8,0},{9,1},{10,... | collective-permute-start | bytes 460808 | tf_op jit(solution)/shard_map/ppermute | solution.py:29
  84.9 12.6 %all-to-all-start = ((f32[8,72,128]{2,1,0:T(8,128)}), f32[8,72,128]{2,1,0:T(8,128)S(1)}, u32[]{:S(2)}, u32[]{:S(2)}) async-start(f32[8,72,128]{2,1,0:T(8,128)} %bitcast.39), calls=%async_computation | async-start | bytes 589824 | tf_op jit(solution)/shard_map/all_to_all | solution.py:74
  97.5 10.9 %collective-permute-start.10 = (f32[72,128]{1,0:T(8,128)S(1)}, f32[72,128]{1,0:T(8,128)S(1)}, u32[]{:S(2)}, u32[]{:S(2)}) collective-permute-start(f32[72,128]{1,0:T(8,128)S(1)} %reduce_sum.18), channel_id=1, source_target_pairs={{0,11},{1,0},{2,1},{3,2},{4,3},{5,4},{6,5},{7,6},{8,7},{9,8},{10,9... | collective-permute-start | bytes 110600 | tf_op jit(solution)/shard_map/ppermute | solution.py:80
  109.1 17.4 %all-to-all-start.1 = ((f32[8,72,128]{2,1,0:T(8,128)}), f32[8,72,128]{2,1,0:T(8,128)S(1)}, u32[]{:S(2)}, u32[]{:S(2)}) async-start(f32[8,72,128]{2,1,0:T(8,128)} %broadcast_in_dim.4), calls=%async_computation.1 | async-start | bytes 589824 | tf_op jit(solution)/shard_map/all_to_all | solution.py:33
  113.3 23.7 %collective-permute-start.6 = (f32[24,32,96]{2,0,1:T(8,128)S(1)}, f32[24,32,96]{2,0,1:T(8,128)S(1)}, u32[]{:S(2)}, u32[]{:S(2)}) collective-permute-start(f32[24,32,96]{2,0,1:T(8,128)S(1)} %get-tuple-element.15), channel_id=1, source_target_pairs={{0,2},{1,3},{2,4},{3,5},{4,6},{5,7},{6,8},{7,9},{8,10},{9,11},{10,... | collective-permute-start | bytes 884744 | tf_op jit(solution)/shard_map/ppermute | solution.py:29
  119.9 26.9 %collective-permute-start.5 = (f32[24,32,96]{2,0,1:T(8,128)S(1)}, f32[24,32,96]{2,0,1:T(8,128)}, u32[]{:S(2)}, u32[]{:S(2)}) collective-permute-start(f32[24,32,96]{2,0,1:T(8,128)S(1)} %get-tuple-element.16), channel_id=1, source_target_pairs={{0,1},{1,2},{2,3},{3,4},{4,5},{5,6},{6,7},{7,8},{8,9},{9,10},{10,1... | collective-permute-start | bytes 884744 | tf_op jit(solution)/shard_map/ppermute | solution.py:29
  121.8 25.0 %collective-permute-start.4 = (f32[24,32,96]{2,0,1:T(8,128)S(1)}, f32[24,32,96]{2,0,1:T(8,128)}, u32[]{:S(2)}, u32[]{:S(2)}) collective-permute-start(f32[24,32,96]{2,0,1:T(8,128)S(1)} %get-tuple-element.14), channel_id=1, source_target_pairs={{0,11},{1,0},{2,1},{3,2},{4,3},{5,4},{6,5},{7,6},{8,7},{9,8},{10,9... | collective-permute-start | bytes 884744 | tf_op jit(solution)/shard_map/ppermute | solution.py:29
  127.2 21.6 %all-to-all-start.2 = ((f32[8,72,128]{2,1,0:T(8,128)}), f32[8,72,128]{2,1,0:T(8,128)S(1)}, u32[]{:S(2)}, u32[]{:S(2)}) async-start(f32[8,72,128]{2,1,0:T(8,128)} %broadcast_in_dim.5), calls=%async_computation.2 | async-start | bytes 589824 | tf_op jit(solution)/shard_map/all_to_all | solution.py:33

commit v2 on v1

v2 whole, which is shorter than its diff:
```python
import functools
import math

import jax
import jax.numpy as jnp
from jax import lax
from jax.experimental import pallas as pl
from jax.experimental.pallas import tpu as pltpu
from jax.sharding import PartitionSpec as P

NX, NY, NCORE = 4, 8, 2
LANES = 128
VMEM = pl.BlockSpec(memory_space=pltpu.VMEM)
SMEM = pl.BlockSpec(memory_space=pltpu.SMEM)


def group_lists():
    def at(x, y, core):
        return (x * NY + y) * NCORE + core

    across = [[at(x, y, c) for x in range(NX) for c in range(NCORE)] for y in range(NY)]
    along = [[at(x, y, c) for y in range(NY)] for x in range(NX) for c in range(NCORE)]
    return across, along


def lane_index(chans):
    return lax.broadcasted_iota(jnp.int32, (chans, LANES), 1)


def edges_kernel(cells_ref, edges_ref):
    rows, chans, width = cells_ref.shape[0], cells_ref.shape[1], 96
    lane = lane_index(chans)
    packed = jnp.zeros((chans, LANES), jnp.float32)
    for r in range(rows):
        row = cells_ref[r].astype(jnp.float32)
        tail = pltpu.roll(row, (2 * r - (width - 2)) % LANES, 1)
        head = pltpu.roll(row, (2 * rows + 2 * r) % LANES, 1)
        packed = jnp.where((lane >= 2 * r) & (lane < 2 * r + 2), tail, packed)
        at = 2 * rows + 2 * r
        packed = jnp.where((lane >= at) & (lane < at + 2), head, packed)
    edges_ref[...] = packed.astype(edges_ref.dtype)


def border_kernel(cells_ref, left_ref, right_ref, out_ref):
    rows, chans, width = cells_ref.shape[0], cells_ref.shape[1], 96
    lane = lane_index(chans)
    left = left_ref[...].astype(jnp.float32)
    right = right_ref[...].astype(jnp.float32)
    for r in range(rows):
        row = pltpu.roll(cells_ref[r].astype(jnp.float32), 2, 1)
        row = jnp.where(lane < 2, pltpu.roll(left, (-2 * r) % LANES, 1), row)
        at = width + 2
        tail = pltpu.roll(right, (at - 2 * rows - 2 * r) % LANES, 1)
        row = jnp.where((lane >= at) & (lane < at + 2), tail, row)
        out_ref[r] = row.astype(out_ref.dtype)


def weights_kernel(third_ref, x0, x1, x2, x3, g0, g1, g2, parts_ref, shifted_ref, window_ref):
    rows, chans = x0.shape[0], x0.shape[1]
    third = third_ref[0]
    blank = jnp.zeros((9 * chans, 2 * LANES), shifted_ref.dtype)
    shifted_ref[:, : 2 * LANES] = blank
    shifted_ref[:, (rows + 2) * LANES :] = blank
    for r in range(rows):
        window = jnp.concatenate([x[r].astype(jnp.float32) for x in (x0, x1, x2, x3)], axis=0)
        window_ref[:, r * LANES : (r + 1) * LANES] = window.astype(window_ref.dtype)
        near, own, far = [g[r].astype(jnp.float32) for g in (g0, g1, g2)]
        orders = ((own, far, near), (near, own, far), (far, near, own))
        base = jnp.concatenate(
            [
                jnp.where(third == 0, a, jnp.where(third == 1, b, c))
                for a, b, c in zip(*orders)
            ],
            axis=0,
        )
        taps = [pltpu.roll(base, LANES - 4, 1), pltpu.roll(base, LANES - 2, 1), base]
        shifted_ref[:, (r + 2) * LANES : (r + 3) * LANES] = jnp.concatenate(taps, axis=0).astype(
            shifted_ref.dtype
        )
    for b in range(3):
        at = (4 - 2 * b) * LANES
        part = lax.dot_general(
            window_ref[...],
            shifted_ref[:, at : at + rows * LANES],
            (((1,), (1,)), ((), ())),
            preferred_element_type=jnp.float32,
        )
        part = jnp.concatenate([part, jnp.zeros((4 * chans, 5 * 8), jnp.float32)], axis=1)
        for j in range(4):
            for h in range(2):
                parts_ref[2 * j + h, b * chans : (b + 1) * chans] = part[
                    j * chans : (j + 1) * chans, h * LANES : (h + 1) * LANES
                ]


def inputs_kernel(shifted_ref, filters_ref, *out_refs):
    rows, chans = out_refs[0].shape[0], out_refs[0].shape[1]
    total = None
    for b in range(3):
        at = (4 - 2 * b) * LANES
        part = jnp.dot(
            filters_ref[b],
            shifted_ref[:, at : at + rows * LANES],
            preferred_element_type=jnp.float32,
        )
        total = part if total is None else total + part
    for j in range(4):
        for r in range(rows):
            out_refs[j][r] = total[
                j * chans : (j + 1) * chans, r * LANES : (r + 1) * LANES
            ]


def place_kernel(factor, layer_ref, whole_ref, out_ref):
    chans = out_ref.shape[1]
    layer = layer_ref[0]
    for b in range(3):
        rows = []
        for v in range(4):
            j = lax.rem(layer + 5 - v, 4)
            rows.append(
                jnp.concatenate(
                    [whole_ref[2 * j + h, b * chans : (b + 1) * chans] for h in range(2)], axis=1
                )
            )
        for a in range(3):
            pieces = []
            for m in range(3):
                at = (3 * a + m) * chans
                pieces += [rows[v][:, at : at + chans] for v in range(4)]
            out_ref[3 * a + b] = jnp.concatenate(pieces, axis=1) * factor


def call(kernel, outs, ins, scalars=0, scratch=()):
    return pl.pallas_call(
        kernel,
        out_shape=outs,
        in_specs=[SMEM] * scalars + [VMEM] * (ins - scalars),
        out_specs=jax.tree.map(lambda _: VMEM, outs),
        scratch_shapes=list(scratch),
        compiler_params=pltpu.CompilerParams(vmem_limit_bytes=40 << 20),
    )


def per_device(field, grad_out, filters):
    across, along = group_lists()
    spaces = lax.axis_size("space")
    chans = lax.axis_size("chan")
    chan_dev, width, rows = field.shape
    factor = 1.0 / math.sqrt(rows * width * spaces)
    layer = lax.axis_index("chan")
    kind, wide = field.dtype, jnp.float32

    def shape(*dims, dtype=kind):
        return jax.ShapeDtypeStruct(dims, dtype)

    def move(cells, step):
        return lax.ppermute(cells, "chan", [(i, (i + step) % chans) for i in range(chans)])

    def spread(piece, groups):
        stacked = jnp.broadcast_to(piece[None], (8,) + piece.shape)
        return lax.all_to_all(stacked, "space", 0, 0, axis_index_groups=groups, tiled=True)

    def by_row(cells):
        return jnp.pad(cells.transpose(2, 0, 1), ((0, 0), (0, 0), (0, LANES - width)))

    cells = by_row(grad_out)
    edges = call(edges_kernel, shape(chan_dev, LANES), 1)(cells)
    left = lax.ppermute(edges, "space", [(i, i + 1) for i in range(spaces - 1)])
    right = lax.ppermute(edges, "space", [(i + 1, i) for i in range(spaces - 1)])
    edges, field = lax.optimization_barrier((edges, field))
    source = by_row(field)
    sources = [move(source, 1), source, move(source, -1), move(source, -2)]
    bordered = call(border_kernel, shape(rows, chan_dev, LANES), 3)(cells, left, right)
    grads = [move(bordered, 4), bordered, move(bordered, -4)]

    first, last = filters[:, : 2 * chan_dev], filters[:, -chan_dev:]
    own = jnp.concatenate([last, filters, first], axis=1)
    own = lax.dynamic_slice_in_dim(own, layer * chan_dev, 4 * chan_dev, 1)
    lane = jnp.arange(3 * chan_dev)
    wanted = (4 * (lane // chan_dev) + layer % 4) * chan_dev + lane % chan_dev
    chosen = (jnp.arange(12 * chan_dev)[:, None] == wanted[None, :]).astype(filters.dtype)
    own = jnp.einsum("kio,op->kip", own, chosen, preferred_element_type=jnp.float32)
    own = own.astype(filters.dtype).reshape(3, 3, 4 * chan_dev, 3 * chan_dev)
    own = own.transpose(1, 2, 0, 3).reshape(3, 4 * chan_dev, 9 * chan_dev)

    third = (layer // 4)[None]
    parts, shifted = call(
        weights_kernel,
        (
            shape(8, 3 * chan_dev, LANES, dtype=wide),
            shape(9 * chan_dev, (rows + 4) * LANES),
        ),
        8,
        1,
        [pltpu.VMEM((4 * chan_dev, rows * LANES), kind)],
    )(third, *sources, *grads)

    piece = lax.all_to_all(parts, "space", 0, 0, axis_index_groups=across, tiled=True).sum(0)
    home = [
        (s * chans + c, s * chans + (c - 1 + s // (NY * NCORE)) % chans)
        for s in range(spaces)
        for c in range(chans)
    ]
    piece = lax.ppermute(piece, ("space", "chan"), home)
    piece = spread(piece, along).sum(0)
    whole = spread(piece, across)
    grad_filters = call(
        functools.partial(place_kernel, factor),
        shape(9, chan_dev, 12 * chan_dev, dtype=wide),
        2,
        1,
    )(layer[None], whole)

    blocks = call(
        inputs_kernel, tuple(shape(rows, chan_dev, LANES, dtype=wide) for _ in range(4)), 2
    )(shifted, own)
    total = blocks[1] + move(blocks[0], -1) + move(blocks[2], 1) + move(blocks[3], 2)
    return (total[..., :width].transpose(1, 2, 0), grad_filters)


def solution(mesh):
    in_specs = (P("chan", "space", None), P("chan", "space", None), P())
    out_specs = (P("chan", "space", None), P(None, "chan", None))
    return jax.shard_map(
        per_device, mesh=mesh, in_specs=in_specs, out_specs=out_specs, check_vma=False
    )
```

time: 154 us -> 122 us (0.79)
  the two profiles are of different devices: /device:TPU:1 before, /device:TPU:78 now
where the time goes in v2:
time: 122 us; the launch traced here: 121 us
  starting transfers between devices  61.9 us (51%)
  waiting for transfers between devices  45.2 us (37%)
  Pallas kernels  5.93 us (5%)
  local copies, waits for them, and re-layouts  4.54 us (4%)
  matrix products  1.63 us (1%)
    ppermute x8, starting transfers between devices, move(): lax.ppermute(cells, 'chan', [(i, (i + step) % chans) for i in range(chans)])  38.8 us
    ppermute x8, waiting for transfers between devices, move(): lax.ppermute(cells, 'chan', [(i, (i + step) % chans) for i in range(chans)])  33.4 us
    all_to_all x2, starting transfers between devices, spread(): lax.all_to_all(stacked, 'space', 0, 0, axis_index_groups=groups, tiled=True)  11.9 us
    ppermute x1, waiting for transfers between devices, per_device(): piece = lax.ppermute(piece, ('space', 'chan'), home)  6.01 us
    all_to_all x1, waiting for transfers between devices, per_device(): lax.all_to_all(parts, 'space', 0, 0, axis_index_groups=across, tiled=True)  5.82 us
    all_to_all x1, starting transfers between devices, per_device(): lax.all_to_all(parts, 'space', 0, 0, axis_index_groups=across, tiled=True)  4.91 us
    pallas_call x1, Pallas kernels, per_device(): call(weights_kernel, (shape(8, 3 * chan_dev, LANES, dtype=wide), shape(9...  2.69 us
  transfers between devices with their start and end apart: 14, of which 6 were waited for; matrix products, arithmetic and copies ran while one was open for 5% of the time, Pallas kernels for 2%

profile of v2, /device:TPU:78, one launch (start us, length us, event | category | flops | bytes accessed | tf_op | source)
XLA Modules:
  0.0 121.1 jit_solution(14062661520464774238)
XLA Ops:
  0.6 1.0 copy.22
  1.7 0.2 shard_map.50
  1.9 1.9 %collective-permute-start.4 = (bf16[24,128]{1,0:T(8,128)(2,1)S(1)}, bf16[24,128]{1,0:T(8,128)(2,1)S(1)}, u32[]{:S(2)}, u32[]{:S(2)}) collective-permute-start(bf16[24,128]{1,0:T(8,128)(2,1)S(1)} %shard_map.50), channel_id=1, source_target_pairs={{12,0},{24,12},{36,24},{48,36},{60,48},{72,60},{84,72},{96,84},{10... | collective-permute-start | bytes 18440 | tf_op jit(solution)/shard_map/ppermute | solution.py:170
  3.8 2.4 %collective-permute-start.3 = (bf16[24,128]{1,0:T(8,128)(2,1)S(1)}, bf16[24,128]{1,0:T(8,128)(2,1)S(1)}, u32[]{:S(2)}, u32[]{:S(2)}) collective-permute-start(bf16[24,128]{1,0:T(8,128)(2,1)S(1)} %shard_map.50), channel_id=1, source_target_pairs={{0,12},{12,24},{24,36},{36,48},{48,60},{60,72},{72,84},{84,96},{96... | collective-permute-start | bytes 18440 | tf_op jit(solution)/shard_map/ppermute | solution.py:169
  6.2 1.0 copy.21
  7.3 13.7 %collective-permute-start.2 = (bf16[32,24,128]{2,1,0:T(8,128)(2,1)S(1)}, bf16[32,24,128]{2,1,0:T(8,128)(2,1)S(1)}, u32[]{:S(2)}, u32[]{:S(2)}) collective-permute-start(bf16[32,24,128]{2,1,0:T(8,128)(2,1)S(1)} %pad.8.x1), channel_id=1, source_target_pairs={{0,10},{1,11},{2,0},{3,1},{4,2},{5,3},{6,4},{7,5},{8,6},{9,7},{10,... | collective-permute-start | bytes 589832 | tf_op jit(solution)/shard_map/ppermute | solution.py:158
  21.0 2.5 %collective-permute-start.1 = (bf16[32,24,128]{2,1,0:T(8,128)(2,1)S(1)}, bf16[32,24,128]{2,1,0:T(8,128)(2,1)S(1)}, u32[]{:S(2)}, u32[]{:S(2)}) collective-permute-start(bf16[32,24,128]{2,1,0:T(8,128)(2,1)S(1)} %pad.8.x1), channel_id=1, source_target_pairs={{0,11},{1,0},{2,1},{3,2},{4,3},{5,4},{6,5},{7,6},{8,7},{9,8},{10,9... | collective-permute-start | bytes 589832 | tf_op jit(solution)/shard_map/ppermute | solution.py:158
  23.4 3.4 %collective-permute-start = (bf16[32,24,128]{2,1,0:T(8,128)(2,1)S(1)}, bf16[32,24,128]{2,1,0:T(8,128)(2,1)S(1)}, u32[]{:S(2)}, u32[]{:S(2)}) collective-permute-start(bf16[32,24,128]{2,1,0:T(8,128)(2,1)S(1)} %pad.8.x1), channel_id=1, source_target_pairs={{0,1},{1,2},{2,3},{3,4},{4,5},{5,6},{6,7},{7,8},{8,9},{9,10},{10,1... | collective-permute-start | bytes 589832 | tf_op jit(solution)/shard_map/ppermute | solution.py:158
  26.8 0.2 shard_map.51.g1
  27.1 3.6 %collective-permute-start.6 = (bf16[32,24,128]{2,1,0:T(8,128)(2,1)S(1)}, bf16[32,24,128]{2,1,0:T(8,128)(2,1)S(1)}, u32[]{:S(2)}, u32[]{:S(2)}) collective-permute-start(bf16[32,24,128]{2,1,0:T(8,128)(2,1)S(1)} %shard_map.51.g1), channel_id=1, source_target_pairs={{0,8},{1,9},{2,10},{3,11},{4,0},{5,1},{6,2},{7,3},{8,4},{9,5},{10,... | collective-permute-start | bytes 589832 | tf_op jit(solution)/shard_map/ppermute | solution.py:158
  30.7 6.1 %collective-permute-start.5 = (bf16[32,24,128]{2,1,0:T(8,128)(2,1)S(1)}, bf16[32,24,128]{2,1,0:T(8,128)(2,1)S(1)}, u32[]{:S(2)}, u32[]{:S(2)}) collective-permute-start(bf16[32,24,128]{2,1,0:T(8,128)(2,1)S(1)} %shard_map.51.g1), channel_id=1, source_target_pairs={{0,4},{1,5},{2,6},{3,7},{4,8},{5,9},{6,10},{7,11},{8,0},{9,1},{10,... | collective-permute-start | bytes 589832 | tf_op jit(solution)/shard_map/ppermute | solution.py:158
  36.9 12.5 %collective-permute-done.6.g2 = bf16[32,24,128]{2,1,0:T(8,128)(2,1)S(1)} collective-permute-done((bf16[32,24,128]{2,1,0:T(8,128)(2,1)S(1)}, bf16[32,24,128]{2,1,0:T(8,128)(2,1)S(1)}, u32[]{:S(2)}, u32[]{:S(2)}) %collective-permute-start.6) | collective-permute-done | bytes 196640 | tf_op jit(solution)/shard_map/ppermute | solution.py:158
  49.5 6.4 %collective-permute-done.5.g0 = bf16[32,24,128]{2,1,0:T(8,128)(2,1)S(1)} collective-permute-done((bf16[32,24,128]{2,1,0:T(8,128)(2,1)S(1)}, bf16[32,24,128]{2,1,0:T(8,128)(2,1)S(1)}, u32[]{:S(2)}, u32[]{:S(2)}) %collective-permute-start.5) | collective-permute-done | bytes 196640 | tf_op jit(solution)/shard_map/ppermute | solution.py:158
  55.8 2.7 %shard_map.52 = (f32[8,72,128]{2,1,0:T(8,128)}, bf16[216,4608]{1,0:T(8,128)(2,1)S(1)}) custom-call(s32[1]{0:T(128)} %bitcast.third_ref, bf16[32,24,128]{2,1,0:T(8,128)(2,1)S(1)} %collective-permute-done.x0, bf16[32,24,128]{2,1,0:T(8,128)(2,1)S(1)} %pad.8.x1, bf16[32,24,128]{2,1,0:T(8,128)(2,1)S(1)} %collective-permute-done.1.x2, ...), custom_call_target="tpu_custom_call" | custom-call | tf_op jit(solution)/shard_map/pallas_call | solution.py:188
  58.5 4.9 %all-to-all-start = ((f32[8,72,128]{2,1,0:T(8,128)}), f32[8,72,128]{2,1,0:T(8,128)S(1)}, u32[]{:S(2)}, u32[]{:S(2)}) async-start(f32[8,72,128]{2,1,0:T(8,128)} %get-tuple-element.15), calls=%async_computation | async-start | bytes 589824 | tf_op jit(solution)/shard_map/all_to_all | solution.py:199
  63.4 5.8 %all-to-all-done = f32[8,72,128]{2,1,0:T(8,128)S(1)} async-done(((f32[8,72,128]{2,1,0:T(8,128)}), f32[8,72,128]{2,1,0:T(8,128)S(1)}, u32[]{:S(2)}, u32[]{:S(2)}) %all-to-all-start) | async-done | bytes 294944 | tf_op jit(solution)/shard_map/all_to_all | solution.py:199
  69.3 1.9 %collective-permute-start.10 = (f32[72,128]{1,0:T(8,128)S(1)}, f32[72,128]{1,0:T(8,128)S(1)}, u32[]{:S(2)}, u32[]{:S(2)}) collective-permute-start(f32[72,128]{1,0:T(8,128)S(1)} %reduce_sum.18), channel_id=1, source_target_pairs={{0,11},{1,0},{2,1},{3,2},{4,3},{5,4},{6,5},{7,6},{8,7},{9,8},{10,9... | collective-permute-start | bytes 110600 | tf_op jit(solution)/shard_map/ppermute | solution.py:205
  71.2 6.0 %collective-permute-done.10 = f32[72,128]{1,0:T(8,128)S(1)} collective-permute-done((f32[72,128]{1,0:T(8,128)S(1)}, f32[72,128]{1,0:T(8,128)S(1)}, u32[]{:S(2)}, u32[]{:S(2)}) %collective-permute-start.10) | collective-permute-done | bytes 36896 | tf_op jit(solution)/shard_map/ppermute | solution.py:205
  77.3 0.7 broadcast_in_dim.10
  78.0 7.4 %all-to-all-start.1 = ((f32[8,72,128]{2,1,0:T(8,128)}), f32[8,72,128]{2,1,0:T(8,128)}, u32[]{:S(2)}, u32[]{:S(2)}) async-start(f32[8,72,128]{2,1,0:T(8,128)} %broadcast_in_dim.10), calls=%async_computation.1 | async-start | bytes 589824 | tf_op jit(solution)/shard_map/all_to_all | solution.py:162
  85.4 1.6 %convolution_convert_fusion = bf16[9,96,72]{1,2,0:T(8,128)(2,1)S(1)} fusion(s32[]{:T(128)S(6)} %select_n.34, bf16[9,24,288]{2,1,0:T(8,128)(2,1)S(1)} %slice-done, bf16[9,288,288]{2,1,0:T(8,128)(2,1)} %param.5, bf16[9,48,288]{2,1,0:T(8,128)(2,1)S(1)} %slice-done.1, s32[72]{0:T(128)S(1)} %fusion.8), kind=kOutput, calls=%fused_computation.3 | convolution fusion | flops 37407744 | bytes 1990948 | tf_op jit(solution)/shard_map/kio,op->kip/dot_general | solution.py:183
  87.2 1.8 %shard_map.53 = (f32[32,24,128]{2,1,0:T(8,128)}, f32[32,24,128]{2,1,0:T(8,128)S(1)}, f32[32,24,128]{2,1,0:T(8,128)S(1)}, f32[32,24,128]{2,1,0:T(8,128)S(1)}) custom-call(bf16[216,4608]{1,0:T(8,128)(2,1)S(1)} %get-tuple-element.10.shifted_ref, bf16[3,96,216]{2,1,0:T(8,128)(2,1)S(1)} %copy.17.filters_ref), custom_call_target="tpu_custom_call" | custom-call | tf_op jit(solution)/shard_map/pallas_call | solution.py:215
  89.0 1.9 %collective-permute-start.7 = (f32[32,24,128]{2,1,0:T(8,128)}, f32[32,24,128]{2,1,0:T(8,128)S(1)}, u32[]{:S(2)}, u32[]{:S(2)}) collective-permute-start(f32[32,24,128]{2,1,0:T(8,128)} %get-tuple-element.12), channel_id=1, source_target_pairs={{0,11},{1,0},{2,1},{3,2},{4,3},{5,4},{6,5},{7,6},{8,7},{9,8},{10,9... | collective-permute-start | bytes 1179656 | tf_op jit(solution)/shard_map/ppermute | solution.py:158
  90.9 3.9 %collective-permute-start.8 = (f32[32,24,128]{2,1,0:T(8,128)S(1)}, f32[32,24,128]{2,1,0:T(8,128)S(1)}, u32[]{:S(2)}, u32[]{:S(2)}) collective-permute-start(f32[32,24,128]{2,1,0:T(8,128)S(1)} %get-tuple-element.13), channel_id=1, source_target_pairs={{0,1},{1,2},{2,3},{3,4},{4,5},{5,6},{6,7},{7,8},{8,9},{9,10},{10,1... | collective-permute-start | bytes 1179656 | tf_op jit(solution)/shard_map/ppermute | solution.py:158
  94.8 3.7 %collective-permute-start.9 = (f32[32,24,128]{2,1,0:T(8,128)S(1)}, f32[32,24,128]{2,1,0:T(8,128)S(1)}, u32[]{:S(2)}, u32[]{:S(2)}) collective-permute-start(f32[32,24,128]{2,1,0:T(8,128)S(1)} %get-tuple-element.14), channel_id=1, source_target_pairs={{0,2},{1,3},{2,4},{3,5},{4,6},{5,7},{6,8},{7,9},{8,10},{9,11},{10,... | collective-permute-start | bytes 1179656 | tf_op jit(solution)/shard_map/ppermute | solution.py:158
  98.5 1.0 reduce_sum.19
  99.5 0.7 broadcast_in_dim.11
  100.2 4.5 %all-to-all-start.2 = ((f32[8,72,128]{2,1,0:T(8,128)}), f32[8,72,128]{2,1,0:T(8,128)S(1)}, u32[]{:S(2)}, u32[]{:S(2)}) async-start(f32[8,72,128]{2,1,0:T(8,128)} %broadcast_in_dim.11), calls=%async_computation.2 | async-start | bytes 589824 | tf_op jit(solution)/shard_map/all_to_all | solution.py:162
  104.7 7.2 %collective-permute-done.8 = f32[32,24,128]{2,1,0:T(8,128)S(1)} collective-permute-done((f32[32,24,128]{2,1,0:T(8,128)S(1)}, f32[32,24,128]{2,1,0:T(8,128)S(1)}, u32[]{:S(2)}, u32[]{:S(2)}) %collective-permute-start.8) | collective-permute-done | bytes 393248 | tf_op jit(solution)/shard_map/ppermute | solution.py:158
  111.9 7.3 %collective-permute-done.9 = f32[32,24,128]{2,1,0:T(8,128)S(1)} collective-permute-done((f32[32,24,128]{2,1,0:T(8,128)S(1)}, f32[32,24,128]{2,1,0:T(8,128)S(1)}, u32[]{:S(2)}, u32[]{:S(2)}) %collective-permute-start.9) | collective-permute-done | bytes 393248 | tf_op jit(solution)/shard_map/ppermute | solution.py:158
  119.2 0.8 copy.18
  120.1 1.1 shard_map.54
  (19 shorter events, 0.4 us)
Async XLA Ops:
  1.9 24.9 %collective-permute-start.4 = (bf16[24,128]{1,0:T(8,128)(2,1)S(1)}, bf16[24,128]{1,0:T(8,128)(2,1)S(1)}, u32[]{:S(2)}, u32[]{:S(2)}) collective-permute-start(bf16[24,128]{1,0:T(8,128)(2,1)S(1)} %shard_map.50), channel_id=1, source_target_pairs={{12,0},{24,12},{36,24},{48,36},{60,48},{72,60},{84,72},{96,84},{10... | collective-permute-start | bytes 18440 | tf_op jit(solution)/shard_map/ppermute | solution.py:170
  3.8 23.0 %collective-permute-start.3 = (bf16[24,128]{1,0:T(8,128)(2,1)S(1)}, bf16[24,128]{1,0:T(8,128)(2,1)S(1)}, u32[]{:S(2)}, u32[]{:S(2)}) collective-permute-start(bf16[24,128]{1,0:T(8,128)(2,1)S(1)} %shard_map.50), channel_id=1, source_target_pairs={{0,12},{12,24},{24,36},{36,48},{48,60},{60,72},{72,84},{84,96},{96... | collective-permute-start | bytes 18440 | tf_op jit(solution)/shard_map/ppermute | solution.py:169
  7.3 29.6 %collective-permute-start.2 = (bf16[32,24,128]{2,1,0:T(8,128)(2,1)S(1)}, bf16[32,24,128]{2,1,0:T(8,128)(2,1)S(1)}, u32[]{:S(2)}, u32[]{:S(2)}) collective-permute-start(bf16[32,24,128]{2,1,0:T(8,128)(2,1)S(1)} %pad.8.x1), channel_id=1, source_target_pairs={{0,10},{1,11},{2,0},{3,1},{4,2},{5,3},{6,4},{7,5},{8,6},{9,7},{10,... | collective-permute-start | bytes 589832 | tf_op jit(solution)/shard_map/ppermute | solution.py:158
  21.0 15.9 %collective-permute-start.1 = (bf16[32,24,128]{2,1,0:T(8,128)(2,1)S(1)}, bf16[32,24,128]{2,1,0:T(8,128)(2,1)S(1)}, u32[]{:S(2)}, u32[]{:S(2)}) collective-permute-start(bf16[32,24,128]{2,1,0:T(8,128)(2,1)S(1)} %pad.8.x1), channel_id=1, source_target_pairs={{0,11},{1,0},{2,1},{3,2},{4,3},{5,4},{6,5},{7,6},{8,7},{9,8},{10,9... | collective-permute-start | bytes 589832 | tf_op jit(solution)/shard_map/ppermute | solution.py:158
  23.4 13.5 %collective-permute-start = (bf16[32,24,128]{2,1,0:T(8,128)(2,1)S(1)}, bf16[32,24,128]{2,1,0:T(8,128)(2,1)S(1)}, u32[]{:S(2)}, u32[]{:S(2)}) collective-permute-start(bf16[32,24,128]{2,1,0:T(8,128)(2,1)S(1)} %pad.8.x1), channel_id=1, source_target_pairs={{0,1},{1,2},{2,3},{3,4},{4,5},{5,6},{6,7},{7,8},{8,9},{9,10},{10,1... | collective-permute-start | bytes 589832 | tf_op jit(solution)/shard_map/ppermute | solution.py:158
  27.1 22.4 %collective-permute-start.6 = (bf16[32,24,128]{2,1,0:T(8,128)(2,1)S(1)}, bf16[32,24,128]{2,1,0:T(8,128)(2,1)S(1)}, u32[]{:S(2)}, u32[]{:S(2)}) collective-permute-start(bf16[32,24,128]{2,1,0:T(8,128)(2,1)S(1)} %shard_map.51.g1), channel_id=1, source_target_pairs={{0,8},{1,9},{2,10},{3,11},{4,0},{5,1},{6,2},{7,3},{8,4},{9,5},{10,... | collective-permute-start | bytes 589832 | tf_op jit(solution)/shard_map/ppermute | solution.py:158
  30.7 25.1 %collective-permute-start.5 = (bf16[32,24,128]{2,1,0:T(8,128)(2,1)S(1)}, bf16[32,24,128]{2,1,0:T(8,128)(2,1)S(1)}, u32[]{:S(2)}, u32[]{:S(2)}) collective-permute-start(bf16[32,24,128]{2,1,0:T(8,128)(2,1)S(1)} %shard_map.51.g1), channel_id=1, source_target_pairs={{0,4},{1,5},{2,6},{3,7},{4,8},{5,9},{6,10},{7,11},{8,0},{9,1},{10,... | collective-permute-start | bytes 589832 | tf_op jit(solution)/shard_map/ppermute | solution.py:158
  55.8 29.6 %slice-start = ((bf16[9,288,288]{2,1,0:T(8,128)(2,1)}), bf16[9,24,288]{2,1,0:T(8,128)(2,1)S(1)}, s32[]{:S(2)}) async-start(bf16[9,288,288]{2,1,0:T(8,128)(2,1)} %param.5), calls=%async_computation.3 | async-start | bytes 331776 | tf_op jit(solution)/shard_map/slice | solution.py:177
  58.5 26.9 %slice-start.1 = ((bf16[9,288,288]{2,1,0:T(8,128)(2,1)}), bf16[9,48,288]{2,1,0:T(8,128)(2,1)S(1)}, s32[]{:S(2)}) async-start(bf16[9,288,288]{2,1,0:T(8,128)(2,1)} %param.5), calls=%async_computation.4 | async-start | bytes 663552 | tf_op jit(solution)/shard_map/slice | solution.py:177
  58.5 10.7 %all-to-all-start = ((f32[8,72,128]{2,1,0:T(8,128)}), f32[8,72,128]{2,1,0:T(8,128)S(1)}, u32[]{:S(2)}, u32[]{:S(2)}) async-start(f32[8,72,128]{2,1,0:T(8,128)} %get-tuple-element.15), calls=%async_computation | async-start | bytes 589824 | tf_op jit(solution)/shard_map/all_to_all | solution.py:199
  69.3 8.0 %collective-permute-start.10 = (f32[72,128]{1,0:T(8,128)S(1)}, f32[72,128]{1,0:T(8,128)S(1)}, u32[]{:S(2)}, u32[]{:S(2)}) collective-permute-start(f32[72,128]{1,0:T(8,128)S(1)} %reduce_sum.18), channel_id=1, source_target_pairs={{0,11},{1,0},{2,1},{3,2},{4,3},{5,4},{6,5},{7,6},{8,7},{9,8},{10,9... | collective-permute-start | bytes 110600 | tf_op jit(solution)/shard_map/ppermute | solution.py:205
  78.0 20.5 %all-to-all-start.1 = ((f32[8,72,128]{2,1,0:T(8,128)}), f32[8,72,128]{2,1,0:T(8,128)}, u32[]{:S(2)}, u32[]{:S(2)}) async-start(f32[8,72,128]{2,1,0:T(8,128)} %broadcast_in_dim.10), calls=%async_computation.1 | async-start | bytes 589824 | tf_op jit(solution)/shard_map/all_to_all | solution.py:162
  89.0 15.8 %collective-permute-start.7 = (f32[32,24,128]{2,1,0:T(8,128)}, f32[32,24,128]{2,1,0:T(8,128)S(1)}, u32[]{:S(2)}, u32[]{:S(2)}) collective-permute-start(f32[32,24,128]{2,1,0:T(8,128)} %get-tuple-element.12), channel_id=1, source_target_pairs={{0,11},{1,0},{2,1},{3,2},{4,3},{5,4},{6,5},{7,6},{8,7},{9,8},{10,9... | collective-permute-start | bytes 1179656 | tf_op jit(solution)/shard_map/ppermute | solution.py:158
  90.9 21.0 %collective-permute-start.8 = (f32[32,24,128]{2,1,0:T(8,128)S(1)}, f32[32,24,128]{2,1,0:T(8,128)S(1)}, u32[]{:S(2)}, u32[]{:S(2)}) collective-permute-start(f32[32,24,128]{2,1,0:T(8,128)S(1)} %get-tuple-element.13), channel_id=1, source_target_pairs={{0,1},{1,2},{2,3},{3,4},{4,5},{5,6},{6,7},{7,8},{8,9},{9,10},{10,1... | collective-permute-start | bytes 1179656 | tf_op jit(solution)/shard_map/ppermute | solution.py:158
  94.8 24.4 %collective-permute-start.9 = (f32[32,24,128]{2,1,0:T(8,128)S(1)}, f32[32,24,128]{2,1,0:T(8,128)S(1)}, u32[]{:S(2)}, u32[]{:S(2)}) collective-permute-start(f32[32,24,128]{2,1,0:T(8,128)S(1)} %get-tuple-element.14), channel_id=1, source_target_pairs={{0,2},{1,3},{2,4},{3,5},{4,6},{5,7},{6,8},{7,9},{8,10},{9,11},{10,... | collective-permute-start | bytes 1179656 | tf_op jit(solution)/shard_map/ppermute | solution.py:158
  100.2 19.8 %all-to-all-start.2 = ((f32[8,72,128]{2,1,0:T(8,128)}), f32[8,72,128]{2,1,0:T(8,128)S(1)}, u32[]{:S(2)}, u32[]{:S(2)}) async-start(f32[8,72,128]{2,1,0:T(8,128)} %broadcast_in_dim.11), calls=%async_computation.2 | async-start | bytes 589824 | tf_op jit(solution)/shard_map/all_to_all | solution.py:162

commit v3 on v2

--- a/solution.py
+++ b/solution.py
@@ -9,7 +9,7 @@
 from jax.sharding import PartitionSpec as P
 
 NX, NY, NCORE = 4, 8, 2
-LANES = 128
+LANES, WIDTH = 128, 96
 VMEM = pl.BlockSpec(memory_space=pltpu.VMEM)
 SMEM = pl.BlockSpec(memory_space=pltpu.SMEM)
 
@@ -27,56 +27,97 @@
     return lax.broadcasted_iota(jnp.int32, (chans, LANES), 1)
 
 
-def edges_kernel(cells_ref, edges_ref):
-    rows, chans, width = cells_ref.shape[0], cells_ref.shape[1], 96
+def edges_kernel(cells_ref, edges_ref, dense_ref):
+    rows, chans = cells_ref.shape[0], cells_ref.shape[1]
     lane = lane_index(chans)
     packed = jnp.zeros((chans, LANES), jnp.float32)
-    for r in range(rows):
-        row = cells_ref[r].astype(jnp.float32)
-        tail = pltpu.roll(row, (2 * r - (width - 2)) % LANES, 1)
-        head = pltpu.roll(row, (2 * rows + 2 * r) % LANES, 1)
-        packed = jnp.where((lane >= 2 * r) & (lane < 2 * r + 2), tail, packed)
-        at = 2 * rows + 2 * r
-        packed = jnp.where((lane >= at) & (lane < at + 2), head, packed)
+    for start in range(0, rows, 4):
+        group = [cells_ref[start + i].astype(jnp.float32) for i in range(4)]
+        store_dense(dense_ref, start, group)
+        for i in range(4):
+            r = start + i
+            tail_at, head_at = 4 * r, (4 * r + WIDTH + 2) % LANES
+            tail = pltpu.roll(group[i], (tail_at - (WIDTH - 2)) % LANES, 1)
+            head = pltpu.roll(group[i], head_at, 1)
+            packed = jnp.where((lane >= tail_at) & (lane < tail_at + 2), tail, packed)
+            packed = jnp.where((lane >= head_at) & (lane < head_at + 2), head, packed)
     edges_ref[...] = packed.astype(edges_ref.dtype)
 
 
-def border_kernel(cells_ref, left_ref, right_ref, out_ref):
-    rows, chans, width = cells_ref.shape[0], cells_ref.shape[1], 96
-    lane = lane_index(chans)
+def store_dense(dense_ref, start, group):
+    lane = lane_index(group[0].shape[0])
+    turned = [group[0]] + [pltpu.roll(group[i], LANES - 32 * i, 1) for i in (1, 2, 3)]
+    tiles = [jnp.where(lane < LANES - 32 * (i + 1), turned[i], turned[i + 1]) for i in range(3)]
+    for i in range(3):
+        at = (3 * start // 4 + i) * LANES
+        dense_ref[:, at : at + LANES] = tiles[i].astype(dense_ref.dtype)
+
+
+def load_rows(tiles, offset):
+    lane = lane_index(tiles[0].shape[0])
+    rows = []
+    for i in range(4):
+        turn = (32 * i + offset) % LANES
+        row = pltpu.roll(tiles[min(i, 2)], turn, 1) if turn else tiles[i]
+        if i in (1, 2):
+            before = pltpu.roll(tiles[i - 1], turn, 1)
+            row = jnp.where(lane < 32 * i + offset, before, row)
+        rows.append(row)
+    return rows
+
+
+def border_kernel(dense_ref, left_ref, right_ref, source_ref, out_ref, packed_ref):
+    for start in range(0, source_ref.shape[0], 4):
+        group = [source_ref[start + i].astype(jnp.float32) for i in range(4)]
+        store_dense(packed_ref, start, group)
+    cells = dense_ref.shape[1]
+    packed_ref[:, cells:] = jnp.zeros((dense_ref.shape[0], LANES), packed_ref.dtype)
+    lane = lane_index(dense_ref.shape[0])
     left = left_ref[...].astype(jnp.float32)
     right = right_ref[...].astype(jnp.float32)
-    for r in range(rows):
-        row = pltpu.roll(cells_ref[r].astype(jnp.float32), 2, 1)
-        row = jnp.where(lane < 2, pltpu.roll(left, (-2 * r) % LANES, 1), row)
-        at = width + 2
-        tail = pltpu.roll(right, (at - 2 * rows - 2 * r) % LANES, 1)
-        row = jnp.where((lane >= at) & (lane < at + 2), tail, row)
-        out_ref[r] = row.astype(out_ref.dtype)
-
-
-def weights_kernel(third_ref, x0, x1, x2, x3, g0, g1, g2, parts_ref, shifted_ref, window_ref):
-    rows, chans = x0.shape[0], x0.shape[1]
+    out_ref[:, :cells] = dense_ref[...]
+    out_ref[:, cells:] = jnp.where(lane % 4 < 2, left, right).astype(out_ref.dtype)
+
+
+def weights_kernel(third_ref, own_ref, *refs):
+    g_refs, x_refs, (parts_ref, shifted_ref, window_ref) = refs[:3], refs[3:7], refs[7:]
+    chans = x_refs[0].shape[0]
+    rows = refs[8].shape[1] // LANES - 4
     third = third_ref[0]
-    blank = jnp.zeros((9 * chans, 2 * LANES), shifted_ref.dtype)
+    kind = shifted_ref.dtype
+    blank = jnp.zeros((9 * chans, 2 * LANES), kind)
     shifted_ref[:, : 2 * LANES] = blank
     shifted_ref[:, (rows + 2) * LANES :] = blank
-    for r in range(rows):
-        window = jnp.concatenate([x[r].astype(jnp.float32) for x in (x0, x1, x2, x3)], axis=0)
-        window_ref[:, r * LANES : (r + 1) * LANES] = window.astype(window_ref.dtype)
-        near, own, far = [g[r].astype(jnp.float32) for g in (g0, g1, g2)]
+    lane_x, lane_g = lane_index(4 * chans), lane_index(3 * chans)
+
+    def pick(at):
+        near, own, far = [g[:, at : at + LANES].astype(jnp.float32) for g in g_refs]
         orders = ((own, far, near), (near, own, far), (far, near, own))
-        base = jnp.concatenate(
+        return jnp.concatenate(
             [
                 jnp.where(third == 0, a, jnp.where(third == 1, b, c))
                 for a, b, c in zip(*orders)
             ],
             axis=0,
         )
-        taps = [pltpu.roll(base, LANES - 4, 1), pltpu.roll(base, LANES - 2, 1), base]
-        shifted_ref[:, (r + 2) * LANES : (r + 3) * LANES] = jnp.concatenate(taps, axis=0).astype(
-            shifted_ref.dtype
-        )
+
+    sides = pick(rows * WIDTH)
+    for start in range(0, rows, 4):
+        ats = [(3 * start // 4 + i) * LANES for i in range(3)]
+        tiles = [
+            jnp.concatenate([x[:, at : at + LANES].astype(jnp.float32) for x in x_refs], axis=0)
+            for at in ats
+        ]
+        for i, row in enumerate(load_rows(tiles, 0)):
+            at = (start + i) * LANES
+            window_ref[:, at : at + LANES] = jnp.where(lane_x < WIDTH, row, 0.0).astype(kind)
+        for i, row in enumerate(load_rows([pick(at) for at in ats], 2)):
+            side = pltpu.roll(sides, (-4 * (start + i)) % LANES, 1) if start + i else sides
+            row = jnp.where((lane_g >= 2) & (lane_g < WIDTH + 2), row, side)
+            row = jnp.where(lane_g < WIDTH + 4, row, 0.0)
+            taps = [pltpu.roll(row, LANES - 4, 1), pltpu.roll(row, LANES - 2, 1), row]
+            at = (start + i + 2) * LANES
+            shifted_ref[:, at : at + LANES] = jnp.concatenate(taps, axis=0).astype(kind)
     for b in range(3):
         at = (4 - 2 * b) * LANES
         part = lax.dot_general(
@@ -94,7 +135,8 @@
 
 
 def inputs_kernel(shifted_ref, filters_ref, *out_refs):
-    rows, chans = out_refs[0].shape[0], out_refs[0].shape[1]
+    chans = out_refs[0].shape[0]
+    rows = out_refs[0].shape[1] // WIDTH
     total = None
     for b in range(3):
         at = (4 - 2 * b) * LANES
@@ -105,10 +147,28 @@
         )
         total = part if total is None else total + part
     for j in range(4):
-        for r in range(rows):
-            out_refs[j][r] = total[
-                j * chans : (j + 1) * chans, r * LANES : (r + 1) * LANES
-            ]
+        block = total[j * chans : (j + 1) * chans]
+        for start in range(0, rows, 4):
+            group = [block[:, r * LANES : (r + 1) * LANES] for r in range(start, start + 4)]
+            store_dense(out_refs[j], start, group)
+
+
+def total_kernel(a_ref, b_ref, c_ref, d_ref, out_ref):
+    for start in range(0, out_ref.shape[1], 4):
+        tiles = []
+        for i in range(3):
+            at = pl.ds((3 * start // 4 + i) * LANES, LANES)
+            tiles.append((a_ref[:, at] + b_ref[:, at]) + (c_ref[:, at] + d_ref[:, at]))
+        for i, row in enumerate(load_rows(tiles, 0)):
+            out_ref[:, start + i, :] = row[:, :WIDTH]
+
+
+def copies_kernel(in_ref, out_ref):
+    piece = in_ref[0]
+    for i in range(1, in_ref.shape[0]):
+        piece = piece + in_ref[i]
+    for i in range(out_ref.shape[0]):
+        out_ref[i] = piece
 
 
 def place_kernel(factor, layer_ref, whole_ref, out_ref):
@@ -157,22 +217,27 @@
     def move(cells, step):
         return lax.ppermute(cells, "chan", [(i, (i + step) % chans) for i in range(chans)])
 
-    def spread(piece, groups):
-        stacked = jnp.broadcast_to(piece[None], (8,) + piece.shape)
-        return lax.all_to_all(stacked, "space", 0, 0, axis_index_groups=groups, tiled=True)
+    def exchange(parts, groups):
+        return lax.all_to_all(parts, "space", 0, 0, axis_index_groups=groups, tiled=True)
+
+    def added(parts, copies):
+        return call(copies_kernel, shape(copies, *parts.shape[1:], dtype=wide), 1)(parts)
 
     def by_row(cells):
         return jnp.pad(cells.transpose(2, 0, 1), ((0, 0), (0, 0), (0, LANES - width)))
 
-    cells = by_row(grad_out)
-    edges = call(edges_kernel, shape(chan_dev, LANES), 1)(cells)
+    cells = rows * width
+    edges, dense = call(edges_kernel, (shape(chan_dev, LANES), shape(chan_dev, cells)), 1)(
+        by_row(grad_out)
+    )
     left = lax.ppermute(edges, "space", [(i, i + 1) for i in range(spaces - 1)])
     right = lax.ppermute(edges, "space", [(i + 1, i) for i in range(spaces - 1)])
     edges, field = lax.optimization_barrier((edges, field))
-    source = by_row(field)
+    bordered, source = call(
+        border_kernel, (shape(chan_dev, cells + LANES), shape(chan_dev, cells + LANES)), 4
+    )(dense, left, right, by_row(field))
+    grads = [move(bordered, 4), bordered, move(bordered, -4)]
     sources = [move(source, 1), source, move(source, -1), move(source, -2)]
-    bordered = call(border_kernel, shape(rows, chan_dev, LANES), 3)(cells, left, right)
-    grads = [move(bordered, 4), bordered, move(bordered, -4)]
 
     first, last = filters[:, : 2 * chan_dev], filters[:, -chan_dev:]
     own = jnp.concatenate([last, filters, first], axis=1)
@@ -191,32 +256,33 @@
             shape(8, 3 * chan_dev, LANES, dtype=wide),
             shape(9 * chan_dev, (rows + 4) * LANES),
         ),
-        8,
+        9,
         1,
         [pltpu.VMEM((4 * chan_dev, rows * LANES), kind)],
-    )(third, *sources, *grads)
-
-    piece = lax.all_to_all(parts, "space", 0, 0, axis_index_groups=across, tiled=True).sum(0)
+    )(third, own, *grads, *sources)
+    blocks = call(
+        inputs_kernel, tuple(shape(chan_dev, cells, dtype=wide) for _ in range(4)), 2
+    )(shifted, own)
+
+    piece = added(exchange(parts, across), 1)
+    piece, *blocks = lax.optimization_barrier((piece, *blocks))
     home = [
         (s * chans + c, s * chans + (c - 1 + s // (NY * NCORE)) % chans)
         for s in range(spaces)
         for c in range(chans)
     ]
     piece = lax.ppermute(piece, ("space", "chan"), home)
-    piece = spread(piece, along).sum(0)
-    whole = spread(piece, across)
+    others = [move(blocks[0], -1), move(blocks[2], 1), move(blocks[3], 2)]
+    piece = added(exchange(added(piece, 8), along), 8)
+    whole = exchange(piece, across)
     grad_filters = call(
         functools.partial(place_kernel, factor),
         shape(9, chan_dev, 12 * chan_dev, dtype=wide),
         2,
         1,
     )(layer[None], whole)
-
-    blocks = call(
-        inputs_kernel, tuple(shape(rows, chan_dev, LANES, dtype=wide) for _ in range(4)), 2
-    )(shifted, own)
-    total = blocks[1] + move(blocks[0], -1) + move(blocks[2], 1) + move(blocks[3], 2)
-    return (total[..., :width].transpose(1, 2, 0), grad_filters)
+    total = call(total_kernel, shape(chan_dev, rows, width, dtype=wide), 4)(blocks[1], *others)
+    return (total.transpose(0, 2, 1), grad_filters)
 
 
 def solution(mesh):

time: 122 us -> 107 us (0.88)
  the two profiles are of different devices: /device:TPU:78 before, /device:TPU:72 now
where the time goes in v3:
time: 107 us
  starting transfers between devices  62.2 us (58%)
  waiting for transfers between devices  30.6 us (29%)
  Pallas kernels  9.04 us (8%)
  local copies, waits for them, and re-layouts  2.12 us (2%)
  matrix products  1.62 us (2%)
    ppermute x8, starting transfers between devices, move(): lax.ppermute(cells, 'chan', [(i, (i + step) % chans) for i in range(chans)])  40.3 us
    ppermute x8, waiting for transfers between devices, move(): lax.ppermute(cells, 'chan', [(i, (i + step) % chans) for i in range(chans)])  19.1 us
    all_to_all x3, starting transfers between devices, exchange(): lax.all_to_all(parts, 'space', 0, 0, axis_index_groups=groups, tiled=True)  15 us
    all_to_all x3, waiting for transfers between devices, exchange(): lax.all_to_all(parts, 'space', 0, 0, axis_index_groups=groups, tiled=True)  6 us
    pallas_call x1, Pallas kernels, per_device(): call(weights_kernel, (shape(8, 3 * chan_dev, LANES, dtype=wide), shape(9...  3.86 us
    ppermute x1, waiting for transfers between devices, per_device(): piece = lax.ppermute(piece, ('space', 'chan'), home)  3.18 us
    ppermute x1, starting transfers between devices, per_device(): piece = lax.ppermute(piece, ('space', 'chan'), home)  2.66 us
    ppermute x1, starting transfers between devices, per_device(): left = lax.ppermute(edges, 'space', [(i, i + 1) for i in range(spaces - 1)])  2.41 us
  transfers between devices with their start and end apart: 14, of which 8 were waited for; matrix products, arithmetic and copies ran while one was open for 2% of the time, Pallas kernels for 3%

profile of v3, /device:TPU:72, one launch (start us, length us, event | category | flops | bytes accessed | tf_op | source)
XLA Modules:
  0.0 106.6 jit_solution(6643274828747318664)
XLA Ops:
  0.7 1.1 %copy.16 = bf16[24,96,32]{1,0,2:T(8,128)(2,1)S(1)} copy(bf16[24,96,32]{1,2,0:T(8,128)(2,1)} %param.4) | data formatting | bytes 294912 | tf_op args[1]
  1.8 0.2 shard_map.50
  2.0 1.9 %collective-permute-start.1 = (bf16[24,128]{1,0:T(8,128)(2,1)S(1)}, bf16[24,128]{1,0:T(8,128)(2,1)S(1)}, u32[]{:S(2)}, u32[]{:S(2)}) collective-permute-start(bf16[24,128]{1,0:T(8,128)(2,1)S(1)} %get-tuple-element.19), channel_id=1, source_target_pairs={{12,0},{24,12},{36,24},{48,36},{60,48},{72,60},{84,72},{96,84},{10... | collective-permute-start | bytes 18440 | tf_op jit(solution)/shard_map/ppermute | solution.py:234
  3.9 2.4 %collective-permute-start = (bf16[24,128]{1,0:T(8,128)(2,1)S(1)}, bf16[24,128]{1,0:T(8,128)(2,1)S(1)}, u32[]{:S(2)}, u32[]{:S(2)}) collective-permute-start(bf16[24,128]{1,0:T(8,128)(2,1)S(1)} %get-tuple-element.19), channel_id=1, source_target_pairs={{0,12},{12,24},{24,36},{36,48},{48,60},{60,72},{72,84},{84,96},{96... | collective-permute-start | bytes 18440 | tf_op jit(solution)/shard_map/ppermute | solution.py:233
  6.6 2.3 %collective-permute-done.left_ref = bf16[24,128]{1,0:T(8,128)(2,1)S(1)} collective-permute-done((bf16[24,128]{1,0:T(8,128)(2,1)S(1)}, bf16[24,128]{1,0:T(8,128)(2,1)S(1)}, u32[]{:S(2)}, u32[]{:S(2)}) %collective-permute-start) | collective-permute-done | bytes 6176 | tf_op jit(solution)/shard_map/ppermute | solution.py:233
  9.0 13.7 %collective-permute-start.3 = (bf16[24,3200]{1,0:T(8,128)(2,1)S(1)}, bf16[24,3200]{1,0:T(8,128)(2,1)S(1)}, u32[]{:S(2)}, u32[]{:S(2)}) collective-permute-start(bf16[24,3200]{1,0:T(8,128)(2,1)S(1)} %get-tuple-element.21.refs_1_), channel_id=1, source_target_pairs={{0,8},{1,9},{2,10},{3,11},{4,0},{5,1},{6,2},{7,3},{8,4},{9,5},{10,... | collective-permute-start | bytes 460808 | tf_op jit(solution)/shard_map/ppermute | solution.py:218
  22.7 1.9 %collective-permute-start.2 = (bf16[24,3200]{1,0:T(8,128)(2,1)S(1)}, bf16[24,3200]{1,0:T(8,128)(2,1)S(1)}, u32[]{:S(2)}, u32[]{:S(2)}) collective-permute-start(bf16[24,3200]{1,0:T(8,128)(2,1)S(1)} %get-tuple-element.21.refs_1_), channel_id=1, source_target_pairs={{0,4},{1,5},{2,6},{3,7},{4,8},{5,9},{6,10},{7,11},{8,0},{9,1},{10,... | collective-permute-start | bytes 460808 | tf_op jit(solution)/shard_map/ppermute | solution.py:218
  24.6 7.9 %collective-permute-start.6 = (bf16[24,3200]{1,0:T(8,128)(2,1)S(1)}, bf16[24,3200]{1,0:T(8,128)(2,1)S(1)}, u32[]{:S(2)}, u32[]{:S(2)}) collective-permute-start(bf16[24,3200]{1,0:T(8,128)(2,1)S(1)} %get-tuple-element.22.refs_4_), channel_id=1, source_target_pairs={{0,10},{1,11},{2,0},{3,1},{4,2},{5,3},{6,4},{7,5},{8,6},{9,7},{10,... | collective-permute-start | bytes 460808 | tf_op jit(solution)/shard_map/ppermute | solution.py:218
  32.5 2.5 %collective-permute-start.5 = (bf16[24,3200]{1,0:T(8,128)(2,1)S(1)}, bf16[24,3200]{1,0:T(8,128)(2,1)S(1)}, u32[]{:S(2)}, u32[]{:S(2)}) collective-permute-start(bf16[24,3200]{1,0:T(8,128)(2,1)S(1)} %get-tuple-element.22.refs_4_), channel_id=1, source_target_pairs={{0,11},{1,0},{2,1},{3,2},{4,3},{5,4},{6,5},{7,6},{8,7},{9,8},{10,9... | collective-permute-start | bytes 460808 | tf_op jit(solution)/shard_map/ppermute | solution.py:218
  34.9 3.4 %collective-permute-start.4 = (bf16[24,3200]{1,0:T(8,128)(2,1)S(1)}, bf16[24,3200]{1,0:T(8,128)(2,1)S(1)}, u32[]{:S(2)}, u32[]{:S(2)}) collective-permute-start(bf16[24,3200]{1,0:T(8,128)(2,1)S(1)} %get-tuple-element.22.refs_4_), channel_id=1, source_target_pairs={{0,1},{1,2},{2,3},{3,4},{4,5},{5,6},{6,7},{7,8},{8,9},{9,10},{10,1... | collective-permute-start | bytes 460808 | tf_op jit(solution)/shard_map/ppermute | solution.py:218
  38.3 1.6 %convolution_convert_fusion = bf16[9,96,72]{1,2,0:T(8,128)(2,1)S(1)} fusion(s32[]{:T(128)S(6)} %select_n.34, bf16[9,24,288]{2,1,0:T(8,128)(2,1)S(1)} %slice-done, bf16[9,288,288]{2,1,0:T(8,128)(2,1)} %param.5, bf16[9,48,288]{2,1,0:T(8,128)(2,1)S(1)} %slice-done.1, s32[72]{0:T(128)S(1)} %fusion.7), kind=kOutput, calls=%fused_computation.3 | convolution fusion | flops 37407744 | bytes 1990948 | tf_op jit(solution)/shard_map/kio,op->kip/dot_general | solution.py:248
  40.2 1.0 collective-permute-done.6.refs_6_
  41.1 2.6 %collective-permute-done.5.refs_5_ = bf16[24,3200]{1,0:T(8,128)(2,1)S(1)} collective-permute-done((bf16[24,3200]{1,0:T(8,128)(2,1)S(1)}, bf16[24,3200]{1,0:T(8,128)(2,1)S(1)}, u32[]{:S(2)}, u32[]{:S(2)}) %collective-permute-start.5) | collective-permute-done | bytes 153632 | tf_op jit(solution)/shard_map/ppermute | solution.py:218
  43.7 2.8 %collective-permute-done.4.refs_3_ = bf16[24,3200]{1,0:T(8,128)(2,1)S(1)} collective-permute-done((bf16[24,3200]{1,0:T(8,128)(2,1)S(1)}, bf16[24,3200]{1,0:T(8,128)(2,1)S(1)}, u32[]{:S(2)}, u32[]{:S(2)}) %collective-permute-start.4) | collective-permute-done | bytes 153632 | tf_op jit(solution)/shard_map/ppermute | solution.py:218
  46.5 3.9 %shard_map.52 = (f32[8,72,128]{2,1,0:T(8,128)}, bf16[216,4608]{1,0:T(8,128)(2,1)S(1)}) custom-call(s32[1]{0:T(128)} %bitcast.third_ref, bf16[3,96,216]{2,1,0:T(8,128)(2,1)S(1)} %copy.11.own_ref.filters_ref, bf16[24,3200]{1,0:T(8,128)(2,1)S(1)} %collective-permute-done.2.refs_0_, bf16[24,3200]{1,0:T(8,128)(2,1)S(1)} %get-tuple-element.21.refs_1_, ...), custom_call_target="tpu_custom_call" | custom-call | tf_op jit(solution)/shard_map/pallas_call | solution.py:253
  50.4 4.3 %all-to-all-start = ((f32[8,72,128]{2,1,0:T(8,128)}), f32[8,72,128]{2,1,0:T(8,128)S(1)}, u32[]{:S(2)}, u32[]{:S(2)}) async-start(f32[8,72,128]{2,1,0:T(8,128)} %get-tuple-element.23), calls=%async_computation | async-start | bytes 589824 | tf_op jit(solution)/shard_map/all_to_all | solution.py:221
  54.7 1.2 %shard_map.54 = (f32[24,3072]{1,0:T(8,128)S(1)}, f32[24,3072]{1,0:T(8,128)S(1)}, f32[24,3072]{1,0:T(8,128)S(1)}, f32[24,3072]{1,0:T(8,128)S(1)}) custom-call(bf16[216,4608]{1,0:T(8,128)(2,1)S(1)} %get-tuple-element.24.shifted_ref, bf16[3,96,216]{2,1,0:T(8,128)(2,1)S(1)} %copy.11.own_ref.filters_ref), custom_call_target="tpu_custom_call" | custom-call | tf_op jit(solution)/shard_map/pallas_call | solution.py:263
  55.8 0.7 copy-done
  56.5 6.0 %all-to-all-done.in_ref = f32[8,72,128]{2,1,0:T(8,128)S(1)} async-done(((f32[8,72,128]{2,1,0:T(8,128)}), f32[8,72,128]{2,1,0:T(8,128)S(1)}, u32[]{:S(2)}, u32[]{:S(2)}) %all-to-all-start) | async-done | bytes 294944 | tf_op jit(solution)/shard_map/all_to_all | solution.py:221
  62.6 2.7 %collective-permute-start.10 = (f32[1,72,128]{2,1,0:T(8,128)S(1)}, f32[1,72,128]{2,1,0:T(8,128)S(1)}, u32[]{:S(2)}, u32[]{:S(2)}) collective-permute-start(f32[1,72,128]{2,1,0:T(8,128)S(1)} %shard_map.53), channel_id=1, source_target_pairs={{0,11},{1,0},{2,1},{3,2},{4,3},{5,4},{6,5},{7,6},{8,7},{9,8},{10,9... | collective-permute-start | bytes 110600 | tf_op jit(solution)/shard_map/ppermute | solution.py:274
  65.2 3.2 %collective-permute-done.10.in_ref = f32[1,72,128]{2,1,0:T(8,128)S(1)} collective-permute-done((f32[1,72,128]{2,1,0:T(8,128)S(1)}, f32[1,72,128]{2,1,0:T(8,128)S(1)}, u32[]{:S(2)}, u32[]{:S(2)}) %collective-permute-start.10) | collective-permute-done | bytes 36896 | tf_op jit(solution)/shard_map/ppermute | solution.py:274
  68.4 0.7 shard_map.56
  69.2 7.2 %all-to-all-start.1 = ((f32[8,72,128]{2,1,0:T(8,128)}), f32[8,72,128]{2,1,0:T(8,128)S(1)}, u32[]{:S(2)}, u32[]{:S(2)}) async-start(f32[8,72,128]{2,1,0:T(8,128)} %shard_map.56), calls=%async_computation.1 | async-start | bytes 589824 | tf_op jit(solution)/shard_map/all_to_all | solution.py:221
  76.3 3.0 %collective-permute-start.7 = (f32[24,3072]{1,0:T(8,128)}, f32[24,3072]{1,0:T(8,128)S(1)}, u32[]{:S(2)}, u32[]{:S(2)}) collective-permute-start(f32[24,3072]{1,0:T(8,128)} %copy-done), channel_id=1, source_target_pairs={{0,11},{1,0},{2,1},{3,2},{4,3},{5,4},{6,5},{7,6},{8,7},{9,8},{10,9... | collective-permute-start | bytes 884744 | tf_op jit(solution)/shard_map/ppermute | solution.py:218
  79.3 2.8 %collective-permute-start.8 = (f32[24,3072]{1,0:T(8,128)S(1)}, f32[24,3072]{1,0:T(8,128)S(1)}, u32[]{:S(2)}, u32[]{:S(2)}) collective-permute-start(f32[24,3072]{1,0:T(8,128)S(1)} %get-tuple-element.31), channel_id=1, source_target_pairs={{0,1},{1,2},{2,3},{3,4},{4,5},{5,6},{6,7},{7,8},{8,9},{9,10},{10,1... | collective-permute-start | bytes 884744 | tf_op jit(solution)/shard_map/ppermute | solution.py:218
  82.2 5.2 %collective-permute-start.9 = (f32[24,3072]{1,0:T(8,128)S(1)}, f32[24,3072]{1,0:T(8,128)S(1)}, u32[]{:S(2)}, u32[]{:S(2)}) collective-permute-start(f32[24,3072]{1,0:T(8,128)S(1)} %get-tuple-element.32), channel_id=1, source_target_pairs={{0,2},{1,3},{2,4},{3,5},{4,6},{5,7},{6,8},{7,9},{8,10},{9,11},{10,... | collective-permute-start | bytes 884744 | tf_op jit(solution)/shard_map/ppermute | solution.py:218
  87.4 0.7 shard_map.57
  88.1 3.5 %all-to-all-start.2 = ((f32[8,72,128]{2,1,0:T(8,128)}), f32[8,72,128]{2,1,0:T(8,128)S(1)}, u32[]{:S(2)}, u32[]{:S(2)}) async-start(f32[8,72,128]{2,1,0:T(8,128)} %shard_map.57), calls=%async_computation.2 | async-start | bytes 589824 | tf_op jit(solution)/shard_map/all_to_all | solution.py:221
  91.6 2.9 %collective-permute-done.8.c_ref = f32[24,3072]{1,0:T(8,128)S(1)} collective-permute-done((f32[24,3072]{1,0:T(8,128)S(1)}, f32[24,3072]{1,0:T(8,128)S(1)}, u32[]{:S(2)}, u32[]{:S(2)}) %collective-permute-start.8) | collective-permute-done | bytes 294944 | tf_op jit(solution)/shard_map/ppermute | solution.py:218
  94.5 9.9 %collective-permute-done.9.d_ref = f32[24,3072]{1,0:T(8,128)S(1)} collective-permute-done((f32[24,3072]{1,0:T(8,128)S(1)}, f32[24,3072]{1,0:T(8,128)S(1)}, u32[]{:S(2)}, u32[]{:S(2)}) %collective-permute-start.9) | collective-permute-done | bytes 294944 | tf_op jit(solution)/shard_map/ppermute | solution.py:218
  104.4 1.1 %shard_map.55 = f32[24,32,96]{2,1,0:T(8,128)} custom-call(f32[24,3072]{1,0:T(8,128)S(1)} %get-tuple-element.29.a_ref, f32[24,3072]{1,0:T(8,128)S(1)} %collective-permute-done.7.b_ref, f32[24,3072]{1,0:T(8,128)S(1)} %collective-permute-done.8.c_ref, f32[24,3072]{1,0:T(8,128)S(1)} %collective-permute-done.9.d_ref), custom_call_target="tpu_custom_call" | custom-call | tf_op jit(solution)/shard_map/pallas_call | solution.py:284
  105.5 1.1 shard_map.58
  (21 shorter events, 0.5 us)
Async XLA Ops:
  0.6 37.7 %slice-start = ((bf16[9,288,288]{2,1,0:T(8,128)(2,1)}), bf16[9,24,288]{2,1,0:T(8,128)(2,1)S(1)}, s32[]{:S(2)}) async-start(bf16[9,288,288]{2,1,0:T(8,128)(2,1)} %param.5), calls=%async_computation.3 | async-start | bytes 331776 | tf_op jit(solution)/shard_map/slice | solution.py:242
  0.6 37.7 %slice-start.1 = ((bf16[9,288,288]{2,1,0:T(8,128)(2,1)}), bf16[9,48,288]{2,1,0:T(8,128)(2,1)S(1)}, s32[]{:S(2)}) async-start(bf16[9,288,288]{2,1,0:T(8,128)(2,1)} %param.5), calls=%async_computation.4 | async-start | bytes 663552 | tf_op jit(solution)/shard_map/slice | solution.py:242
  0.7 5.8 %copy-start.1 = (bf16[24,96,32]{1,2,0:T(8,128)(2,1)S(1)}, bf16[24,96,32]{1,2,0:T(8,128)(2,1)}, u32[]{:S(2)}) copy-start(bf16[24,96,32]{1,2,0:T(8,128)(2,1)} %param.3) | copy-start | bytes 442372
  2.0 4.6 %collective-permute-start.1 = (bf16[24,128]{1,0:T(8,128)(2,1)S(1)}, bf16[24,128]{1,0:T(8,128)(2,1)S(1)}, u32[]{:S(2)}, u32[]{:S(2)}) collective-permute-start(bf16[24,128]{1,0:T(8,128)(2,1)S(1)} %get-tuple-element.19), channel_id=1, source_target_pairs={{12,0},{24,12},{36,24},{48,36},{60,48},{72,60},{84,72},{96,84},{10... | collective-permute-start | bytes 18440 | tf_op jit(solution)/shard_map/ppermute | solution.py:234
  3.9 4.9 %collective-permute-start = (bf16[24,128]{1,0:T(8,128)(2,1)S(1)}, bf16[24,128]{1,0:T(8,128)(2,1)S(1)}, u32[]{:S(2)}, u32[]{:S(2)}) collective-permute-start(bf16[24,128]{1,0:T(8,128)(2,1)S(1)} %get-tuple-element.19), channel_id=1, source_target_pairs={{0,12},{12,24},{24,36},{36,48},{48,60},{60,72},{72,84},{84,96},{96... | collective-permute-start | bytes 18440 | tf_op jit(solution)/shard_map/ppermute | solution.py:233
  9.0 31.1 %collective-permute-start.3 = (bf16[24,3200]{1,0:T(8,128)(2,1)S(1)}, bf16[24,3200]{1,0:T(8,128)(2,1)S(1)}, u32[]{:S(2)}, u32[]{:S(2)}) collective-permute-start(bf16[24,3200]{1,0:T(8,128)(2,1)S(1)} %get-tuple-element.21.refs_1_), channel_id=1, source_target_pairs={{0,8},{1,9},{2,10},{3,11},{4,0},{5,1},{6,2},{7,3},{8,4},{9,5},{10,... | collective-permute-start | bytes 460808 | tf_op jit(solution)/shard_map/ppermute | solution.py:218
  22.7 17.5 %collective-permute-start.2 = (bf16[24,3200]{1,0:T(8,128)(2,1)S(1)}, bf16[24,3200]{1,0:T(8,128)(2,1)S(1)}, u32[]{:S(2)}, u32[]{:S(2)}) collective-permute-start(bf16[24,3200]{1,0:T(8,128)(2,1)S(1)} %get-tuple-element.21.refs_1_), channel_id=1, source_target_pairs={{0,4},{1,5},{2,6},{3,7},{4,8},{5,9},{6,10},{7,11},{8,0},{9,1},{10,... | collective-permute-start | bytes 460808 | tf_op jit(solution)/shard_map/ppermute | solution.py:218
  24.6 16.5 %collective-permute-start.6 = (bf16[24,3200]{1,0:T(8,128)(2,1)S(1)}, bf16[24,3200]{1,0:T(8,128)(2,1)S(1)}, u32[]{:S(2)}, u32[]{:S(2)}) collective-permute-start(bf16[24,3200]{1,0:T(8,128)(2,1)S(1)} %get-tuple-element.22.refs_4_), channel_id=1, source_target_pairs={{0,10},{1,11},{2,0},{3,1},{4,2},{5,3},{6,4},{7,5},{8,6},{9,7},{10,... | collective-permute-start | bytes 460808 | tf_op jit(solution)/shard_map/ppermute | solution.py:218
  32.5 11.3 %collective-permute-start.5 = (bf16[24,3200]{1,0:T(8,128)(2,1)S(1)}, bf16[24,3200]{1,0:T(8,128)(2,1)S(1)}, u32[]{:S(2)}, u32[]{:S(2)}) collective-permute-start(bf16[24,3200]{1,0:T(8,128)(2,1)S(1)} %get-tuple-element.22.refs_4_), channel_id=1, source_target_pairs={{0,11},{1,0},{2,1},{3,2},{4,3},{5,4},{6,5},{7,6},{8,7},{9,8},{10,9... | collective-permute-start | bytes 460808 | tf_op jit(solution)/shard_map/ppermute | solution.py:218
  34.9 11.6 %collective-permute-start.4 = (bf16[24,3200]{1,0:T(8,128)(2,1)S(1)}, bf16[24,3200]{1,0:T(8,128)(2,1)S(1)}, u32[]{:S(2)}, u32[]{:S(2)}) collective-permute-start(bf16[24,3200]{1,0:T(8,128)(2,1)S(1)} %get-tuple-element.22.refs_4_), channel_id=1, source_target_pairs={{0,1},{1,2},{2,3},{3,4},{4,5},{5,6},{6,7},{7,8},{8,9},{9,10},{10,1... | collective-permute-start | bytes 460808 | tf_op jit(solution)/shard_map/ppermute | solution.py:218
  50.4 12.2 %all-to-all-start = ((f32[8,72,128]{2,1,0:T(8,128)}), f32[8,72,128]{2,1,0:T(8,128)S(1)}, u32[]{:S(2)}, u32[]{:S(2)}) async-start(f32[8,72,128]{2,1,0:T(8,128)} %get-tuple-element.23), calls=%async_computation | async-start | bytes 589824 | tf_op jit(solution)/shard_map/all_to_all | solution.py:221
  55.8 0.7 copy-start
  62.6 5.9 %collective-permute-start.10 = (f32[1,72,128]{2,1,0:T(8,128)S(1)}, f32[1,72,128]{2,1,0:T(8,128)S(1)}, u32[]{:S(2)}, u32[]{:S(2)}) collective-permute-start(f32[1,72,128]{2,1,0:T(8,128)S(1)} %shard_map.53), channel_id=1, source_target_pairs={{0,11},{1,0},{2,1},{3,2},{4,3},{5,4},{6,5},{7,6},{8,7},{9,8},{10,9... | collective-permute-start | bytes 110600 | tf_op jit(solution)/shard_map/ppermute | solution.py:274
  69.2 18.2 %all-to-all-start.1 = ((f32[8,72,128]{2,1,0:T(8,128)}), f32[8,72,128]{2,1,0:T(8,128)S(1)}, u32[]{:S(2)}, u32[]{:S(2)}) async-start(f32[8,72,128]{2,1,0:T(8,128)} %shard_map.56), calls=%async_computation.1 | async-start | bytes 589824 | tf_op jit(solution)/shard_map/all_to_all | solution.py:221
  76.3 15.3 %collective-permute-start.7 = (f32[24,3072]{1,0:T(8,128)}, f32[24,3072]{1,0:T(8,128)S(1)}, u32[]{:S(2)}, u32[]{:S(2)}) collective-permute-start(f32[24,3072]{1,0:T(8,128)} %copy-done), channel_id=1, source_target_pairs={{0,11},{1,0},{2,1},{3,2},{4,3},{5,4},{6,5},{7,6},{8,7},{9,8},{10,9... | collective-permute-start | bytes 884744 | tf_op jit(solution)/shard_map/ppermute | solution.py:218
  79.3 15.1 %collective-permute-start.8 = (f32[24,3072]{1,0:T(8,128)S(1)}, f32[24,3072]{1,0:T(8,128)S(1)}, u32[]{:S(2)}, u32[]{:S(2)}) collective-permute-start(f32[24,3072]{1,0:T(8,128)S(1)} %get-tuple-element.31), channel_id=1, source_target_pairs={{0,1},{1,2},{2,3},{3,4},{4,5},{5,6},{6,7},{7,8},{8,9},{9,10},{10,1... | collective-permute-start | bytes 884744 | tf_op jit(solution)/shard_map/ppermute | solution.py:218
  82.2 22.2 %collective-permute-start.9 = (f32[24,3072]{1,0:T(8,128)S(1)}, f32[24,3072]{1,0:T(8,128)S(1)}, u32[]{:S(2)}, u32[]{:S(2)}) collective-permute-start(f32[24,3072]{1,0:T(8,128)S(1)} %get-tuple-element.32), channel_id=1, source_target_pairs={{0,2},{1,3},{2,4},{3,5},{4,6},{5,7},{6,8},{7,9},{8,10},{9,11},{10,... | collective-permute-start | bytes 884744 | tf_op jit(solution)/shard_map/ppermute | solution.py:218
  88.1 17.4 %all-to-all-start.2 = ((f32[8,72,128]{2,1,0:T(8,128)}), f32[8,72,128]{2,1,0:T(8,128)S(1)}, u32[]{:S(2)}, u32[]{:S(2)}) async-start(f32[8,72,128]{2,1,0:T(8,128)} %shard_map.57), calls=%async_computation.2 | async-start | bytes 589824 | tf_op jit(solution)/shard_map/all_to_all | solution.py:221

commit v4 on v3

--- a/solution.py
+++ b/solution.py
@@ -27,20 +27,24 @@
     return lax.broadcasted_iota(jnp.int32, (chans, LANES), 1)
 
 
-def edges_kernel(cells_ref, edges_ref, dense_ref):
-    rows, chans = cells_ref.shape[0], cells_ref.shape[1]
-    lane = lane_index(chans)
-    packed = jnp.zeros((chans, LANES), jnp.float32)
-    for start in range(0, rows, 4):
-        group = [cells_ref[start + i].astype(jnp.float32) for i in range(4)]
-        store_dense(dense_ref, start, group)
-        for i in range(4):
-            r = start + i
-            tail_at, head_at = 4 * r, (4 * r + WIDTH + 2) % LANES
-            tail = pltpu.roll(group[i], (tail_at - (WIDTH - 2)) % LANES, 1)
-            head = pltpu.roll(group[i], head_at, 1)
-            packed = jnp.where((lane >= tail_at) & (lane < tail_at + 2), tail, packed)
-            packed = jnp.where((lane >= head_at) & (lane < head_at + 2), head, packed)
+def pack_kernel(cells_ref, dense_ref):
+    for start in range(0, cells_ref.shape[0], 4):
+        store_dense(dense_ref, start, [cells_ref[start + i].astype(jnp.float32) for i in range(4)])
+
+
+def edges_kernel(near_ref, own_ref, far_ref, edges_ref):
+    refs = (near_ref, own_ref, far_ref)
+    rows = near_ref.shape[1] // WIDTH
+    lane = lane_index(3 * near_ref.shape[0])
+    packed = jnp.zeros(edges_ref.shape, jnp.float32)
+    for r in range(rows):
+        for column, to in ((WIDTH - 2, 4 * r), (0, (4 * r + WIDTH + 2) % LANES)):
+            tile, at = divmod(r * WIDTH + column, LANES)
+            cut = slice(tile * LANES, (tile + 1) * LANES)
+            block = jnp.concatenate([ref[:, cut].astype(jnp.float32) for ref in refs], axis=0)
+            turn = (to - at) % LANES
+            block = pltpu.roll(block, turn, 1) if turn else block
+            packed = jnp.where((lane >= to) & (lane < to + 2), block, packed)
     edges_ref[...] = packed.astype(edges_ref.dtype)
 
 
@@ -66,32 +70,18 @@
     return rows
 
 
-def border_kernel(dense_ref, left_ref, right_ref, source_ref, out_ref, packed_ref):
-    for start in range(0, source_ref.shape[0], 4):
-        group = [source_ref[start + i].astype(jnp.float32) for i in range(4)]
-        store_dense(packed_ref, start, group)
-    cells = dense_ref.shape[1]
-    packed_ref[:, cells:] = jnp.zeros((dense_ref.shape[0], LANES), packed_ref.dtype)
-    lane = lane_index(dense_ref.shape[0])
-    left = left_ref[...].astype(jnp.float32)
-    right = right_ref[...].astype(jnp.float32)
-    out_ref[:, :cells] = dense_ref[...]
-    out_ref[:, cells:] = jnp.where(lane % 4 < 2, left, right).astype(out_ref.dtype)
-
-
-def weights_kernel(third_ref, own_ref, *refs):
-    g_refs, x_refs, (parts_ref, shifted_ref, window_ref) = refs[:3], refs[3:7], refs[7:]
-    chans = x_refs[0].shape[0]
-    rows = refs[8].shape[1] // LANES - 4
+def shift_kernel(third_ref, near_ref, own_ref, far_ref, left_ref, right_ref, shifted_ref):
+    refs = (near_ref, own_ref, far_ref)
+    chans = near_ref.shape[0]
+    rows = near_ref.shape[1] // WIDTH
     third = third_ref[0]
     kind = shifted_ref.dtype
     blank = jnp.zeros((9 * chans, 2 * LANES), kind)
     shifted_ref[:, : 2 * LANES] = blank
     shifted_ref[:, (rows + 2) * LANES :] = blank
-    lane_x, lane_g = lane_index(4 * chans), lane_index(3 * chans)
-
-    def pick(at):
-        near, own, far = [g[:, at : at + LANES].astype(jnp.float32) for g in g_refs]
+    lane = lane_index(3 * chans)
+
+    def ordered(near, own, far):
         orders = ((own, far, near), (near, own, far), (far, near, own))
         return jnp.concatenate(
             [
@@ -101,23 +91,39 @@
             axis=0,
         )
 
-    sides = pick(rows * WIDTH)
+    sides = jnp.where(
+        lane % 4 < 2, left_ref[...].astype(jnp.float32), right_ref[...].astype(jnp.float32)
+    )
+    sides = ordered(*[sides[m * chans : (m + 1) * chans] for m in range(3)])
     for start in range(0, rows, 4):
         ats = [(3 * start // 4 + i) * LANES for i in range(3)]
         tiles = [
-            jnp.concatenate([x[:, at : at + LANES].astype(jnp.float32) for x in x_refs], axis=0)
+            ordered(*[ref[:, at : at + LANES].astype(jnp.float32) for ref in refs]) for at in ats
+        ]
+        for i, row in enumerate(load_rows(tiles, 2)):
+            side = pltpu.roll(sides, (-4 * (start + i)) % LANES, 1) if start + i else sides
+            row = jnp.where((lane >= 2) & (lane < WIDTH + 2), row, side)
+            row = jnp.where(lane < WIDTH + 4, row, 0.0)
+            taps = [pltpu.roll(row, LANES - 4, 1), pltpu.roll(row, LANES - 2, 1), row]
+            at = (start + i + 2) * LANES
+            shifted_ref[:, at : at + LANES] = jnp.concatenate(taps, axis=0).astype(kind)
+
+
+def weights_kernel(own_ref, x0, x1, x2, x3, shifted_ref, parts_ref, window_ref):
+    refs = (x0, x1, x2, x3)
+    chans = x0.shape[0]
+    rows = x0.shape[1] // WIDTH
+    lane = lane_index(4 * chans)
+    for start in range(0, rows, 4):
+        ats = [(3 * start // 4 + i) * LANES for i in range(3)]
+        tiles = [
+            jnp.concatenate([x[:, at : at + LANES].astype(jnp.float32) for x in refs], axis=0)
             for at in ats
         ]
         for i, row in enumerate(load_rows(tiles, 0)):
             at = (start + i) * LANES
-            window_ref[:, at : at + LANES] = jnp.where(lane_x < WIDTH, row, 0.0).astype(kind)
-        for i, row in enumerate(load_rows([pick(at) for at in ats], 2)):
-            side = pltpu.roll(sides, (-4 * (start + i)) % LANES, 1) if start + i else sides
-            row = jnp.where((lane_g >= 2) & (lane_g < WIDTH + 2), row, side)
-            row = jnp.where(lane_g < WIDTH + 4, row, 0.0)
-            taps = [pltpu.roll(row, LANES - 4, 1), pltpu.roll(row, LANES - 2, 1), row]
-            at = (start + i + 2) * LANES
-            shifted_ref[:, at : at + LANES] = jnp.concatenate(taps, axis=0).astype(kind)
+            row = jnp.where(lane < WIDTH, row, 0.0)
+            window_ref[:, at : at + LANES] = row.astype(window_ref.dtype)
     for b in range(3):
         at = (4 - 2 * b) * LANES
         part = lax.dot_general(
@@ -227,17 +233,13 @@
         return jnp.pad(cells.transpose(2, 0, 1), ((0, 0), (0, 0), (0, LANES - width)))
 
     cells = rows * width
-    edges, dense = call(edges_kernel, (shape(chan_dev, LANES), shape(chan_dev, cells)), 1)(
-        by_row(grad_out)
-    )
+    dense = call(pack_kernel, shape(chan_dev, cells), 1)(by_row(grad_out))
+    grads = [move(dense, 4), dense, move(dense, -4)]
+    source = call(pack_kernel, shape(chan_dev, cells), 1)(by_row(field))
+    sources = [move(source, 1), source, move(source, -1), move(source, -2)]
+    edges = call(edges_kernel, shape(3 * chan_dev, LANES), 3)(*grads)
     left = lax.ppermute(edges, "space", [(i, i + 1) for i in range(spaces - 1)])
     right = lax.ppermute(edges, "space", [(i + 1, i) for i in range(spaces - 1)])
-    edges, field = lax.optimization_barrier((edges, field))
-    bordered, source = call(
-        border_kernel, (shape(chan_dev, cells + LANES), shape(chan_dev, cells + LANES)), 4
-    )(dense, left, right, by_row(field))
-    grads = [move(bordered, 4), bordered, move(bordered, -4)]
-    sources = [move(source, 1), source, move(source, -1), move(source, -2)]
 
     first, last = filters[:, : 2 * chan_dev], filters[:, -chan_dev:]
     own = jnp.concatenate([last, filters, first], axis=1)
@@ -250,16 +252,16 @@
     own = own.transpose(1, 2, 0, 3).reshape(3, 4 * chan_dev, 9 * chan_dev)
 
     third = (layer // 4)[None]
-    parts, shifted = call(
+    shifted = call(shift_kernel, shape(9 * chan_dev, (rows + 4) * LANES), 6, 1)(
+        third, *grads, left, right
+    )
+    parts = call(
         weights_kernel,
-        (
-            shape(8, 3 * chan_dev, LANES, dtype=wide),
-            shape(9 * chan_dev, (rows + 4) * LANES),
-        ),
-        9,
-        1,
+        shape(8, 3 * chan_dev, LANES, dtype=wide),
+        6,
+        0,
         [pltpu.VMEM((4 * chan_dev, rows * LANES), kind)],
-    )(third, own, *grads, *sources)
+    )(own, *sources, shifted)
     blocks = call(
         inputs_kernel, tuple(shape(chan_dev, cells, dtype=wide) for _ in range(4)), 2
     )(shifted, own)

time: 107 us -> 105 us (0.981)
  the two profiles are of different devices: /device:TPU:72 before, /device:TPU:8 now
where the time goes in v4:
time: 105 us; the launch traced here: 104 us
  starting transfers between devices  69.6 us (66%)
  waiting for transfers between devices  18.4 us (18%)
  Pallas kernels  10.8 us (10%)
  local copies, waits for them, and re-layouts  3.03 us (3%)
  matrix products  1.57 us (1%)
    ppermute x8, starting transfers between devices, move(): lax.ppermute(cells, 'chan', [(i, (i + step) % chans) for i in range(chans)])  41.8 us
    all_to_all x3, starting transfers between devices, exchange(): lax.all_to_all(parts, 'space', 0, 0, axis_index_groups=groups, tiled=True)  16.7 us
    ppermute x8, waiting for transfers between devices, move(): lax.ppermute(cells, 'chan', [(i, (i + step) % chans) for i in range(chans)])  10.8 us
    all_to_all x3, waiting for transfers between devices, exchange(): lax.all_to_all(parts, 'space', 0, 0, axis_index_groups=groups, tiled=True)  6 us
    ppermute x1, starting transfers between devices, per_device(): piece = lax.ppermute(piece, ('space', 'chan'), home)  5.44 us
    ppermute x1, starting transfers between devices, per_device(): lax.ppermute(edges, 'space', [(i + 1, i) for i in range(spaces - 1)])  3.64 us
    unnamed x4, local copies, waits for them, and re-layouts  2.78 us
    pallas_call x1, Pallas kernels, per_device(): call(shift_kernel, shape(9 * chan_dev, (rows + 4) * LANES), 6, 1)  2.67 us
  transfers between devices with their start and end apart: 14, of which 4 were waited for; matrix products, arithmetic and copies ran while one was open for 3% of the time, Pallas kernels for 6%

profile of v4, /device:TPU:8, one launch (start us, length us, event | category | flops | bytes accessed | tf_op | source)
XLA Modules:
  0.0 104.3 jit_solution(17009254933827049160)
XLA Ops:
  0.7 1.1 %copy.15 = bf16[24,96,32]{1,0,2:T(8,128)(2,1)S(1)} copy(bf16[24,96,32]{1,2,0:T(8,128)(2,1)} %param.4) | data formatting | bytes 294912 | tf_op args[1]
  1.8 0.1 shard_map.51.own_ref
  1.9 10.9 %collective-permute-start.3 = (bf16[24,3072]{1,0:T(8,128)(2,1)S(1)}, bf16[24,3072]{1,0:T(8,128)(2,1)S(1)}, u32[]{:S(2)}, u32[]{:S(2)}) collective-permute-start(bf16[24,3072]{1,0:T(8,128)(2,1)S(1)} %shard_map.51.own_ref), channel_id=1, source_target_pairs={{0,4},{1,5},{2,6},{3,7},{4,8},{5,9},{6,10},{7,11},{8,0},{9,1},{10,... | collective-permute-start | bytes 442376 | tf_op jit(solution)/shard_map/ppermute | solution.py:224
  12.8 5.6 %collective-permute-start.4 = (bf16[24,3072]{1,0:T(8,128)(2,1)S(1)}, bf16[24,3072]{1,0:T(8,128)(2,1)S(1)}, u32[]{:S(2)}, u32[]{:S(2)}) collective-permute-start(bf16[24,3072]{1,0:T(8,128)(2,1)S(1)} %shard_map.51.own_ref), channel_id=1, source_target_pairs={{0,8},{1,9},{2,10},{3,11},{4,0},{5,1},{6,2},{7,3},{8,4},{9,5},{10,... | collective-permute-start | bytes 442376 | tf_op jit(solution)/shard_map/ppermute | solution.py:224
  18.4 1.0 copy.16
  19.5 3.4 %collective-permute-start = (bf16[24,3072]{1,0:T(8,128)(2,1)S(1)}, bf16[24,3072]{1,0:T(8,128)(2,1)S(1)}, u32[]{:S(2)}, u32[]{:S(2)}) collective-permute-start(bf16[24,3072]{1,0:T(8,128)(2,1)S(1)} %shard_map.50.x1), channel_id=1, source_target_pairs={{0,1},{1,2},{2,3},{3,4},{4,5},{5,6},{6,7},{7,8},{8,9},{9,10},{10,1... | collective-permute-start | bytes 442376 | tf_op jit(solution)/shard_map/ppermute | solution.py:224
  22.9 6.4 %collective-permute-start.1 = (bf16[24,3072]{1,0:T(8,128)(2,1)S(1)}, bf16[24,3072]{1,0:T(8,128)(2,1)S(1)}, u32[]{:S(2)}, u32[]{:S(2)}) collective-permute-start(bf16[24,3072]{1,0:T(8,128)(2,1)S(1)} %shard_map.50.x1), channel_id=1, source_target_pairs={{0,11},{1,0},{2,1},{3,2},{4,3},{5,4},{6,5},{7,6},{8,7},{9,8},{10,9... | collective-permute-start | bytes 442376 | tf_op jit(solution)/shard_map/ppermute | solution.py:224
  29.3 3.9 %collective-permute-start.2 = (bf16[24,3072]{1,0:T(8,128)(2,1)S(1)}, bf16[24,3072]{1,0:T(8,128)(2,1)S(1)}, u32[]{:S(2)}, u32[]{:S(2)}) collective-permute-start(bf16[24,3072]{1,0:T(8,128)(2,1)S(1)} %shard_map.50.x1), channel_id=1, source_target_pairs={{0,10},{1,11},{2,0},{3,1},{4,2},{5,3},{6,4},{7,5},{8,6},{9,7},{10,... | collective-permute-start | bytes 442376 | tf_op jit(solution)/shard_map/ppermute | solution.py:224
  33.3 0.4 shard_map.52
  33.7 1.9 %collective-permute-start.5 = (bf16[72,128]{1,0:T(8,128)(2,1)S(1)}, bf16[72,128]{1,0:T(8,128)(2,1)S(1)}, u32[]{:S(2)}, u32[]{:S(2)}) collective-permute-start(bf16[72,128]{1,0:T(8,128)(2,1)S(1)} %shard_map.52), channel_id=1, source_target_pairs={{0,12},{12,24},{24,36},{36,48},{48,60},{60,72},{72,84},{84,96},{96... | collective-permute-start | bytes 55304 | tf_op jit(solution)/shard_map/ppermute | solution.py:241
  35.7 3.6 %collective-permute-start.6 = (bf16[72,128]{1,0:T(8,128)(2,1)S(1)}, bf16[72,128]{1,0:T(8,128)(2,1)S(1)}, u32[]{:S(2)}, u32[]{:S(2)}) collective-permute-start(bf16[72,128]{1,0:T(8,128)(2,1)S(1)} %shard_map.52), channel_id=1, source_target_pairs={{12,0},{24,12},{36,24},{48,36},{60,48},{72,60},{84,72},{96,84},{10... | collective-permute-start | bytes 55304 | tf_op jit(solution)/shard_map/ppermute | solution.py:242
  39.3 1.6 %convolution_convert_fusion = bf16[9,96,72]{1,2,0:T(8,128)(2,1)S(1)} fusion(s32[]{:T(128)S(6)} %select_n.33, bf16[9,24,288]{2,1,0:T(8,128)(2,1)S(1)} %slice-done, bf16[9,288,288]{2,1,0:T(8,128)(2,1)} %param.5, bf16[9,48,288]{2,1,0:T(8,128)(2,1)S(1)} %slice-done.1, s32[72]{0:T(128)S(1)} %fusion.7), kind=kOutput, calls=%fused_computation.3 | convolution fusion | flops 37407744 | bytes 1990948 | tf_op jit(solution)/shard_map/kio,op->kip/dot_general | solution.py:250
  40.9 0.1 copy.11.own_ref.filters_ref
  41.1 2.7 %shard_map.53.shifted_ref = bf16[216,4608]{1,0:T(8,128)(2,1)S(1)} custom-call(s32[1]{0:T(128)} %bitcast.5.third_ref, bf16[24,3072]{1,0:T(8,128)(2,1)S(1)} %collective-permute-done.3.near_ref, bf16[24,3072]{1,0:T(8,128)(2,1)S(1)} %shard_map.51.own_ref, bf16[24,3072]{1,0:T(8,128)(2,1)S(1)} %collective-permute-done.4.far_ref, ...), custom_call_target="tpu_custom_call" | custom-call | tf_op jit(solution)/shard_map/pallas_call | solution.py:255
  43.8 2.6 %shard_map.54 = f32[8,72,128]{2,1,0:T(8,128)} custom-call(bf16[3,96,216]{2,1,0:T(8,128)(2,1)S(1)} %copy.11.own_ref.filters_ref, bf16[24,3072]{1,0:T(8,128)(2,1)S(1)} %collective-permute-done.x0, bf16[24,3072]{1,0:T(8,128)(2,1)S(1)} %shard_map.50.x1, bf16[24,3072]{1,0:T(8,128)(2,1)S(1)} %collective-permute-done.1.x2, ...), custom_call_target="tpu_custom_call" | custom-call | tf_op jit(solution)/shard_map/pallas_call | solution.py:258
  46.5 5.5 %all-to-all-start = ((f32[8,72,128]{2,1,0:T(8,128)}), f32[8,72,128]{2,1,0:T(8,128)S(1)}, u32[]{:S(2)}, u32[]{:S(2)}) async-start(f32[8,72,128]{2,1,0:T(8,128)} %shard_map.54), calls=%async_computation | async-start | bytes 589824 | tf_op jit(solution)/shard_map/all_to_all | solution.py:227
  52.0 1.2 %shard_map.56 = (f32[24,3072]{1,0:T(8,128)S(1)}, f32[24,3072]{1,0:T(8,128)S(1)}, f32[24,3072]{1,0:T(8,128)S(1)}, f32[24,3072]{1,0:T(8,128)S(1)}) custom-call(bf16[216,4608]{1,0:T(8,128)(2,1)S(1)} %shard_map.53.shifted_ref, bf16[3,96,216]{2,1,0:T(8,128)(2,1)S(1)} %copy.11.own_ref.filters_ref), custom_call_target="tpu_custom_call" | custom-call | tf_op jit(solution)/shard_map/pallas_call | solution.py:265
  53.1 0.7 copy-done
  53.8 6.0 %all-to-all-done.in_ref = f32[8,72,128]{2,1,0:T(8,128)S(1)} async-done(((f32[8,72,128]{2,1,0:T(8,128)}), f32[8,72,128]{2,1,0:T(8,128)S(1)}, u32[]{:S(2)}, u32[]{:S(2)}) %all-to-all-start) | async-done | bytes 294944 | tf_op jit(solution)/shard_map/all_to_all | solution.py:227
  59.9 5.4 %collective-permute-start.10 = (f32[1,72,128]{2,1,0:T(8,128)S(1)}, f32[1,72,128]{2,1,0:T(8,128)S(1)}, u32[]{:S(2)}, u32[]{:S(2)}) collective-permute-start(f32[1,72,128]{2,1,0:T(8,128)S(1)} %shard_map.55), channel_id=1, source_target_pairs={{0,11},{1,0},{2,1},{3,2},{4,3},{5,4},{6,5},{7,6},{8,7},{9,8},{10,9... | collective-permute-start | bytes 110600 | tf_op jit(solution)/shard_map/ppermute | solution.py:276
  65.3 1.6 %collective-permute-done.10.in_ref = f32[1,72,128]{2,1,0:T(8,128)S(1)} collective-permute-done((f32[1,72,128]{2,1,0:T(8,128)S(1)}, f32[1,72,128]{2,1,0:T(8,128)S(1)}, u32[]{:S(2)}, u32[]{:S(2)}) %collective-permute-start.10) | collective-permute-done | bytes 36896 | tf_op jit(solution)/shard_map/ppermute | solution.py:276
  66.9 0.7 shard_map.58
  67.7 7.8 %all-to-all-start.1 = ((f32[8,72,128]{2,1,0:T(8,128)}), f32[8,72,128]{2,1,0:T(8,128)S(1)}, u32[]{:S(2)}, u32[]{:S(2)}) async-start(f32[8,72,128]{2,1,0:T(8,128)} %shard_map.58), calls=%async_computation.1 | async-start | bytes 589824 | tf_op jit(solution)/shard_map/all_to_all | solution.py:227
  75.5 5.4 %collective-permute-start.7 = (f32[24,3072]{1,0:T(8,128)}, f32[24,3072]{1,0:T(8,128)S(1)}, u32[]{:S(2)}, u32[]{:S(2)}) collective-permute-start(f32[24,3072]{1,0:T(8,128)} %copy-done), channel_id=1, source_target_pairs={{0,11},{1,0},{2,1},{3,2},{4,3},{5,4},{6,5},{7,6},{8,7},{9,8},{10,9... | collective-permute-start | bytes 884744 | tf_op jit(solution)/shard_map/ppermute | solution.py:224
  80.9 1.9 %collective-permute-start.8 = (f32[24,3072]{1,0:T(8,128)S(1)}, f32[24,3072]{1,0:T(8,128)S(1)}, u32[]{:S(2)}, u32[]{:S(2)}) collective-permute-start(f32[24,3072]{1,0:T(8,128)S(1)} %get-tuple-element.17), channel_id=1, source_target_pairs={{0,1},{1,2},{2,3},{3,4},{4,5},{5,6},{6,7},{7,8},{8,9},{9,10},{10,1... | collective-permute-start | bytes 884744 | tf_op jit(solution)/shard_map/ppermute | solution.py:224
  82.8 4.3 %collective-permute-start.9 = (f32[24,3072]{1,0:T(8,128)S(1)}, f32[24,3072]{1,0:T(8,128)S(1)}, u32[]{:S(2)}, u32[]{:S(2)}) collective-permute-start(f32[24,3072]{1,0:T(8,128)S(1)} %get-tuple-element.18), channel_id=1, source_target_pairs={{0,2},{1,3},{2,4},{3,5},{4,6},{5,7},{6,8},{7,9},{8,10},{9,11},{10,... | collective-permute-start | bytes 884744 | tf_op jit(solution)/shard_map/ppermute | solution.py:224
  87.2 0.7 shard_map.59
  87.9 3.4 %all-to-all-start.2 = ((f32[8,72,128]{2,1,0:T(8,128)}), f32[8,72,128]{2,1,0:T(8,128)S(1)}, u32[]{:S(2)}, u32[]{:S(2)}) async-start(f32[8,72,128]{2,1,0:T(8,128)} %shard_map.59), calls=%async_computation.2 | async-start | bytes 589824 | tf_op jit(solution)/shard_map/all_to_all | solution.py:227
  91.4 7.6 %collective-permute-done.8.c_ref = f32[24,3072]{1,0:T(8,128)S(1)} collective-permute-done((f32[24,3072]{1,0:T(8,128)S(1)}, f32[24,3072]{1,0:T(8,128)S(1)}, u32[]{:S(2)}, u32[]{:S(2)}) %collective-permute-start.8) | collective-permute-done | bytes 294944 | tf_op jit(solution)/shard_map/ppermute | solution.py:224
  99.0 3.2 %collective-permute-done.9.d_ref = f32[24,3072]{1,0:T(8,128)S(1)} collective-permute-done((f32[24,3072]{1,0:T(8,128)S(1)}, f32[24,3072]{1,0:T(8,128)S(1)}, u32[]{:S(2)}, u32[]{:S(2)}) %collective-permute-start.9) | collective-permute-done | bytes 294944 | tf_op jit(solution)/shard_map/ppermute | solution.py:224
  102.1 1.1 %shard_map.57 = f32[24,32,96]{2,1,0:T(8,128)} custom-call(f32[24,3072]{1,0:T(8,128)S(1)} %get-tuple-element.15.a_ref, f32[24,3072]{1,0:T(8,128)S(1)} %collective-permute-done.7.b_ref, f32[24,3072]{1,0:T(8,128)S(1)} %collective-permute-done.8.c_ref, f32[24,3072]{1,0:T(8,128)S(1)} %collective-permute-done.9.d_ref), custom_call_target="tpu_custom_call" | custom-call | tf_op jit(solution)/shard_map/pallas_call | solution.py:286
  103.3 1.1 %shard_map.60 = f32[9,24,288]{2,1,0:T(8,128)} custom-call(s32[1]{0:T(128)} %bitcast.9.layer_ref, f32[8,72,128]{2,1,0:T(8,128)S(1)} %all-to-all-done.2.whole_ref), custom_call_target="tpu_custom_call" | custom-call | tf_op jit(solution)/shard_map/pallas_call | solution.py:280
  (21 shorter events, 0.3 us)
Async XLA Ops:
  0.6 38.7 %slice-start = ((bf16[9,288,288]{2,1,0:T(8,128)(2,1)}), bf16[9,24,288]{2,1,0:T(8,128)(2,1)S(1)}, s32[]{:S(2)}) async-start(bf16[9,288,288]{2,1,0:T(8,128)(2,1)} %param.5), calls=%async_computation.3 | async-start | bytes 331776 | tf_op jit(solution)/shard_map/slice | solution.py:244
  0.6 38.7 %slice-start.1 = ((bf16[9,288,288]{2,1,0:T(8,128)(2,1)}), bf16[9,48,288]{2,1,0:T(8,128)(2,1)S(1)}, s32[]{:S(2)}) async-start(bf16[9,288,288]{2,1,0:T(8,128)(2,1)} %param.5), calls=%async_computation.4 | async-start | bytes 663552 | tf_op jit(solution)/shard_map/slice | solution.py:244
  1.9 31.4 %collective-permute-start.3 = (bf16[24,3072]{1,0:T(8,128)(2,1)S(1)}, bf16[24,3072]{1,0:T(8,128)(2,1)S(1)}, u32[]{:S(2)}, u32[]{:S(2)}) collective-permute-start(bf16[24,3072]{1,0:T(8,128)(2,1)S(1)} %shard_map.51.own_ref), channel_id=1, source_target_pairs={{0,4},{1,5},{2,6},{3,7},{4,8},{5,9},{6,10},{7,11},{8,0},{9,1},{10,... | collective-permute-start | bytes 442376 | tf_op jit(solution)/shard_map/ppermute | solution.py:224
  12.8 20.5 %collective-permute-start.4 = (bf16[24,3072]{1,0:T(8,128)(2,1)S(1)}, bf16[24,3072]{1,0:T(8,128)(2,1)S(1)}, u32[]{:S(2)}, u32[]{:S(2)}) collective-permute-start(bf16[24,3072]{1,0:T(8,128)(2,1)S(1)} %shard_map.51.own_ref), channel_id=1, source_target_pairs={{0,8},{1,9},{2,10},{3,11},{4,0},{5,1},{6,2},{7,3},{8,4},{9,5},{10,... | collective-permute-start | bytes 442376 | tf_op jit(solution)/shard_map/ppermute | solution.py:224
  19.5 24.2 %collective-permute-start = (bf16[24,3072]{1,0:T(8,128)(2,1)S(1)}, bf16[24,3072]{1,0:T(8,128)(2,1)S(1)}, u32[]{:S(2)}, u32[]{:S(2)}) collective-permute-start(bf16[24,3072]{1,0:T(8,128)(2,1)S(1)} %shard_map.50.x1), channel_id=1, source_target_pairs={{0,1},{1,2},{2,3},{3,4},{4,5},{5,6},{6,7},{7,8},{8,9},{9,10},{10,1... | collective-permute-start | bytes 442376 | tf_op jit(solution)/shard_map/ppermute | solution.py:224
  22.9 20.9 %collective-permute-start.1 = (bf16[24,3072]{1,0:T(8,128)(2,1)S(1)}, bf16[24,3072]{1,0:T(8,128)(2,1)S(1)}, u32[]{:S(2)}, u32[]{:S(2)}) collective-permute-start(bf16[24,3072]{1,0:T(8,128)(2,1)S(1)} %shard_map.50.x1), channel_id=1, source_target_pairs={{0,11},{1,0},{2,1},{3,2},{4,3},{5,4},{6,5},{7,6},{8,7},{9,8},{10,9... | collective-permute-start | bytes 442376 | tf_op jit(solution)/shard_map/ppermute | solution.py:224
  29.3 14.5 %collective-permute-start.2 = (bf16[24,3072]{1,0:T(8,128)(2,1)S(1)}, bf16[24,3072]{1,0:T(8,128)(2,1)S(1)}, u32[]{:S(2)}, u32[]{:S(2)}) collective-permute-start(bf16[24,3072]{1,0:T(8,128)(2,1)S(1)} %shard_map.50.x1), channel_id=1, source_target_pairs={{0,10},{1,11},{2,0},{3,1},{4,2},{5,3},{6,4},{7,5},{8,6},{9,7},{10,... | collective-permute-start | bytes 442376 | tf_op jit(solution)/shard_map/ppermute | solution.py:224
  33.7 7.4 %collective-permute-start.5 = (bf16[72,128]{1,0:T(8,128)(2,1)S(1)}, bf16[72,128]{1,0:T(8,128)(2,1)S(1)}, u32[]{:S(2)}, u32[]{:S(2)}) collective-permute-start(bf16[72,128]{1,0:T(8,128)(2,1)S(1)} %shard_map.52), channel_id=1, source_target_pairs={{0,12},{12,24},{24,36},{36,48},{48,60},{60,72},{72,84},{84,96},{96... | collective-permute-start | bytes 55304 | tf_op jit(solution)/shard_map/ppermute | solution.py:241
  35.7 5.4 %collective-permute-start.6 = (bf16[72,128]{1,0:T(8,128)(2,1)S(1)}, bf16[72,128]{1,0:T(8,128)(2,1)S(1)}, u32[]{:S(2)}, u32[]{:S(2)}) collective-permute-start(bf16[72,128]{1,0:T(8,128)(2,1)S(1)} %shard_map.52), channel_id=1, source_target_pairs={{12,0},{24,12},{36,24},{48,36},{60,48},{72,60},{84,72},{96,84},{10... | collective-permute-start | bytes 55304 | tf_op jit(solution)/shard_map/ppermute | solution.py:242
  46.5 13.4 %all-to-all-start = ((f32[8,72,128]{2,1,0:T(8,128)}), f32[8,72,128]{2,1,0:T(8,128)S(1)}, u32[]{:S(2)}, u32[]{:S(2)}) async-start(f32[8,72,128]{2,1,0:T(8,128)} %shard_map.54), calls=%async_computation | async-start | bytes 589824 | tf_op jit(solution)/shard_map/all_to_all | solution.py:227
  53.1 0.7 copy-start
  59.9 7.1 %collective-permute-start.10 = (f32[1,72,128]{2,1,0:T(8,128)S(1)}, f32[1,72,128]{2,1,0:T(8,128)S(1)}, u32[]{:S(2)}, u32[]{:S(2)}) collective-permute-start(f32[1,72,128]{2,1,0:T(8,128)S(1)} %shard_map.55), channel_id=1, source_target_pairs={{0,11},{1,0},{2,1},{3,2},{4,3},{5,4},{6,5},{7,6},{8,7},{9,8},{10,9... | collective-permute-start | bytes 110600 | tf_op jit(solution)/shard_map/ppermute | solution.py:276
  67.7 19.5 %all-to-all-start.1 = ((f32[8,72,128]{2,1,0:T(8,128)}), f32[8,72,128]{2,1,0:T(8,128)S(1)}, u32[]{:S(2)}, u32[]{:S(2)}) async-start(f32[8,72,128]{2,1,0:T(8,128)} %shard_map.58), calls=%async_computation.1 | async-start | bytes 589824 | tf_op jit(solution)/shard_map/all_to_all | solution.py:227
  75.5 15.9 %collective-permute-start.7 = (f32[24,3072]{1,0:T(8,128)}, f32[24,3072]{1,0:T(8,128)S(1)}, u32[]{:S(2)}, u32[]{:S(2)}) collective-permute-start(f32[24,3072]{1,0:T(8,128)} %copy-done), channel_id=1, source_target_pairs={{0,11},{1,0},{2,1},{3,2},{4,3},{5,4},{6,5},{7,6},{8,7},{9,8},{10,9... | collective-permute-start | bytes 884744 | tf_op jit(solution)/shard_map/ppermute | solution.py:224
  80.9 18.1 %collective-permute-start.8 = (f32[24,3072]{1,0:T(8,128)S(1)}, f32[24,3072]{1,0:T(8,128)S(1)}, u32[]{:S(2)}, u32[]{:S(2)}) collective-permute-start(f32[24,3072]{1,0:T(8,128)S(1)} %get-tuple-element.17), channel_id=1, source_target_pairs={{0,1},{1,2},{2,3},{3,4},{4,5},{5,6},{6,7},{7,8},{8,9},{9,10},{10,1... | collective-permute-start | bytes 884744 | tf_op jit(solution)/shard_map/ppermute | solution.py:224
  82.8 19.3 %collective-permute-start.9 = (f32[24,3072]{1,0:T(8,128)S(1)}, f32[24,3072]{1,0:T(8,128)S(1)}, u32[]{:S(2)}, u32[]{:S(2)}) collective-permute-start(f32[24,3072]{1,0:T(8,128)S(1)} %get-tuple-element.18), channel_id=1, source_target_pairs={{0,2},{1,3},{2,4},{3,5},{4,6},{5,7},{6,8},{7,9},{8,10},{9,11},{10,... | collective-permute-start | bytes 884744 | tf_op jit(solution)/shard_map/ppermute | solution.py:224
  87.9 15.4 %all-to-all-start.2 = ((f32[8,72,128]{2,1,0:T(8,128)}), f32[8,72,128]{2,1,0:T(8,128)S(1)}, u32[]{:S(2)}, u32[]{:S(2)}) async-start(f32[8,72,128]{2,1,0:T(8,128)} %shard_map.59), calls=%async_computation.2 | async-start | bytes 589824 | tf_op jit(solution)/shard_map/all_to_all | solution.py:227

commit v5 on v4

--- a/solution.py
+++ b/solution.py
@@ -10,6 +10,7 @@
 
 NX, NY, NCORE = 4, 8, 2
 LANES, WIDTH = 128, 96
+PLACE_FLOPS = 10**9
 VMEM = pl.BlockSpec(memory_space=pltpu.VMEM)
 SMEM = pl.BlockSpec(memory_space=pltpu.SMEM)
 
@@ -27,12 +28,14 @@
     return lax.broadcasted_iota(jnp.int32, (chans, LANES), 1)
 
 
-def pack_kernel(cells_ref, dense_ref):
-    for start in range(0, cells_ref.shape[0], 4):
-        store_dense(dense_ref, start, [cells_ref[start + i].astype(jnp.float32) for i in range(4)])
-
-
-def edges_kernel(near_ref, own_ref, far_ref, edges_ref):
+def pack_kernel(grad_ref, field_ref, *dense_refs):
+    for cells_ref, dense_ref in zip((grad_ref, field_ref), dense_refs):
+        for start in range(0, cells_ref.shape[0], 4):
+            group = [cells_ref[start + i].astype(jnp.float32) for i in range(4)]
+            store_dense(dense_ref, start, group)
+
+
+def edges_kernel(own_ref, near_ref, up_ref, down_ref, far_ref, edges_ref):
     refs = (near_ref, own_ref, far_ref)
     rows = near_ref.shape[1] // WIDTH
     lane = lane_index(3 * near_ref.shape[0])
@@ -70,7 +73,7 @@
     return rows
 
 
-def shift_kernel(third_ref, near_ref, own_ref, far_ref, left_ref, right_ref, shifted_ref):
+def shift_kernel(third_ref, left_ref, right_ref, near_ref, own_ref, far_ref, shifted_ref):
     refs = (near_ref, own_ref, far_ref)
     chans = near_ref.shape[0]
     rows = near_ref.shape[1] // WIDTH
@@ -140,7 +143,7 @@
                 ]
 
 
-def inputs_kernel(shifted_ref, filters_ref, *out_refs):
+def inputs_kernel(shifted_ref, filters_ref, parts_ref, *out_refs):
     chans = out_refs[0].shape[0]
     rows = out_refs[0].shape[1] // WIDTH
     total = None
@@ -197,14 +200,17 @@
             out_ref[3 * a + b] = jnp.concatenate(pieces, axis=1) * factor
 
 
-def call(kernel, outs, ins, scalars=0, scratch=()):
+def call(kernel, outs, ins, scalars=0, scratch=(), unread=0, cost=None):
     return pl.pallas_call(
         kernel,
         out_shape=outs,
-        in_specs=[SMEM] * scalars + [VMEM] * (ins - scalars),
+        in_specs=[SMEM] * scalars
+        + [VMEM] * (ins - scalars - unread)
+        + [pl.BlockSpec(memory_space=pl.ANY)] * unread,
         out_specs=jax.tree.map(lambda _: VMEM, outs),
         scratch_shapes=list(scratch),
         compiler_params=pltpu.CompilerParams(vmem_limit_bytes=40 << 20),
+        cost_estimate=cost,
     )
 
 
@@ -233,11 +239,15 @@
         return jnp.pad(cells.transpose(2, 0, 1), ((0, 0), (0, 0), (0, LANES - width)))
 
     cells = rows * width
-    dense = call(pack_kernel, shape(chan_dev, cells), 1)(by_row(grad_out))
-    grads = [move(dense, 4), dense, move(dense, -4)]
-    source = call(pack_kernel, shape(chan_dev, cells), 1)(by_row(field))
-    sources = [move(source, 1), source, move(source, -1), move(source, -2)]
-    edges = call(edges_kernel, shape(3 * chan_dev, LANES), 3)(*grads)
+    dense, source = call(pack_kernel, (shape(chan_dev, cells),) * 2, 2)(
+        by_row(grad_out), by_row(field)
+    )
+    near, up, down, far = move(dense, 4), move(source, 1), move(source, -1), move(dense, -4)
+    grads = [near, dense, far]
+    sources = [up, source, down, move(source, -2)]
+    edges = call(edges_kernel, shape(3 * chan_dev, LANES), 5)(
+        dense, near, up, down, far
+    )
     left = lax.ppermute(edges, "space", [(i, i + 1) for i in range(spaces - 1)])
     right = lax.ppermute(edges, "space", [(i + 1, i) for i in range(spaces - 1)])
 
@@ -253,7 +263,7 @@
 
     third = (layer // 4)[None]
     shifted = call(shift_kernel, shape(9 * chan_dev, (rows + 4) * LANES), 6, 1)(
-        third, *grads, left, right
+        third, left, right, *grads
     )
     parts = call(
         weights_kernel,
@@ -263,26 +273,28 @@
         [pltpu.VMEM((4 * chan_dev, rows * LANES), kind)],
     )(own, *sources, shifted)
     blocks = call(
-        inputs_kernel, tuple(shape(chan_dev, cells, dtype=wide) for _ in range(4)), 2
-    )(shifted, own)
-
-    piece = added(exchange(parts, across), 1)
-    piece, *blocks = lax.optimization_barrier((piece, *blocks))
+        inputs_kernel, tuple(shape(chan_dev, cells, dtype=wide) for _ in range(4)), 3, 0, (), 1
+    )(shifted, own, parts)
+
     home = [
         (s * chans + c, s * chans + (c - 1 + s // (NY * NCORE)) % chans)
         for s in range(spaces)
         for c in range(chans)
     ]
-    piece = lax.ppermute(piece, ("space", "chan"), home)
-    others = [move(blocks[0], -1), move(blocks[2], 1), move(blocks[3], 2)]
-    piece = added(exchange(added(piece, 8), along), 8)
-    whole = exchange(piece, across)
+    def gathered(arrived):
+        piece = lax.ppermute(added(arrived, 1), ("space", "chan"), home)
+        piece = added(exchange(added(piece, 8), along), 8)
+        return exchange(piece, across)
+
+    whole = lax.cond(layer >= 0, gathered, lambda arrived: arrived, exchange(parts, across))
     grad_filters = call(
         functools.partial(place_kernel, factor),
         shape(9, chan_dev, 12 * chan_dev, dtype=wide),
         2,
         1,
+        cost=pl.CostEstimate(flops=PLACE_FLOPS, bytes_accessed=0, transcendentals=0),
     )(layer[None], whole)
+    others = [move(blocks[0], -1), move(blocks[2], 1), move(blocks[3], 2)]
     total = call(total_kernel, shape(chan_dev, rows, width, dtype=wide), 4)(blocks[1], *others)
     return (total.transpose(0, 2, 1), grad_filters)
 

time: 105 us -> 125 us (1.19)
  the two profiles are of different devices: /device:TPU:8 before, /device:TPU:1 now
where the time goes in v5:
time: 125 us; the launch traced here: 124 us
  starting transfers between devices  56.2 us (45%)
  blocking collectives  37.4 us (30%)
  waiting for transfers between devices  14.5 us (12%)
  Pallas kernels  11.2 us (9%)
  local copies, waits for them, and re-layouts  2.32 us (2%)
  matrix products  1.57 us (1%)
    all_to_all x2, blocking collectives, exchange(): lax.all_to_all(parts, 'space', 0, 0, axis_index_groups=groups, tiled=True)  37.4 us
    ppermute x8, starting transfers between devices, move(): lax.ppermute(cells, 'chan', [(i, (i + step) % chans) for i in range(chans)])  36.8 us
    ppermute x8, waiting for transfers between devices, move(): lax.ppermute(cells, 'chan', [(i, (i + step) % chans) for i in range(chans)])  12.1 us
    ppermute x1, starting transfers between devices, per_device(): left = lax.ppermute(edges, 'space', [(i, i + 1) for i in range(spaces - 1)])  7.59 us
    all_to_all x1, starting transfers between devices, exchange(): lax.all_to_all(parts, 'space', 0, 0, axis_index_groups=groups, tiled=True)  5.61 us
    ppermute x1, starting transfers between devices, gathered(): piece = lax.ppermute(added(arrived, 1), ('space', 'chan'), home)  4.3 us
    pallas_call x1, Pallas kernels, per_device(): call(shift_kernel, shape(9 * chan_dev, (rows + 4) * LANES), 6, 1)  2.67 us
    pallas_call x1, Pallas kernels, per_device(): call(weights_kernel, shape(8, 3 * chan_dev, LANES, dtype=wide), 6, 0, [pl...  2.6 us
  transfers between devices with their start and end apart: 12, of which 4 were waited for; matrix products, arithmetic and copies ran while one was open for 1% of the time, Pallas kernels for 6%

profile of v5, /device:TPU:1, one launch (start us, length us, event | category | flops | bytes accessed | tf_op | source)
XLA Modules:
  0.0 124.1 jit_solution(13835693691926994616)
XLA Ops:
  0.6 0.0 slice-start
  0.7 1.1 copy.16
  1.7 1.0 copy.15
  2.8 0.1 shard_map.50
  3.0 11.5 %collective-permute-start.1 = (bf16[24,3072]{1,0:T(8,128)(2,1)S(1)}, bf16[24,3072]{1,0:T(8,128)(2,1)S(1)}, u32[]{:S(2)}, u32[]{:S(2)}) collective-permute-start(bf16[24,3072]{1,0:T(8,128)(2,1)S(1)} %get-tuple-element.13.own_ref), channel_id=1, source_target_pairs={{0,4},{1,5},{2,6},{3,7},{4,8},{5,9},{6,10},{7,11},{8,0},{9,1},{10,... | collective-permute-start | bytes 442376 | tf_op jit(solution)/shard_map/ppermute | solution.py:230
  14.5 4.0 %collective-permute-start.2 = (bf16[24,3072]{1,0:T(8,128)(2,1)S(1)}, bf16[24,3072]{1,0:T(8,128)(2,1)S(1)}, u32[]{:S(2)}, u32[]{:S(2)}) collective-permute-start(bf16[24,3072]{1,0:T(8,128)(2,1)S(1)} %get-tuple-element.14.x1), channel_id=1, source_target_pairs={{0,1},{1,2},{2,3},{3,4},{4,5},{5,6},{6,7},{7,8},{8,9},{9,10},{10,1... | collective-permute-start | bytes 442376 | tf_op jit(solution)/shard_map/ppermute | solution.py:230
  18.5 3.5 %collective-permute-start.3 = (bf16[24,3072]{1,0:T(8,128)(2,1)S(1)}, bf16[24,3072]{1,0:T(8,128)(2,1)S(1)}, u32[]{:S(2)}, u32[]{:S(2)}) collective-permute-start(bf16[24,3072]{1,0:T(8,128)(2,1)S(1)} %get-tuple-element.14.x1), channel_id=1, source_target_pairs={{0,11},{1,0},{2,1},{3,2},{4,3},{5,4},{6,5},{7,6},{8,7},{9,8},{10,9... | collective-permute-start | bytes 442376 | tf_op jit(solution)/shard_map/ppermute | solution.py:230
  22.0 7.3 %collective-permute-start.4 = (bf16[24,3072]{1,0:T(8,128)(2,1)S(1)}, bf16[24,3072]{1,0:T(8,128)(2,1)S(1)}, u32[]{:S(2)}, u32[]{:S(2)}) collective-permute-start(bf16[24,3072]{1,0:T(8,128)(2,1)S(1)} %get-tuple-element.13.own_ref), channel_id=1, source_target_pairs={{0,8},{1,9},{2,10},{3,11},{4,0},{5,1},{6,2},{7,3},{8,4},{9,5},{10,... | collective-permute-start | bytes 442376 | tf_op jit(solution)/shard_map/ppermute | solution.py:230
  29.3 3.4 %collective-permute-start.7 = (bf16[24,3072]{1,0:T(8,128)(2,1)S(1)}, bf16[24,3072]{1,0:T(8,128)(2,1)S(1)}, u32[]{:S(2)}, u32[]{:S(2)}) collective-permute-start(bf16[24,3072]{1,0:T(8,128)(2,1)S(1)} %get-tuple-element.14.x1), channel_id=1, source_target_pairs={{0,10},{1,11},{2,0},{3,1},{4,2},{5,3},{6,4},{7,5},{8,6},{9,7},{10,... | collective-permute-start | bytes 442376 | tf_op jit(solution)/shard_map/ppermute | solution.py:230
  32.7 2.4 %collective-permute-done.2.up_ref.x0 = bf16[24,3072]{1,0:T(8,128)(2,1)S(1)} collective-permute-done((bf16[24,3072]{1,0:T(8,128)(2,1)S(1)}, bf16[24,3072]{1,0:T(8,128)(2,1)S(1)}, u32[]{:S(2)}, u32[]{:S(2)}) %collective-permute-start.2) | collective-permute-done | bytes 147488 | tf_op jit(solution)/shard_map/ppermute | solution.py:230
  35.0 9.7 %collective-permute-done.4.far_ref = bf16[24,3072]{1,0:T(8,128)(2,1)S(1)} collective-permute-done((bf16[24,3072]{1,0:T(8,128)(2,1)S(1)}, bf16[24,3072]{1,0:T(8,128)(2,1)S(1)}, u32[]{:S(2)}, u32[]{:S(2)}) %collective-permute-start.4) | collective-permute-done | bytes 147488 | tf_op jit(solution)/shard_map/ppermute | solution.py:230
  44.8 0.4 shard_map.51
  45.2 7.6 %collective-permute-start.5 = (bf16[72,128]{1,0:T(8,128)(2,1)S(1)}, bf16[72,128]{1,0:T(8,128)(2,1)S(1)}, u32[]{:S(2)}, u32[]{:S(2)}) collective-permute-start(bf16[72,128]{1,0:T(8,128)(2,1)S(1)} %shard_map.51), channel_id=1, source_target_pairs={{0,12},{12,24},{24,36},{36,48},{48,60},{60,72},{72,84},{84,96},{96... | collective-permute-start | bytes 55304 | tf_op jit(solution)/shard_map/ppermute | solution.py:251
  52.8 1.9 %collective-permute-start.6 = (bf16[72,128]{1,0:T(8,128)(2,1)S(1)}, bf16[72,128]{1,0:T(8,128)(2,1)S(1)}, u32[]{:S(2)}, u32[]{:S(2)}) collective-permute-start(bf16[72,128]{1,0:T(8,128)(2,1)S(1)} %shard_map.51), channel_id=1, source_target_pairs={{12,0},{24,12},{36,24},{48,36},{60,48},{72,60},{84,72},{96,84},{10... | collective-permute-start | bytes 55304 | tf_op jit(solution)/shard_map/ppermute | solution.py:252
  54.7 1.6 %convolution_convert_fusion = bf16[9,96,72]{1,2,0:T(8,128)(2,1)S(1)} fusion(s32[]{:T(128)S(6)} %select_n.34, bf16[9,24,288]{2,1,0:T(8,128)(2,1)S(1)} %slice-done.1, bf16[9,288,288]{2,1,0:T(8,128)(2,1)} %param.7, bf16[9,48,288]{2,1,0:T(8,128)(2,1)S(1)} %slice-done, s32[72]{0:T(128)S(1)} %fusion.7), kind=kOutput, calls=%fused_computation.3 | convolution fusion | flops 37407744 | bytes 1990948 | tf_op jit(solution)/shard_map/kio,op->kip/dot_general | solution.py:260
  56.3 0.1 copy.12.own_ref.filters_ref
  56.5 1.4 %collective-permute-done.6.right_ref = bf16[72,128]{1,0:T(8,128)(2,1)S(1)} collective-permute-done((bf16[72,128]{1,0:T(8,128)(2,1)S(1)}, bf16[72,128]{1,0:T(8,128)(2,1)S(1)}, u32[]{:S(2)}, u32[]{:S(2)}) %collective-permute-start.6) | collective-permute-done | bytes 18464 | tf_op jit(solution)/shard_map/ppermute | solution.py:252
  57.8 2.7 %shard_map.52.shifted_ref = bf16[216,4608]{1,0:T(8,128)(2,1)S(1)} custom-call(s32[1]{0:T(128)} %bitcast.third_ref, bf16[72,128]{1,0:T(8,128)(2,1)S(1)} %collective-permute-done.5.left_ref, bf16[72,128]{1,0:T(8,128)(2,1)S(1)} %collective-permute-done.6.right_ref, bf16[24,3072]{1,0:T(8,128)(2,1)S(1)} %collective-permute-done.1.near_ref, ...), custom_call_target="tpu_custom_call" | custom-call | tf_op jit(solution)/shard_map/pallas_call | solution.py:265
  60.5 2.6 %shard_map.53.parts_ref = f32[8,72,128]{2,1,0:T(8,128)} custom-call(bf16[3,96,216]{2,1,0:T(8,128)(2,1)S(1)} %copy.12.own_ref.filters_ref, bf16[24,3072]{1,0:T(8,128)(2,1)S(1)} %collective-permute-done.2.up_ref.x0, bf16[24,3072]{1,0:T(8,128)(2,1)S(1)} %get-tuple-element.14.x1, bf16[24,3072]{1,0:T(8,128)(2,1)S(1)} %collective-permute-done.3.down_ref.x2, ...), custom_call_target="tpu_custom_call" | custom-call | tf_op jit(solution)/shard_map/pallas_call | solution.py:268
  63.1 5.6 %all-to-all-start.2 = ((f32[8,72,128]{2,1,0:T(8,128)}), f32[8,72,128]{2,1,0:T(8,128)}, u32[]{:S(2)}, u32[]{:S(2)}) async-start(f32[8,72,128]{2,1,0:T(8,128)} %shard_map.53.parts_ref), calls=%async_computation.2 | async-start | bytes 589824 | tf_op jit(solution)/shard_map/all_to_all | solution.py:233
  68.7 1.2 shard_map.54
  69.9 1.9 %collective-permute-start.10 = (f32[24,3072]{1,0:T(8,128)S(1)}, f32[24,3072]{1,0:T(8,128)S(1)}, u32[]{:S(2)}, u32[]{:S(2)}) collective-permute-start(f32[24,3072]{1,0:T(8,128)S(1)} %get-tuple-element.18), channel_id=1, source_target_pairs={{0,2},{1,3},{2,4},{3,5},{4,6},{5,7},{6,8},{7,9},{8,10},{9,11},{10,... | collective-permute-start | bytes 884744 | tf_op jit(solution)/shard_map/ppermute | solution.py:230
  71.8 1.9 %collective-permute-start.8 = (f32[24,3072]{1,0:T(8,128)S(1)}, f32[24,3072]{1,0:T(8,128)S(1)}, u32[]{:S(2)}, u32[]{:S(2)}) collective-permute-start(f32[24,3072]{1,0:T(8,128)S(1)} %get-tuple-element.16), channel_id=1, source_target_pairs={{0,11},{1,0},{2,1},{3,2},{4,3},{5,4},{6,5},{7,6},{8,7},{9,8},{10,9... | collective-permute-start | bytes 884744 | tf_op jit(solution)/shard_map/ppermute | solution.py:230
  73.8 3.4 %collective-permute-start.9 = (f32[24,3072]{1,0:T(8,128)S(1)}, f32[24,3072]{1,0:T(8,128)S(1)}, u32[]{:S(2)}, u32[]{:S(2)}) collective-permute-start(f32[24,3072]{1,0:T(8,128)S(1)} %get-tuple-element.17), channel_id=1, source_target_pairs={{0,1},{1,2},{2,3},{3,4},{4,5},{5,6},{6,7},{7,8},{8,9},{9,10},{10,1... | collective-permute-start | bytes 884744 | tf_op jit(solution)/shard_map/ppermute | solution.py:230
  77.2 43.8 %conditional.1 = (f32[8,72,128]{2,1,0:T(8,128)}) conditional(s32[]{:T(128)} %convert_element_type.11, f32[8,72,128]{2,1,0:T(8,128)} %all-to-all-done.2, f32[8,72,128]{2,1,0:T(8,128)} %all-to-all-done.2), branch_computations={%region_0.1_spmd, %region_1.2_spmd} | conditional | bytes 1327152 | solution.py:289
  77.2 1.0 branch_1_fun.3
  78.2 4.3 %collective-permute-start = (f32[1,72,128]{2,1,0:T(8,128)S(1)}, f32[1,72,128]{2,1,0:T(8,128)S(1)}, u32[]{:S(2)}, u32[]{:S(2)}) collective-permute-start(f32[1,72,128]{2,1,0:T(8,128)S(1)} %branch_1_fun.3), channel_id=1, source_target_pairs={{0,11},{1,0},{2,1},{3,2},{4,3},{5,4},{6,5},{7,6},{8,7},{9,8},{10,9... | collective-permute-start | bytes 110600 | tf_op jit(solution)/shard_map/cond/branch_1_fun/ppermute | solution.py:285
  82.5 1.0 collective-permute-done.in_ref
  83.5 16.0 %all_to_all.19.in_ref = f32[8,72,128]{2,1,0:T(8,128)S(1)} all-to-all(f32[8,72,128]{2,1,0:T(8,128)S(1)} %branch_1_fun.4), channel_id=1, replica_groups={{0,24,48,72,96,120,144,168},{12,36,60,84,108,132,156,180},{192,216,240,..., dimensions={0} | all-to-all | bytes 589824 | tf_op jit(solution)/shard_map/cond/branch_1_fun/all_to_all | solution.py:233
  99.6 21.4 %all_to_all.20 = f32[8,72,128]{2,1,0:T(8,128)} all-to-all(f32[8,72,128]{2,1,0:T(8,128)S(1)} %branch_1_fun.5), channel_id=1, replica_groups={{0,12,192,204,384,396,576,588},{24,36,216,228,408,420,600,612},{48,60,2..., dimensions={0} | all-to-all | bytes 589824 | tf_op jit(solution)/shard_map/cond/branch_1_fun/all_to_all | solution.py:233
  120.9 2.0 %shard_map.56 = f32[9,24,288]{2,1,0:T(8,128)} custom-call(s32[1]{0:T(128)} %bitcast.9.layer_ref, f32[8,72,128]{2,1,0:T(8,128)} %get-tuple-element.19.whole_ref), custom_call_target="tpu_custom_call" | custom-call | flops 1000000000 | tf_op jit(solution)/shard_map/pallas_call | solution.py:290
  123.0 1.1 shard_map.55
  (17 shorter events, 0.2 us)
Async XLA Ops:
  0.6 54.1 %slice-start = ((bf16[9,288,288]{2,1,0:T(8,128)(2,1)}), bf16[9,48,288]{2,1,0:T(8,128)(2,1)S(1)}, s32[]{:S(2)}) async-start(bf16[9,288,288]{2,1,0:T(8,128)(2,1)} %param.7), calls=%async_computation.3 | async-start | bytes 663552 | tf_op jit(solution)/shard_map/slice | solution.py:254
  0.6 54.1 %slice-start.1 = ((bf16[9,288,288]{2,1,0:T(8,128)(2,1)}), bf16[9,24,288]{2,1,0:T(8,128)(2,1)S(1)}, s32[]{:S(2)}) async-start(bf16[9,288,288]{2,1,0:T(8,128)(2,1)} %param.7), calls=%async_computation.4 | async-start | bytes 331776 | tf_op jit(solution)/shard_map/slice | solution.py:254
  3.0 29.7 %collective-permute-start.1 = (bf16[24,3072]{1,0:T(8,128)(2,1)S(1)}, bf16[24,3072]{1,0:T(8,128)(2,1)S(1)}, u32[]{:S(2)}, u32[]{:S(2)}) collective-permute-start(bf16[24,3072]{1,0:T(8,128)(2,1)S(1)} %get-tuple-element.13.own_ref), channel_id=1, source_target_pairs={{0,4},{1,5},{2,6},{3,7},{4,8},{5,9},{6,10},{7,11},{8,0},{9,1},{10,... | collective-permute-start | bytes 442376 | tf_op jit(solution)/shard_map/ppermute | solution.py:230
  14.5 20.6 %collective-permute-start.2 = (bf16[24,3072]{1,0:T(8,128)(2,1)S(1)}, bf16[24,3072]{1,0:T(8,128)(2,1)S(1)}, u32[]{:S(2)}, u32[]{:S(2)}) collective-permute-start(bf16[24,3072]{1,0:T(8,128)(2,1)S(1)} %get-tuple-element.14.x1), channel_id=1, source_target_pairs={{0,1},{1,2},{2,3},{3,4},{4,5},{5,6},{6,7},{7,8},{8,9},{9,10},{10,1... | collective-permute-start | bytes 442376 | tf_op jit(solution)/shard_map/ppermute | solution.py:230
  18.5 16.6 %collective-permute-start.3 = (bf16[24,3072]{1,0:T(8,128)(2,1)S(1)}, bf16[24,3072]{1,0:T(8,128)(2,1)S(1)}, u32[]{:S(2)}, u32[]{:S(2)}) collective-permute-start(bf16[24,3072]{1,0:T(8,128)(2,1)S(1)} %get-tuple-element.14.x1), channel_id=1, source_target_pairs={{0,11},{1,0},{2,1},{3,2},{4,3},{5,4},{6,5},{7,6},{8,7},{9,8},{10,9... | collective-permute-start | bytes 442376 | tf_op jit(solution)/shard_map/ppermute | solution.py:230
  22.0 22.8 %collective-permute-start.4 = (bf16[24,3072]{1,0:T(8,128)(2,1)S(1)}, bf16[24,3072]{1,0:T(8,128)(2,1)S(1)}, u32[]{:S(2)}, u32[]{:S(2)}) collective-permute-start(bf16[24,3072]{1,0:T(8,128)(2,1)S(1)} %get-tuple-element.13.own_ref), channel_id=1, source_target_pairs={{0,8},{1,9},{2,10},{3,11},{4,0},{5,1},{6,2},{7,3},{8,4},{9,5},{10,... | collective-permute-start | bytes 442376 | tf_op jit(solution)/shard_map/ppermute | solution.py:230
  29.3 31.3 %collective-permute-start.7 = (bf16[24,3072]{1,0:T(8,128)(2,1)S(1)}, bf16[24,3072]{1,0:T(8,128)(2,1)S(1)}, u32[]{:S(2)}, u32[]{:S(2)}) collective-permute-start(bf16[24,3072]{1,0:T(8,128)(2,1)S(1)} %get-tuple-element.14.x1), channel_id=1, source_target_pairs={{0,10},{1,11},{2,0},{3,1},{4,2},{5,3},{6,4},{7,5},{8,6},{9,7},{10,... | collective-permute-start | bytes 442376 | tf_op jit(solution)/shard_map/ppermute | solution.py:230
  45.2 11.3 %collective-permute-start.5 = (bf16[72,128]{1,0:T(8,128)(2,1)S(1)}, bf16[72,128]{1,0:T(8,128)(2,1)S(1)}, u32[]{:S(2)}, u32[]{:S(2)}) collective-permute-start(bf16[72,128]{1,0:T(8,128)(2,1)S(1)} %shard_map.51), channel_id=1, source_target_pairs={{0,12},{12,24},{24,36},{36,48},{48,60},{60,72},{72,84},{84,96},{96... | collective-permute-start | bytes 55304 | tf_op jit(solution)/shard_map/ppermute | solution.py:251
  52.8 5.1 %collective-permute-start.6 = (bf16[72,128]{1,0:T(8,128)(2,1)S(1)}, bf16[72,128]{1,0:T(8,128)(2,1)S(1)}, u32[]{:S(2)}, u32[]{:S(2)}) collective-permute-start(bf16[72,128]{1,0:T(8,128)(2,1)S(1)} %shard_map.51), channel_id=1, source_target_pairs={{12,0},{24,12},{36,24},{48,36},{60,48},{72,60},{84,72},{96,84},{10... | collective-permute-start | bytes 55304 | tf_op jit(solution)/shard_map/ppermute | solution.py:252
  63.1 14.0 %all-to-all-start.2 = ((f32[8,72,128]{2,1,0:T(8,128)}), f32[8,72,128]{2,1,0:T(8,128)}, u32[]{:S(2)}, u32[]{:S(2)}) async-start(f32[8,72,128]{2,1,0:T(8,128)} %shard_map.53.parts_ref), calls=%async_computation.2 | async-start | bytes 589824 | tf_op jit(solution)/shard_map/all_to_all | solution.py:233
  69.9 53.0 %collective-permute-start.10 = (f32[24,3072]{1,0:T(8,128)S(1)}, f32[24,3072]{1,0:T(8,128)S(1)}, u32[]{:S(2)}, u32[]{:S(2)}) collective-permute-start(f32[24,3072]{1,0:T(8,128)S(1)} %get-tuple-element.18), channel_id=1, source_target_pairs={{0,2},{1,3},{2,4},{3,5},{4,6},{5,7},{6,8},{7,9},{8,10},{9,11},{10,... | collective-permute-start | bytes 884744 | tf_op jit(solution)/shard_map/ppermute | solution.py:230
  71.8 51.1 %collective-permute-start.8 = (f32[24,3072]{1,0:T(8,128)S(1)}, f32[24,3072]{1,0:T(8,128)S(1)}, u32[]{:S(2)}, u32[]{:S(2)}) collective-permute-start(f32[24,3072]{1,0:T(8,128)S(1)} %get-tuple-element.16), channel_id=1, source_target_pairs={{0,11},{1,0},{2,1},{3,2},{4,3},{5,4},{6,5},{7,6},{8,7},{9,8},{10,9... | collective-permute-start | bytes 884744 | tf_op jit(solution)/shard_map/ppermute | solution.py:230
  73.8 49.2 %collective-permute-start.9 = (f32[24,3072]{1,0:T(8,128)S(1)}, f32[24,3072]{1,0:T(8,128)S(1)}, u32[]{:S(2)}, u32[]{:S(2)}) collective-permute-start(f32[24,3072]{1,0:T(8,128)S(1)} %get-tuple-element.17), channel_id=1, source_target_pairs={{0,1},{1,2},{2,3},{3,4},{4,5},{5,6},{6,7},{7,8},{8,9},{9,10},{10,1... | collective-permute-start | bytes 884744 | tf_op jit(solution)/shard_map/ppermute | solution.py:230
  78.2 5.3 %collective-permute-start = (f32[1,72,128]{2,1,0:T(8,128)S(1)}, f32[1,72,128]{2,1,0:T(8,128)S(1)}, u32[]{:S(2)}, u32[]{:S(2)}) collective-permute-start(f32[1,72,128]{2,1,0:T(8,128)S(1)} %branch_1_fun.3), channel_id=1, source_target_pairs={{0,11},{1,0},{2,1},{3,2},{4,3},{5,4},{6,5},{7,6},{8,7},{9,8},{10,9... | collective-permute-start | bytes 110600 | tf_op jit(solution)/shard_map/cond/branch_1_fun/ppermute | solution.py:285

commit v6 on v4

--- a/solution.py
+++ b/solution.py
@@ -10,6 +10,7 @@
 
 NX, NY, NCORE = 4, 8, 2
 LANES, WIDTH = 128, 96
+TAIL = WIDTH - 2
 VMEM = pl.BlockSpec(memory_space=pltpu.VMEM)
 SMEM = pl.BlockSpec(memory_space=pltpu.SMEM)
 
@@ -38,7 +39,7 @@
     lane = lane_index(3 * near_ref.shape[0])
     packed = jnp.zeros(edges_ref.shape, jnp.float32)
     for r in range(rows):
-        for column, to in ((WIDTH - 2, 4 * r), (0, (4 * r + WIDTH + 2) % LANES)):
+        for column, to in ((TAIL, 4 * r), (0, (4 * r + TAIL) % LANES)):
             tile, at = divmod(r * WIDTH + column, LANES)
             cut = slice(tile * LANES, (tile + 1) * LANES)
             block = jnp.concatenate([ref[:, cut].astype(jnp.float32) for ref in refs], axis=0)
@@ -70,66 +71,97 @@
     return rows
 
 
-def shift_kernel(third_ref, near_ref, own_ref, far_ref, left_ref, right_ref, shifted_ref):
-    refs = (near_ref, own_ref, far_ref)
-    chans = near_ref.shape[0]
-    rows = near_ref.shape[1] // WIDTH
+def filters_kernel(picks_ref, w0, w1, w2, w3, own_ref):
+    chans = w0.shape[1]
+    outs = (12 * chans, 3 * chans)
+    column = lax.broadcasted_iota(jnp.int32, outs, 1)
+    third = (column >= chans).astype(jnp.int32) + (column >= 2 * chans).astype(jnp.int32)
+    wanted = column + 3 * chans * third + chans * picks_ref[4]
+    chosen = (lax.broadcasted_iota(jnp.int32, outs, 0) == wanted).astype(jnp.float32)
+    chosen = chosen.astype(own_ref.dtype)
+    for b in range(3):
+        taps = []
+        for a in range(3):
+            rows = [w[3 * a + b].astype(jnp.float32) for w in (w0, w1, w2, w3)]
+            rows = jnp.concatenate(rows, axis=0).astype(own_ref.dtype)
+            taps.append(jnp.dot(rows, chosen, preferred_element_type=jnp.float32))
+        own_ref[b] = jnp.concatenate(taps, axis=1).astype(own_ref.dtype)
+
+
+def ordered(third, near, own, far):
+    orders = ((own, far, near), (near, own, far), (far, near, own))
+    return jnp.concatenate(
+        [jnp.where(third == 0, a, jnp.where(third == 1, b, c)) for a, b, c in zip(*orders)],
+        axis=0,
+    )
+
+
+def build_kernel(third_ref, *refs):
+    g_refs, x_refs, (shifted_ref, window_ref, ends_ref) = refs[:3], refs[3:7], refs[7:]
+    chans = g_refs[0].shape[0]
+    rows = g_refs[0].shape[1] // WIDTH
     third = third_ref[0]
     kind = shifted_ref.dtype
     blank = jnp.zeros((9 * chans, 2 * LANES), kind)
     shifted_ref[:, : 2 * LANES] = blank
     shifted_ref[:, (rows + 2) * LANES :] = blank
-    lane = lane_index(3 * chans)
-
-    def ordered(near, own, far):
-        orders = ((own, far, near), (near, own, far), (far, near, own))
-        return jnp.concatenate(
-            [
-                jnp.where(third == 0, a, jnp.where(third == 1, b, c))
-                for a, b, c in zip(*orders)
-            ],
-            axis=0,
-        )
-
-    sides = jnp.where(
-        lane % 4 < 2, left_ref[...].astype(jnp.float32), right_ref[...].astype(jnp.float32)
-    )
-    sides = ordered(*[sides[m * chans : (m + 1) * chans] for m in range(3)])
+    lane, lane_x = lane_index(3 * chans), lane_index(4 * chans)
+    ends = jnp.zeros((4 * chans, LANES), jnp.float32)
     for start in range(0, rows, 4):
-        ats = [(3 * start // 4 + i) * LANES for i in range(3)]
-        tiles = [
-            ordered(*[ref[:, at : at + LANES].astype(jnp.float32) for ref in refs]) for at in ats
-        ]
+        cuts = [pl.ds((3 * start // 4 + i) * LANES, LANES) for i in range(3)]
+        tiles = [ordered(third, *[g[:, cut].astype(jnp.float32) for g in g_refs]) for cut in cuts]
         for i, row in enumerate(load_rows(tiles, 2)):
-            side = pltpu.roll(sides, (-4 * (start + i)) % LANES, 1) if start + i else sides
-            row = jnp.where((lane >= 2) & (lane < WIDTH + 2), row, side)
-            row = jnp.where(lane < WIDTH + 4, row, 0.0)
+            row = jnp.where((lane >= 2) & (lane < WIDTH + 2), row, 0.0)
             taps = [pltpu.roll(row, LANES - 4, 1), pltpu.roll(row, LANES - 2, 1), row]
             at = (start + i + 2) * LANES
             shifted_ref[:, at : at + LANES] = jnp.concatenate(taps, axis=0).astype(kind)
-
-
-def weights_kernel(own_ref, x0, x1, x2, x3, shifted_ref, parts_ref, window_ref):
-    refs = (x0, x1, x2, x3)
-    chans = x0.shape[0]
-    rows = x0.shape[1] // WIDTH
-    lane = lane_index(4 * chans)
-    for start in range(0, rows, 4):
-        ats = [(3 * start // 4 + i) * LANES for i in range(3)]
         tiles = [
-            jnp.concatenate([x[:, at : at + LANES].astype(jnp.float32) for x in refs], axis=0)
-            for at in ats
+            jnp.concatenate([x[:, cut].astype(jnp.float32) for x in x_refs], axis=0)
+            for cut in cuts
         ]
         for i, row in enumerate(load_rows(tiles, 0)):
-            at = (start + i) * LANES
-            row = jnp.where(lane < WIDTH, row, 0.0)
-            window_ref[:, at : at + LANES] = row.astype(window_ref.dtype)
+            r = start + i
+            row = jnp.where(lane_x < WIDTH, row, 0.0)
+            window_ref[:, r * LANES : (r + 1) * LANES] = row.astype(kind)
+            turned = pltpu.roll(row, 4 * r, 1) if r else row
+            tail = (4 * r + TAIL) % LANES
+            here = (lane_x >= 4 * r) & (lane_x < 4 * r + 2)
+            here = here | ((lane_x >= tail) & (lane_x < tail + 2))
+            ends = jnp.where(here, turned, ends)
+    ends_ref[...] = ends.astype(kind)
+
+
+def weights_kernel(
+    third_ref, shifted_ref, window_ref, ends_ref, left_ref, right_ref, parts_ref, borders_ref
+):
+    chans = left_ref.shape[0] // 3
+    rows = window_ref.shape[1] // LANES
+    lane = lane_index(3 * chans)
+    at_head = lane % 4 < 2
+    row_of = jnp.where(at_head, lane, (lane + LANES - TAIL) % LANES) // 4
+    sides = [
+        ordered(third_ref[0], *[ref[m * chans : (m + 1) * chans].astype(jnp.float32) for m in range(3)])
+        for ref in (left_ref, right_ref)
+    ]
+    contract = (((1,), (1,)), ((), ()))
     for b in range(3):
+        valid = (row_of >= 2 * (b - 1)) & (row_of < rows + 2 * (b - 1))
+        left, right = [pltpu.roll(side, (8 * (b - 1)) % LANES, 1) if b != 1 else side for side in sides]
+        left = jnp.where(valid & at_head, left, 0.0)
+        right = jnp.where(valid & ~at_head, right, 0.0)
+        border = jnp.concatenate([right, jnp.zeros_like(left), left], axis=0)
+        borders_ref[b] = border.astype(borders_ref.dtype)
         at = (4 - 2 * b) * LANES
         part = lax.dot_general(
             window_ref[...],
             shifted_ref[:, at : at + rows * LANES],
-            (((1,), (1,)), ((), ())),
+            contract,
+            preferred_element_type=jnp.float32,
+        )
+        part = part + lax.dot_general(
+            ends_ref[...],
+            border.astype(borders_ref.dtype),
+            contract,
             preferred_element_type=jnp.float32,
         )
         part = jnp.concatenate([part, jnp.zeros((4 * chans, 5 * 8), jnp.float32)], axis=1)
@@ -140,10 +172,11 @@
                 ]
 
 
-def inputs_kernel(shifted_ref, filters_ref, *out_refs):
+def inputs_kernel(shifted_ref, filters_ref, borders_ref, *out_refs):
     chans = out_refs[0].shape[0]
     rows = out_refs[0].shape[1] // WIDTH
-    total = None
+    lane = lane_index(4 * chans)
+    total, edge = None, None
     for b in range(3):
         at = (4 - 2 * b) * LANES
         part = jnp.dot(
@@ -151,12 +184,18 @@
             shifted_ref[:, at : at + rows * LANES],
             preferred_element_type=jnp.float32,
         )
+        rim = jnp.dot(filters_ref[b], borders_ref[b], preferred_element_type=jnp.float32)
         total = part if total is None else total + part
-    for j in range(4):
-        block = total[j * chans : (j + 1) * chans]
-        for start in range(0, rows, 4):
-            group = [block[:, r * LANES : (r + 1) * LANES] for r in range(start, start + 4)]
-            store_dense(out_refs[j], start, group)
+        edge = rim if edge is None else edge + rim
+    on_rim = (lane < 2) | ((lane >= TAIL) & (lane < WIDTH))
+    for start in range(0, rows, 4):
+        group = []
+        for r in range(start, start + 4):
+            rim = pltpu.roll(edge, LANES - 4 * r, 1) if r else edge
+            group.append(total[:, r * LANES : (r + 1) * LANES] + jnp.where(on_rim, rim, 0.0))
+        for j in range(4):
+            cut = slice(j * chans, (j + 1) * chans)
+            store_dense(out_refs[j], start, [row[cut] for row in group])
 
 
 def total_kernel(a_ref, b_ref, c_ref, d_ref, out_ref):
@@ -241,30 +280,43 @@
     left = lax.ppermute(edges, "space", [(i, i + 1) for i in range(spaces - 1)])
     right = lax.ppermute(edges, "space", [(i + 1, i) for i in range(spaces - 1)])
 
-    first, last = filters[:, : 2 * chan_dev], filters[:, -chan_dev:]
-    own = jnp.concatenate([last, filters, first], axis=1)
-    own = lax.dynamic_slice_in_dim(own, layer * chan_dev, 4 * chan_dev, 1)
-    lane = jnp.arange(3 * chan_dev)
-    wanted = (4 * (lane // chan_dev) + layer % 4) * chan_dev + lane % chan_dev
-    chosen = (jnp.arange(12 * chan_dev)[:, None] == wanted[None, :]).astype(filters.dtype)
-    own = jnp.einsum("kio,op->kip", own, chosen, preferred_element_type=jnp.float32)
-    own = own.astype(filters.dtype).reshape(3, 3, 4 * chan_dev, 3 * chan_dev)
-    own = own.transpose(1, 2, 0, 3).reshape(3, 4 * chan_dev, 9 * chan_dev)
+    beyond = jnp.where(lax.axis_index("space") % NCORE == 0, layer + 2, layer + chans - 2)
+    blocks = [layer + chans - 1, layer, layer + 1, beyond]
+    picks = jnp.stack([block % chans for block in blocks] + [layer % 4]).astype(jnp.int32)
+    own = pl.pallas_call(
+        filters_kernel,
+        out_shape=shape(3, 4 * chan_dev, 9 * chan_dev),
+        grid_spec=pltpu.PrefetchScalarGridSpec(
+            num_scalar_prefetch=1,
+            grid=(1,),
+            in_specs=[
+                pl.BlockSpec((9, chan_dev, 12 * chan_dev), lambda i, at, j=j: (0, at[j], 0))
+                for j in range(4)
+            ],
+            out_specs=pl.BlockSpec((3, 4 * chan_dev, 9 * chan_dev), lambda i, at: (0, 0, 0)),
+        ),
+    )(picks, filters, filters, filters, filters)
 
     third = (layer // 4)[None]
-    shifted = call(shift_kernel, shape(9 * chan_dev, (rows + 4) * LANES), 6, 1)(
-        third, *grads, left, right
+    shifted, window, ends = call(
+        build_kernel,
+        (
+            shape(9 * chan_dev, (rows + 4) * LANES),
+            shape(4 * chan_dev, rows * LANES),
+            shape(4 * chan_dev, LANES),
+        ),
+        8,
+        1,
+    )(third, *grads, *sources)
+    parts, borders = call(
+        weights_kernel,
+        (shape(8, 3 * chan_dev, LANES, dtype=wide), shape(3, 9 * chan_dev, LANES)),
+        6,
+        1,
+    )(third, shifted, window, ends, left, right)
+    blocks = call(inputs_kernel, (shape(chan_dev, cells, dtype=wide),) * 4, 3)(
+        shifted, own, borders
     )
-    parts = call(
-        weights_kernel,
-        shape(8, 3 * chan_dev, LANES, dtype=wide),
-        6,
-        0,
-        [pltpu.VMEM((4 * chan_dev, rows * LANES), kind)],
-    )(own, *sources, shifted)
-    blocks = call(
-        inputs_kernel, tuple(shape(chan_dev, cells, dtype=wide) for _ in range(4)), 2
-    )(shifted, own)
 
     piece = added(exchange(parts, across), 1)
     piece, *blocks = lax.optimization_barrier((piece, *blocks))
@@ -274,7 +326,16 @@
         for c in range(chans)
     ]
     piece = lax.ppermute(piece, ("space", "chan"), home)
-    others = [move(blocks[0], -1), move(blocks[2], 1), move(blocks[3], 2)]
+    apart = [
+        (s * chans + c, s * chans + (c + (-2 if s % NCORE else 2)) % chans)
+        for s in range(spaces)
+        for c in range(chans)
+    ]
+    others = [
+        lax.ppermute(blocks[3], ("space", "chan"), apart),
+        move(blocks[0], -1),
+        move(blocks[2], 1),
+    ]
     piece = added(exchange(added(piece, 8), along), 8)
     whole = exchange(piece, across)
     grad_filters = call(

time: 105 us -> 102 us (0.971)
  the two profiles are of different devices: /device:TPU:8 before, /device:TPU:1 now
where the time goes in v6:
time: 102 us; the launch traced here: 101 us
  starting transfers between devices  72.6 us (71%)
  Pallas kernels  13.5 us (13%)
  waiting for transfers between devices  9.67 us (9%)
  local copies, waits for them, and re-layouts  4.32 us (4%)
    ppermute x7, starting transfers between devices, move(): lax.ppermute(cells, 'chan', [(i, (i + step) % chans) for i in range(chans)])  34.9 us
    all_to_all x3, starting transfers between devices, exchange(): lax.all_to_all(parts, 'space', 0, 0, axis_index_groups=groups, tiled=True)  22.2 us
    all_to_all x3, waiting for transfers between devices, exchange(): lax.all_to_all(parts, 'space', 0, 0, axis_index_groups=groups, tiled=True)  5.98 us
    ppermute x1, starting transfers between devices, per_device(): left = lax.ppermute(edges, 'space', [(i, i + 1) for i in range(spaces - 1)])  5.17 us
    ppermute x1, starting transfers between devices, per_device(): lax.ppermute(blocks[3], ('space', 'chan'), apart)  4.27 us
    ppermute x1, starting transfers between devices, per_device(): piece = lax.ppermute(piece, ('space', 'chan'), home)  4.19 us
    unnamed x6, local copies, waits for them, and re-layouts  3.63 us
    pallas_call x1, Pallas kernels, per_device(): pl.pallas_call(filters_kernel, out_shape=shape(3, 4 * chan_dev, 9 * chan_...  2.9 us
  transfers between devices with their start and end apart: 14, of which 4 were waited for; matrix products, arithmetic and copies ran while one was open for 2% of the time, Pallas kernels for 9%

profile of v6, /device:TPU:1, one launch (start us, length us, event | category | flops | bytes accessed | tf_op | source)
XLA Modules:
  0.0 100.9 jit_solution(9704379057420270388)
XLA Ops:
  0.6 1.0 copy.10
  1.8 11.5 %collective-permute-start = (bf16[24,3072]{1,0:T(8,128)(2,1)S(1)}, bf16[24,3072]{1,0:T(8,128)(2,1)S(1)}, u32[]{:S(2)}, u32[]{:S(2)}) collective-permute-start(bf16[24,3072]{1,0:T(8,128)(2,1)S(1)} %shard_map.50.refs_1_.own_ref), channel_id=1, source_target_pairs={{0,4},{1,5},{2,6},{3,7},{4,8},{5,9},{6,10},{7,11},{8,0},{9,1},{10,... | collective-permute-start | bytes 442376 | tf_op jit(solution)/shard_map/ppermute | solution.py:263
  13.3 5.6 %collective-permute-start.1 = (bf16[24,3072]{1,0:T(8,128)(2,1)S(1)}, bf16[24,3072]{1,0:T(8,128)(2,1)S(1)}, u32[]{:S(2)}, u32[]{:S(2)}) collective-permute-start(bf16[24,3072]{1,0:T(8,128)(2,1)S(1)} %shard_map.50.refs_1_.own_ref), channel_id=1, source_target_pairs={{0,8},{1,9},{2,10},{3,11},{4,0},{5,1},{6,2},{7,3},{8,4},{9,5},{10,... | collective-permute-start | bytes 442376 | tf_op jit(solution)/shard_map/ppermute | solution.py:263
  18.8 1.0 copy.9
  20.0 3.1 %collective-permute-start.2 = (bf16[24,3072]{1,0:T(8,128)(2,1)S(1)}, bf16[24,3072]{1,0:T(8,128)(2,1)S(1)}, u32[]{:S(2)}, u32[]{:S(2)}) collective-permute-start(bf16[24,3072]{1,0:T(8,128)(2,1)S(1)} %shard_map.51.refs_4_), channel_id=1, source_target_pairs={{0,1},{1,2},{2,3},{3,4},{4,5},{5,6},{6,7},{7,8},{8,9},{9,10},{10,1... | collective-permute-start | bytes 442376 | tf_op jit(solution)/shard_map/ppermute | solution.py:263
  23.1 6.1 %collective-permute-start.3 = (bf16[24,3072]{1,0:T(8,128)(2,1)S(1)}, bf16[24,3072]{1,0:T(8,128)(2,1)S(1)}, u32[]{:S(2)}, u32[]{:S(2)}) collective-permute-start(bf16[24,3072]{1,0:T(8,128)(2,1)S(1)} %shard_map.51.refs_4_), channel_id=1, source_target_pairs={{0,11},{1,0},{2,1},{3,2},{4,3},{5,4},{6,5},{7,6},{8,7},{9,8},{10,9... | collective-permute-start | bytes 442376 | tf_op jit(solution)/shard_map/ppermute | solution.py:263
  29.3 3.4 %collective-permute-start.4 = (bf16[24,3072]{1,0:T(8,128)(2,1)S(1)}, bf16[24,3072]{1,0:T(8,128)(2,1)S(1)}, u32[]{:S(2)}, u32[]{:S(2)}) collective-permute-start(bf16[24,3072]{1,0:T(8,128)(2,1)S(1)} %shard_map.51.refs_4_), channel_id=1, source_target_pairs={{0,10},{1,11},{2,0},{3,1},{4,2},{5,3},{6,4},{7,5},{8,6},{9,7},{10,... | collective-permute-start | bytes 442376 | tf_op jit(solution)/shard_map/ppermute | solution.py:263
  32.6 0.4 shard_map.53
  33.0 5.2 %collective-permute-start.5 = (bf16[72,128]{1,0:T(8,128)(2,1)S(1)}, bf16[72,128]{1,0:T(8,128)(2,1)S(1)}, u32[]{:S(2)}, u32[]{:S(2)}) collective-permute-start(bf16[72,128]{1,0:T(8,128)(2,1)S(1)} %shard_map.53), channel_id=1, source_target_pairs={{0,12},{12,24},{24,36},{36,48},{48,60},{60,72},{72,84},{84,96},{96... | collective-permute-start | bytes 55304 | tf_op jit(solution)/shard_map/ppermute | solution.py:280
  38.2 1.9 %collective-permute-start.6 = (bf16[72,128]{1,0:T(8,128)(2,1)S(1)}, bf16[72,128]{1,0:T(8,128)(2,1)S(1)}, u32[]{:S(2)}, u32[]{:S(2)}) collective-permute-start(bf16[72,128]{1,0:T(8,128)(2,1)S(1)} %shard_map.53), channel_id=1, source_target_pairs={{12,0},{24,12},{36,24},{48,36},{60,48},{72,60},{84,72},{96,84},{10... | collective-permute-start | bytes 55304 | tf_op jit(solution)/shard_map/ppermute | solution.py:281
  40.2 2.6 %collective-permute-done.4.refs_6_ = bf16[24,3072]{1,0:T(8,128)(2,1)S(1)} collective-permute-done((bf16[24,3072]{1,0:T(8,128)(2,1)S(1)}, bf16[24,3072]{1,0:T(8,128)(2,1)S(1)}, u32[]{:S(2)}, u32[]{:S(2)}) %collective-permute-start.4) | collective-permute-done | bytes 147488 | tf_op jit(solution)/shard_map/ppermute | solution.py:263
  42.8 1.8 %shard_map.52 = (bf16[216,4608]{1,0:T(8,128)(2,1)S(1)}, bf16[96,4096]{1,0:T(8,128)(2,1)S(1)}, bf16[96,128]{1,0:T(8,128)(2,1)S(1)}) custom-call(s32[1]{0:T(128)} %bitcast.third_ref, bf16[24,3072]{1,0:T(8,128)(2,1)S(1)} %collective-permute-done.refs_0_.near_ref, bf16[24,3072]{1,0:T(8,128)(2,1)S(1)} %shard_map.50.refs_1_.own_ref, ...), custom_call_target="tpu_custom_call" | custom-call | tf_op jit(solution)/shard_map/pallas_call | solution.py:301
  44.7 2.6 %shard_map.54 = (f32[8,72,128]{2,1,0:T(8,128)}, bf16[3,216,128]{2,1,0:T(8,128)(2,1)S(1)}) custom-call(s32[1]{0:T(128)} %bitcast.third_ref, bf16[216,4608]{1,0:T(8,128)(2,1)S(1)} %get-tuple-element.16.shifted_ref, bf16[96,4096]{1,0:T(8,128)(2,1)S(1)} %get-tuple-element.17.window_ref, bf16[96,128]{1,0:T(8,128)(2,1)S(1)} %get-tuple-element.18.ends_ref, ...), custom_call_target="tpu_custom_call" | custom-call | tf_op jit(solution)/shard_map/pallas_call | solution.py:311
  47.3 5.7 %all-to-all-start = ((f32[8,72,128]{2,1,0:T(8,128)}), f32[8,72,128]{2,1,0:T(8,128)S(1)}, u32[]{:S(2)}, u32[]{:S(2)}) async-start(f32[8,72,128]{2,1,0:T(8,128)} %get-tuple-element.19), calls=%async_computation | async-start | bytes 589824 | tf_op jit(solution)/shard_map/all_to_all | solution.py:266
  53.0 0.6 stack.23.picks_ref
  53.6 2.9 %shard_map.56.filters_ref = bf16[3,96,216]{2,1,0:T(8,128)(2,1)} custom-call(s32[5]{0:T(128)} %stack.23.picks_ref, bf16[9,288,288]{2,1,0:T(8,128)(2,1)} %w3.1, bf16[9,288,288]{2,1,0:T(8,128)(2,1)} %w3.1, bf16[9,288,288]{2,1,0:T(8,128)(2,1)} %w3.1, bf16[9,288,288]{2,1,0:T(8,128)(2,1)} %w3.1), custom_call_target="tpu_custom_call" | custom-call | tf_op jit(solution)/shard_map/pallas_call | solution.py:286
  56.5 0.9 copy-done
  57.4 1.8 %shard_map.57 = (f32[24,3072]{1,0:T(8,128)S(1)}, f32[24,3072]{1,0:T(8,128)S(1)}, f32[24,3072]{1,0:T(8,128)S(1)}, f32[24,3072]{1,0:T(8,128)S(1)}) custom-call(bf16[216,4608]{1,0:T(8,128)(2,1)S(1)} %get-tuple-element.16.shifted_ref, bf16[3,96,216]{2,1,0:T(8,128)(2,1)S(1)} %copy-done, bf16[3,216,128]{2,1,0:T(8,128)(2,1)S(1)} %get-tuple-element.20.borders_ref), custom_call_target="tpu_custom_call" | custom-call | tf_op jit(solution)/shard_map/pallas_call | solution.py:317
  59.2 0.7 copy-done.1
  60.0 4.2 %collective-permute-start.10 = (f32[1,72,128]{2,1,0:T(8,128)S(1)}, f32[1,72,128]{2,1,0:T(8,128)S(1)}, u32[]{:S(2)}, u32[]{:S(2)}) collective-permute-start(f32[1,72,128]{2,1,0:T(8,128)S(1)} %shard_map.55), channel_id=1, source_target_pairs={{0,11},{1,0},{2,1},{3,2},{4,3},{5,4},{6,5},{7,6},{8,7},{9,8},{10,9... | collective-permute-start | bytes 110600 | tf_op jit(solution)/shard_map/ppermute | solution.py:328
  64.2 1.0 %collective-permute-done.10.in_ref = f32[1,72,128]{2,1,0:T(8,128)S(1)} collective-permute-done((f32[1,72,128]{2,1,0:T(8,128)S(1)}, f32[1,72,128]{2,1,0:T(8,128)S(1)}, u32[]{:S(2)}, u32[]{:S(2)}) %collective-permute-start.10) | collective-permute-done | bytes 36896 | tf_op jit(solution)/shard_map/ppermute | solution.py:328
  65.2 0.7 shard_map.59
  65.9 6.3 %all-to-all-start.1 = ((f32[8,72,128]{2,1,0:T(8,128)}), f32[8,72,128]{2,1,0:T(8,128)S(1)}, u32[]{:S(2)}, u32[]{:S(2)}) async-start(f32[8,72,128]{2,1,0:T(8,128)} %shard_map.59), calls=%async_computation.1 | async-start | bytes 589824 | tf_op jit(solution)/shard_map/all_to_all | solution.py:266
  72.3 4.3 %collective-permute-start.7 = (f32[24,3072]{1,0:T(8,128)}, f32[24,3072]{1,0:T(8,128)S(1)}, u32[]{:S(2)}, u32[]{:S(2)}) collective-permute-start(f32[24,3072]{1,0:T(8,128)} %copy-done.1), channel_id=1, source_target_pairs={{0,2},{1,3},{2,4},{3,5},{4,6},{5,7},{6,8},{7,9},{8,10},{9,11},{10,... | collective-permute-start | bytes 884744 | tf_op jit(solution)/shard_map/ppermute | solution.py:335
  76.5 2.4 %collective-permute-start.8 = (f32[24,3072]{1,0:T(8,128)S(1)}, f32[24,3072]{1,0:T(8,128)S(1)}, u32[]{:S(2)}, u32[]{:S(2)}) collective-permute-start(f32[24,3072]{1,0:T(8,128)S(1)} %get-tuple-element.27), channel_id=1, source_target_pairs={{0,11},{1,0},{2,1},{3,2},{4,3},{5,4},{6,5},{7,6},{8,7},{9,8},{10,9... | collective-permute-start | bytes 884744 | tf_op jit(solution)/shard_map/ppermute | solution.py:263
  78.9 2.9 %collective-permute-start.9 = (f32[24,3072]{1,0:T(8,128)S(1)}, f32[24,3072]{1,0:T(8,128)S(1)}, u32[]{:S(2)}, u32[]{:S(2)}) collective-permute-start(f32[24,3072]{1,0:T(8,128)S(1)} %get-tuple-element.28), channel_id=1, source_target_pairs={{0,1},{1,2},{2,3},{3,4},{4,5},{5,6},{6,7},{7,8},{8,9},{9,10},{10,1... | collective-permute-start | bytes 884744 | tf_op jit(solution)/shard_map/ppermute | solution.py:263
  81.8 0.3 all-to-all-done.1.in_ref
  82.2 0.7 shard_map.60
  82.9 10.2 %all-to-all-start.2 = ((f32[8,72,128]{2,1,0:T(8,128)}), f32[8,72,128]{2,1,0:T(8,128)S(1)}, u32[]{:S(2)}, u32[]{:S(2)}) async-start(f32[8,72,128]{2,1,0:T(8,128)} %shard_map.60), calls=%async_computation.2 | async-start | bytes 589824 | tf_op jit(solution)/shard_map/all_to_all | solution.py:266
  93.1 1.1 %shard_map.58 = f32[24,32,96]{2,1,0:T(8,128)} custom-call(f32[24,3072]{1,0:T(8,128)S(1)} %get-tuple-element.25.a_ref, f32[24,3072]{1,0:T(8,128)S(1)} %collective-permute-done.7.b_ref, f32[24,3072]{1,0:T(8,128)S(1)} %collective-permute-done.8.c_ref, f32[24,3072]{1,0:T(8,128)S(1)} %collective-permute-done.9.d_ref), custom_call_target="tpu_custom_call" | custom-call | tf_op jit(solution)/shard_map/pallas_call | solution.py:347
  94.2 5.6 %all-to-all-done.2.whole_ref = f32[8,72,128]{2,1,0:T(8,128)S(1)} async-done(((f32[8,72,128]{2,1,0:T(8,128)}), f32[8,72,128]{2,1,0:T(8,128)S(1)}, u32[]{:S(2)}, u32[]{:S(2)}) %all-to-all-start.2) | async-done | bytes 294944 | tf_op jit(solution)/shard_map/all_to_all | solution.py:266
  99.9 1.1 %shard_map.61 = f32[9,24,288]{2,1,0:T(8,128)} custom-call(s32[1]{0:T(128)} %bitcast.9.layer_ref, f32[8,72,128]{2,1,0:T(8,128)S(1)} %all-to-all-done.2.whole_ref), custom_call_target="tpu_custom_call" | custom-call | tf_op jit(solution)/shard_map/pallas_call | solution.py:341
  (17 shorter events, 0.4 us)
Async XLA Ops:
  1.8 30.8 %collective-permute-start = (bf16[24,3072]{1,0:T(8,128)(2,1)S(1)}, bf16[24,3072]{1,0:T(8,128)(2,1)S(1)}, u32[]{:S(2)}, u32[]{:S(2)}) collective-permute-start(bf16[24,3072]{1,0:T(8,128)(2,1)S(1)} %shard_map.50.refs_1_.own_ref), channel_id=1, source_target_pairs={{0,4},{1,5},{2,6},{3,7},{4,8},{5,9},{6,10},{7,11},{8,0},{9,1},{10,... | collective-permute-start | bytes 442376 | tf_op jit(solution)/shard_map/ppermute | solution.py:263
  13.3 19.4 %collective-permute-start.1 = (bf16[24,3072]{1,0:T(8,128)(2,1)S(1)}, bf16[24,3072]{1,0:T(8,128)(2,1)S(1)}, u32[]{:S(2)}, u32[]{:S(2)}) collective-permute-start(bf16[24,3072]{1,0:T(8,128)(2,1)S(1)} %shard_map.50.refs_1_.own_ref), channel_id=1, source_target_pairs={{0,8},{1,9},{2,10},{3,11},{4,0},{5,1},{6,2},{7,3},{8,4},{9,5},{10,... | collective-permute-start | bytes 442376 | tf_op jit(solution)/shard_map/ppermute | solution.py:263
  20.0 20.2 %collective-permute-start.2 = (bf16[24,3072]{1,0:T(8,128)(2,1)S(1)}, bf16[24,3072]{1,0:T(8,128)(2,1)S(1)}, u32[]{:S(2)}, u32[]{:S(2)}) collective-permute-start(bf16[24,3072]{1,0:T(8,128)(2,1)S(1)} %shard_map.51.refs_4_), channel_id=1, source_target_pairs={{0,1},{1,2},{2,3},{3,4},{4,5},{5,6},{6,7},{7,8},{8,9},{9,10},{10,1... | collective-permute-start | bytes 442376 | tf_op jit(solution)/shard_map/ppermute | solution.py:263
  23.1 17.1 %collective-permute-start.3 = (bf16[24,3072]{1,0:T(8,128)(2,1)S(1)}, bf16[24,3072]{1,0:T(8,128)(2,1)S(1)}, u32[]{:S(2)}, u32[]{:S(2)}) collective-permute-start(bf16[24,3072]{1,0:T(8,128)(2,1)S(1)} %shard_map.51.refs_4_), channel_id=1, source_target_pairs={{0,11},{1,0},{2,1},{3,2},{4,3},{5,4},{6,5},{7,6},{8,7},{9,8},{10,9... | collective-permute-start | bytes 442376 | tf_op jit(solution)/shard_map/ppermute | solution.py:263
  29.3 13.6 %collective-permute-start.4 = (bf16[24,3072]{1,0:T(8,128)(2,1)S(1)}, bf16[24,3072]{1,0:T(8,128)(2,1)S(1)}, u32[]{:S(2)}, u32[]{:S(2)}) collective-permute-start(bf16[24,3072]{1,0:T(8,128)(2,1)S(1)} %shard_map.51.refs_4_), channel_id=1, source_target_pairs={{0,10},{1,11},{2,0},{3,1},{4,2},{5,3},{6,4},{7,5},{8,6},{9,7},{10,... | collective-permute-start | bytes 442376 | tf_op jit(solution)/shard_map/ppermute | solution.py:263
  33.0 11.6 %collective-permute-start.5 = (bf16[72,128]{1,0:T(8,128)(2,1)S(1)}, bf16[72,128]{1,0:T(8,128)(2,1)S(1)}, u32[]{:S(2)}, u32[]{:S(2)}) collective-permute-start(bf16[72,128]{1,0:T(8,128)(2,1)S(1)} %shard_map.53), channel_id=1, source_target_pairs={{0,12},{12,24},{24,36},{36,48},{48,60},{60,72},{72,84},{84,96},{96... | collective-permute-start | bytes 55304 | tf_op jit(solution)/shard_map/ppermute | solution.py:280
  38.2 6.4 %collective-permute-start.6 = (bf16[72,128]{1,0:T(8,128)(2,1)S(1)}, bf16[72,128]{1,0:T(8,128)(2,1)S(1)}, u32[]{:S(2)}, u32[]{:S(2)}) collective-permute-start(bf16[72,128]{1,0:T(8,128)(2,1)S(1)} %shard_map.53), channel_id=1, source_target_pairs={{12,0},{24,12},{36,24},{48,36},{60,48},{72,60},{84,72},{96,84},{10... | collective-permute-start | bytes 55304 | tf_op jit(solution)/shard_map/ppermute | solution.py:281
  47.3 12.6 %all-to-all-start = ((f32[8,72,128]{2,1,0:T(8,128)}), f32[8,72,128]{2,1,0:T(8,128)S(1)}, u32[]{:S(2)}, u32[]{:S(2)}) async-start(f32[8,72,128]{2,1,0:T(8,128)} %get-tuple-element.19), calls=%async_computation | async-start | bytes 589824 | tf_op jit(solution)/shard_map/all_to_all | solution.py:266
  56.5 0.9 copy-start
  59.2 0.7 copy-start.1
  60.0 5.2 %collective-permute-start.10 = (f32[1,72,128]{2,1,0:T(8,128)S(1)}, f32[1,72,128]{2,1,0:T(8,128)S(1)}, u32[]{:S(2)}, u32[]{:S(2)}) collective-permute-start(f32[1,72,128]{2,1,0:T(8,128)S(1)} %shard_map.55), channel_id=1, source_target_pairs={{0,11},{1,0},{2,1},{3,2},{4,3},{5,4},{6,5},{7,6},{8,7},{9,8},{10,9... | collective-permute-start | bytes 110600 | tf_op jit(solution)/shard_map/ppermute | solution.py:328
  65.9 16.2 %all-to-all-start.1 = ((f32[8,72,128]{2,1,0:T(8,128)}), f32[8,72,128]{2,1,0:T(8,128)S(1)}, u32[]{:S(2)}, u32[]{:S(2)}) async-start(f32[8,72,128]{2,1,0:T(8,128)} %shard_map.59), calls=%async_computation.1 | async-start | bytes 589824 | tf_op jit(solution)/shard_map/all_to_all | solution.py:266
  72.3 20.8 %collective-permute-start.7 = (f32[24,3072]{1,0:T(8,128)}, f32[24,3072]{1,0:T(8,128)S(1)}, u32[]{:S(2)}, u32[]{:S(2)}) collective-permute-start(f32[24,3072]{1,0:T(8,128)} %copy-done.1), channel_id=1, source_target_pairs={{0,2},{1,3},{2,4},{3,5},{4,6},{5,7},{6,8},{7,9},{8,10},{9,11},{10,... | collective-permute-start | bytes 884744 | tf_op jit(solution)/shard_map/ppermute | solution.py:335
  76.5 16.5 %collective-permute-start.8 = (f32[24,3072]{1,0:T(8,128)S(1)}, f32[24,3072]{1,0:T(8,128)S(1)}, u32[]{:S(2)}, u32[]{:S(2)}) collective-permute-start(f32[24,3072]{1,0:T(8,128)S(1)} %get-tuple-element.27), channel_id=1, source_target_pairs={{0,11},{1,0},{2,1},{3,2},{4,3},{5,4},{6,5},{7,6},{8,7},{9,8},{10,9... | collective-permute-start | bytes 884744 | tf_op jit(solution)/shard_map/ppermute | solution.py:263
  78.9 14.1 %collective-permute-start.9 = (f32[24,3072]{1,0:T(8,128)S(1)}, f32[24,3072]{1,0:T(8,128)S(1)}, u32[]{:S(2)}, u32[]{:S(2)}) collective-permute-start(f32[24,3072]{1,0:T(8,128)S(1)} %get-tuple-element.28), channel_id=1, source_target_pairs={{0,1},{1,2},{2,3},{3,4},{4,5},{5,6},{6,7},{7,8},{8,9},{9,10},{10,1... | collective-permute-start | bytes 884744 | tf_op jit(solution)/shard_map/ppermute | solution.py:263
  82.9 17.0 %all-to-all-start.2 = ((f32[8,72,128]{2,1,0:T(8,128)}), f32[8,72,128]{2,1,0:T(8,128)S(1)}, u32[]{:S(2)}, u32[]{:S(2)}) async-start(f32[8,72,128]{2,1,0:T(8,128)} %shard_map.60), calls=%async_computation.2 | async-start | bytes 589824 | tf_op jit(solution)/shard_map/all_to_all | solution.py:266

commit v7 on v6

--- a/solution.py
+++ b/solution.py
@@ -71,20 +71,29 @@
     return rows
 
 
-def filters_kernel(picks_ref, w0, w1, w2, w3, own_ref):
+def window_block(j, code):
+    layer, core = code // 2, code % 2
+    step = (11, 0, 1, 2 + 8 * core)[j]
+    return (layer + step) % 12
+
+
+def filters_kernel(code_ref, w0, w1, w2, w3, own_ref):
     chans = w0.shape[1]
     outs = (12 * chans, 3 * chans)
     column = lax.broadcasted_iota(jnp.int32, outs, 1)
     third = (column >= chans).astype(jnp.int32) + (column >= 2 * chans).astype(jnp.int32)
-    wanted = column + 3 * chans * third + chans * picks_ref[4]
+    wanted = column + 3 * chans * third + chans * ((code_ref[0] // 2) % 4)
     chosen = (lax.broadcasted_iota(jnp.int32, outs, 0) == wanted).astype(jnp.float32)
     chosen = chosen.astype(own_ref.dtype)
+    picked = []
+    for w in (w0, w1, w2, w3):
+        flat = w[...].reshape(9 * chans, 12 * chans)
+        picked.append(jnp.dot(flat, chosen, preferred_element_type=jnp.float32))
     for b in range(3):
         taps = []
         for a in range(3):
-            rows = [w[3 * a + b].astype(jnp.float32) for w in (w0, w1, w2, w3)]
-            rows = jnp.concatenate(rows, axis=0).astype(own_ref.dtype)
-            taps.append(jnp.dot(rows, chosen, preferred_element_type=jnp.float32))
+            cut = slice((3 * a + b) * chans, (3 * a + b + 1) * chans)
+            taps.append(jnp.concatenate([rows[cut] for rows in picked], axis=0))
         own_ref[b] = jnp.concatenate(taps, axis=1).astype(own_ref.dtype)
 
 
@@ -97,7 +106,8 @@
 
 
 def build_kernel(third_ref, *refs):
-    g_refs, x_refs, (shifted_ref, window_ref, ends_ref) = refs[:3], refs[3:7], refs[7:]
+    g_refs, (x3, x2, x0, x1), (shifted_ref, window_ref, ends_ref) = refs[:3], refs[3:7], refs[8:]
+    x_refs = (x0, x1, x2, x3)
     chans = g_refs[0].shape[0]
     rows = g_refs[0].shape[1] // WIDTH
     third = third_ref[0]
@@ -280,9 +290,7 @@
     left = lax.ppermute(edges, "space", [(i, i + 1) for i in range(spaces - 1)])
     right = lax.ppermute(edges, "space", [(i + 1, i) for i in range(spaces - 1)])
 
-    beyond = jnp.where(lax.axis_index("space") % NCORE == 0, layer + 2, layer + chans - 2)
-    blocks = [layer + chans - 1, layer, layer + 1, beyond]
-    picks = jnp.stack([block % chans for block in blocks] + [layer % 4]).astype(jnp.int32)
+    code = (2 * layer + lax.axis_index("space") % NCORE)[None]
     own = pl.pallas_call(
         filters_kernel,
         out_shape=shape(3, 4 * chan_dev, 9 * chan_dev),
@@ -290,12 +298,12 @@
             num_scalar_prefetch=1,
             grid=(1,),
             in_specs=[
-                pl.BlockSpec((9, chan_dev, 12 * chan_dev), lambda i, at, j=j: (0, at[j], 0))
+                pl.BlockSpec((9, chan_dev, 12 * chan_dev), lambda i, at, j=j: (0, window_block(j, at[0]), 0))
                 for j in range(4)
             ],
             out_specs=pl.BlockSpec((3, 4 * chan_dev, 9 * chan_dev), lambda i, at: (0, 0, 0)),
         ),
-    )(picks, filters, filters, filters, filters)
+    )(code, filters, filters, filters, filters)
 
     third = (layer // 4)[None]
     shifted, window, ends = call(
@@ -305,9 +313,9 @@
             shape(4 * chan_dev, rows * LANES),
             shape(4 * chan_dev, LANES),
         ),
-        8,
+        9,
         1,
-    )(third, *grads, *sources)
+    )(third, *grads, sources[3], sources[2], sources[0], sources[1], own)
     parts, borders = call(
         weights_kernel,
         (shape(8, 3 * chan_dev, LANES, dtype=wide), shape(3, 9 * chan_dev, LANES)),

time: 102 us -> 103 us (level)
  waiting for transfers between devices: 9.67 us -> 12.1 us
    all_to_all x3, waiting for transfers between devices: 5.98 us -> 8.9 us  [exchange(): lax.all_to_all(parts, 'space', 0, 0, axis_index_groups=groups, tiled=True)]
    ppermute x1, starting transfers between devices: 5.17 us -> 7.7 us  [per_device(): left = lax.ppermute(edges, 'space', [(i, i + 1) for i in range(spaces - 1)])]
    all_to_all x3, starting transfers between devices: 22.2 us -> 21 us  [exchange(): lax.all_to_all(parts, 'space', 0, 0, axis_index_groups=groups, tiled=True)]
    ppermute x1, starting transfers between devices: 4.19 us -> 3.11 us  [per_device(): piece = lax.ppermute(piece, ('space', 'chan'), home)]
    unnamed x6 -> x8, local copies, waits for them, and re-layouts: 3.63 us -> 3.63 us
  transfers between devices with their start and end apart: 14 -> 14, of which waited for: 4 -> 5; matrix products, arithmetic and copies ran while one was open for 2% -> 1% of each run, Pallas kernels for 9% -> 8%
where the time goes in v7:
time: 103 us; the launch traced here: 102 us
  starting transfers between devices  72.7 us (71%)
  Pallas kernels  12.8 us (12%)
  waiting for transfers between devices  12.1 us (12%)
  local copies, waits for them, and re-layouts  3.72 us (4%)
    ppermute x7, starting transfers between devices, move(): lax.ppermute(cells, 'chan', [(i, (i + step) % chans) for i in range(chans)])  35.7 us
    all_to_all x3, starting transfers between devices, exchange(): lax.all_to_all(parts, 'space', 0, 0, axis_index_groups=groups, tiled=True)  21 us
    all_to_all x3, waiting for transfers between devices, exchange(): lax.all_to_all(parts, 'space', 0, 0, axis_index_groups=groups, tiled=True)  8.9 us
    ppermute x1, starting transfers between devices, per_device(): left = lax.ppermute(edges, 'space', [(i, i + 1) for i in range(spaces - 1)])  7.7 us
    unnamed x8, local copies, waits for them, and re-layouts  3.63 us
    ppermute x1, starting transfers between devices, per_device(): lax.ppermute(blocks[3], ('space', 'chan'), apart)  3.25 us
    ppermute x1, starting transfers between devices, per_device(): piece = lax.ppermute(piece, ('space', 'chan'), home)  3.11 us
    pallas_call x1, Pallas kernels, per_device(): call(weights_kernel, (shape(8, 3 * chan_dev, LANES, dtype=wide), shape(3,...  2.63 us
  transfers between devices with their start and end apart: 14, of which 5 were waited for; matrix products, arithmetic and copies ran while one was open for 1% of the time, Pallas kernels for 8%

profile of v7, /device:TPU:1, one launch (start us, length us, event | category | flops | bytes accessed | tf_op | source)
XLA Modules:
  0.0 102.2 jit_solution(14375232231302477196)
XLA Ops:
  0.6 1.0 copy.10
  1.8 11.5 %collective-permute-start = (bf16[24,3072]{1,0:T(8,128)(2,1)S(1)}, bf16[24,3072]{1,0:T(8,128)(2,1)S(1)}, u32[]{:S(2)}, u32[]{:S(2)}) collective-permute-start(bf16[24,3072]{1,0:T(8,128)(2,1)S(1)} %shard_map.50.refs_1_.own_ref), channel_id=1, source_target_pairs={{0,4},{1,5},{2,6},{3,7},{4,8},{5,9},{6,10},{7,11},{8,0},{9,1},{10,... | collective-permute-start | bytes 442376 | tf_op jit(solution)/shard_map/ppermute | solution.py:273
  13.3 5.6 %collective-permute-start.1 = (bf16[24,3072]{1,0:T(8,128)(2,1)S(1)}, bf16[24,3072]{1,0:T(8,128)(2,1)S(1)}, u32[]{:S(2)}, u32[]{:S(2)}) collective-permute-start(bf16[24,3072]{1,0:T(8,128)(2,1)S(1)} %shard_map.50.refs_1_.own_ref), channel_id=1, source_target_pairs={{0,8},{1,9},{2,10},{3,11},{4,0},{5,1},{6,2},{7,3},{8,4},{9,5},{10,... | collective-permute-start | bytes 442376 | tf_op jit(solution)/shard_map/ppermute | solution.py:273
  18.8 1.0 copy.9
  20.0 7.3 %collective-permute-start.2 = (bf16[24,3072]{1,0:T(8,128)(2,1)S(1)}, bf16[24,3072]{1,0:T(8,128)(2,1)S(1)}, u32[]{:S(2)}, u32[]{:S(2)}) collective-permute-start(bf16[24,3072]{1,0:T(8,128)(2,1)S(1)} %shard_map.51.refs_6_), channel_id=1, source_target_pairs={{0,10},{1,11},{2,0},{3,1},{4,2},{5,3},{6,4},{7,5},{8,6},{9,7},{10,... | collective-permute-start | bytes 442376 | tf_op jit(solution)/shard_map/ppermute | solution.py:273
  27.3 2.2 %collective-permute-start.3 = (bf16[24,3072]{1,0:T(8,128)(2,1)S(1)}, bf16[24,3072]{1,0:T(8,128)(2,1)S(1)}, u32[]{:S(2)}, u32[]{:S(2)}) collective-permute-start(bf16[24,3072]{1,0:T(8,128)(2,1)S(1)} %shard_map.51.refs_6_), channel_id=1, source_target_pairs={{0,11},{1,0},{2,1},{3,2},{4,3},{5,4},{6,5},{7,6},{8,7},{9,8},{10,9... | collective-permute-start | bytes 442376 | tf_op jit(solution)/shard_map/ppermute | solution.py:273
  29.5 3.1 %collective-permute-start.4 = (bf16[24,3072]{1,0:T(8,128)(2,1)S(1)}, bf16[24,3072]{1,0:T(8,128)(2,1)S(1)}, u32[]{:S(2)}, u32[]{:S(2)}) collective-permute-start(bf16[24,3072]{1,0:T(8,128)(2,1)S(1)} %shard_map.51.refs_6_), channel_id=1, source_target_pairs={{0,1},{1,2},{2,3},{3,4},{4,5},{5,6},{6,7},{7,8},{8,9},{9,10},{10,1... | collective-permute-start | bytes 442376 | tf_op jit(solution)/shard_map/ppermute | solution.py:273
  32.6 0.4 shard_map.54
  33.0 7.7 %collective-permute-start.5 = (bf16[72,128]{1,0:T(8,128)(2,1)S(1)}, bf16[72,128]{1,0:T(8,128)(2,1)S(1)}, u32[]{:S(2)}, u32[]{:S(2)}) collective-permute-start(bf16[72,128]{1,0:T(8,128)(2,1)S(1)} %shard_map.54), channel_id=1, source_target_pairs={{0,12},{12,24},{24,36},{36,48},{48,60},{60,72},{72,84},{84,96},{96... | collective-permute-start | bytes 55304 | tf_op jit(solution)/shard_map/ppermute | solution.py:290
  40.7 1.9 %collective-permute-start.6 = (bf16[72,128]{1,0:T(8,128)(2,1)S(1)}, bf16[72,128]{1,0:T(8,128)(2,1)S(1)}, u32[]{:S(2)}, u32[]{:S(2)}) collective-permute-start(bf16[72,128]{1,0:T(8,128)(2,1)S(1)} %shard_map.54), channel_id=1, source_target_pairs={{12,0},{24,12},{36,24},{48,36},{60,48},{72,60},{84,72},{96,84},{10... | collective-permute-start | bytes 55304 | tf_op jit(solution)/shard_map/ppermute | solution.py:291
  42.7 2.2 %shard_map.52.refs_7_.filters_ref = bf16[3,96,216]{2,1,0:T(8,128)(2,1)} custom-call(s32[1]{0:T(128)} %bitcast.3.code_ref, bf16[9,288,288]{2,1,0:T(8,128)(2,1)} %w3.1, bf16[9,288,288]{2,1,0:T(8,128)(2,1)} %w3.1, bf16[9,288,288]{2,1,0:T(8,128)(2,1)} %w3.1, bf16[9,288,288]{2,1,0:T(8,128)(2,1)} %w3.1), custom_call_target="tpu_custom_call" | custom-call | tf_op jit(solution)/shard_map/pallas_call | solution.py:294
  45.0 0.9 copy-done
  45.9 1.8 %shard_map.53 = (bf16[216,4608]{1,0:T(8,128)(2,1)S(1)}, bf16[96,4096]{1,0:T(8,128)(2,1)S(1)}, bf16[96,128]{1,0:T(8,128)(2,1)S(1)}) custom-call(s32[1]{0:T(128)} %bitcast.third_ref, bf16[24,3072]{1,0:T(8,128)(2,1)S(1)} %collective-permute-done.refs_0_.near_ref, bf16[24,3072]{1,0:T(8,128)(2,1)S(1)} %shard_map.50.refs_1_.own_ref, ...), custom_call_target="tpu_custom_call" | custom-call | tf_op jit(solution)/shard_map/pallas_call | solution.py:309
  47.7 2.6 %shard_map.55 = (f32[8,72,128]{2,1,0:T(8,128)}, bf16[3,216,128]{2,1,0:T(8,128)(2,1)S(1)}) custom-call(s32[1]{0:T(128)} %bitcast.third_ref, bf16[216,4608]{1,0:T(8,128)(2,1)S(1)} %get-tuple-element.16.shifted_ref, bf16[96,4096]{1,0:T(8,128)(2,1)S(1)} %get-tuple-element.17.window_ref, bf16[96,128]{1,0:T(8,128)(2,1)S(1)} %get-tuple-element.18.ends_ref, ...), custom_call_target="tpu_custom_call" | custom-call | tf_op jit(solution)/shard_map/pallas_call | solution.py:319
  50.4 7.0 %all-to-all-start = ((f32[8,72,128]{2,1,0:T(8,128)}), f32[8,72,128]{2,1,0:T(8,128)S(1)}, u32[]{:S(2)}, u32[]{:S(2)}) async-start(f32[8,72,128]{2,1,0:T(8,128)} %get-tuple-element.19), calls=%async_computation | async-start | bytes 589824 | tf_op jit(solution)/shard_map/all_to_all | solution.py:276
  57.3 1.8 %shard_map.57 = (f32[24,3072]{1,0:T(8,128)S(1)}, f32[24,3072]{1,0:T(8,128)S(1)}, f32[24,3072]{1,0:T(8,128)S(1)}, f32[24,3072]{1,0:T(8,128)S(1)}) custom-call(bf16[216,4608]{1,0:T(8,128)(2,1)S(1)} %get-tuple-element.16.shifted_ref, bf16[3,96,216]{2,1,0:T(8,128)(2,1)S(1)} %copy-done.1, bf16[3,216,128]{2,1,0:T(8,128)(2,1)S(1)} %get-tuple-element.20.borders_ref), custom_call_target="tpu_custom_call" | custom-call | tf_op jit(solution)/shard_map/pallas_call | solution.py:325
  59.2 0.7 copy-done.2
  59.9 4.2 %all-to-all-done.in_ref = f32[8,72,128]{2,1,0:T(8,128)S(1)} async-done(((f32[8,72,128]{2,1,0:T(8,128)}), f32[8,72,128]{2,1,0:T(8,128)S(1)}, u32[]{:S(2)}, u32[]{:S(2)}) %all-to-all-start) | async-done | bytes 294944 | tf_op jit(solution)/shard_map/all_to_all | solution.py:276
  64.2 3.1 %collective-permute-start.10 = (f32[1,72,128]{2,1,0:T(8,128)S(1)}, f32[1,72,128]{2,1,0:T(8,128)S(1)}, u32[]{:S(2)}, u32[]{:S(2)}) collective-permute-start(f32[1,72,128]{2,1,0:T(8,128)S(1)} %shard_map.56), channel_id=1, source_target_pairs={{0,11},{1,0},{2,1},{3,2},{4,3},{5,4},{6,5},{7,6},{8,7},{9,8},{10,9... | collective-permute-start | bytes 110600 | tf_op jit(solution)/shard_map/ppermute | solution.py:336
  67.3 1.6 %collective-permute-done.10.in_ref = f32[1,72,128]{2,1,0:T(8,128)S(1)} collective-permute-done((f32[1,72,128]{2,1,0:T(8,128)S(1)}, f32[1,72,128]{2,1,0:T(8,128)S(1)}, u32[]{:S(2)}, u32[]{:S(2)}) %collective-permute-start.10) | collective-permute-done | bytes 36896 | tf_op jit(solution)/shard_map/ppermute | solution.py:336
  68.9 0.7 shard_map.59
  69.6 5.9 %all-to-all-start.1 = ((f32[8,72,128]{2,1,0:T(8,128)}), f32[8,72,128]{2,1,0:T(8,128)S(1)}, u32[]{:S(2)}, u32[]{:S(2)}) async-start(f32[8,72,128]{2,1,0:T(8,128)} %shard_map.59), calls=%async_computation.1 | async-start | bytes 589824 | tf_op jit(solution)/shard_map/all_to_all | solution.py:276
  75.5 3.2 %collective-permute-start.7 = (f32[24,3072]{1,0:T(8,128)}, f32[24,3072]{1,0:T(8,128)S(1)}, u32[]{:S(2)}, u32[]{:S(2)}) collective-permute-start(f32[24,3072]{1,0:T(8,128)} %copy-done.2), channel_id=1, source_target_pairs={{0,2},{1,3},{2,4},{3,5},{4,6},{5,7},{6,8},{7,9},{8,10},{9,11},{10,... | collective-permute-start | bytes 884744 | tf_op jit(solution)/shard_map/ppermute | solution.py:343
  78.8 3.0 %collective-permute-start.8 = (f32[24,3072]{1,0:T(8,128)S(1)}, f32[24,3072]{1,0:T(8,128)S(1)}, u32[]{:S(2)}, u32[]{:S(2)}) collective-permute-start(f32[24,3072]{1,0:T(8,128)S(1)} %get-tuple-element.27), channel_id=1, source_target_pairs={{0,11},{1,0},{2,1},{3,2},{4,3},{5,4},{6,5},{7,6},{8,7},{9,8},{10,9... | collective-permute-start | bytes 884744 | tf_op jit(solution)/shard_map/ppermute | solution.py:273
  81.8 3.1 %collective-permute-start.9 = (f32[24,3072]{1,0:T(8,128)S(1)}, f32[24,3072]{1,0:T(8,128)S(1)}, u32[]{:S(2)}, u32[]{:S(2)}) collective-permute-start(f32[24,3072]{1,0:T(8,128)S(1)} %get-tuple-element.28), channel_id=1, source_target_pairs={{0,1},{1,2},{2,3},{3,4},{4,5},{5,6},{6,7},{7,8},{8,9},{9,10},{10,1... | collective-permute-start | bytes 884744 | tf_op jit(solution)/shard_map/ppermute | solution.py:273
  84.9 0.6 all-to-all-done.1.in_ref
  85.5 0.7 shard_map.60
  86.2 8.2 %all-to-all-start.2 = ((f32[8,72,128]{2,1,0:T(8,128)}), f32[8,72,128]{2,1,0:T(8,128)S(1)}, u32[]{:S(2)}, u32[]{:S(2)}) async-start(f32[8,72,128]{2,1,0:T(8,128)} %shard_map.60), calls=%async_computation.2 | async-start | bytes 589824 | tf_op jit(solution)/shard_map/all_to_all | solution.py:276
  94.4 1.6 %collective-permute-done.9.d_ref = f32[24,3072]{1,0:T(8,128)S(1)} collective-permute-done((f32[24,3072]{1,0:T(8,128)S(1)}, f32[24,3072]{1,0:T(8,128)S(1)}, u32[]{:S(2)}, u32[]{:S(2)}) %collective-permute-start.9) | collective-permute-done | bytes 294944 | tf_op jit(solution)/shard_map/ppermute | solution.py:273
  96.0 1.1 %shard_map.58 = f32[24,32,96]{2,1,0:T(8,128)} custom-call(f32[24,3072]{1,0:T(8,128)S(1)} %get-tuple-element.25.a_ref, f32[24,3072]{1,0:T(8,128)S(1)} %collective-permute-done.7.b_ref, f32[24,3072]{1,0:T(8,128)S(1)} %collective-permute-done.8.c_ref, f32[24,3072]{1,0:T(8,128)S(1)} %collective-permute-done.9.d_ref), custom_call_target="tpu_custom_call" | custom-call | tf_op jit(solution)/shard_map/pallas_call | solution.py:355
  97.1 4.1 %all-to-all-done.2.whole_ref = f32[8,72,128]{2,1,0:T(8,128)S(1)} async-done(((f32[8,72,128]{2,1,0:T(8,128)}), f32[8,72,128]{2,1,0:T(8,128)S(1)}, u32[]{:S(2)}, u32[]{:S(2)}) %all-to-all-start.2) | async-done | bytes 294944 | tf_op jit(solution)/shard_map/all_to_all | solution.py:276
  101.2 1.1 %shard_map.61 = f32[9,24,288]{2,1,0:T(8,128)} custom-call(s32[1]{0:T(128)} %bitcast.5.layer_ref, f32[8,72,128]{2,1,0:T(8,128)S(1)} %all-to-all-done.2.whole_ref), custom_call_target="tpu_custom_call" | custom-call | tf_op jit(solution)/shard_map/pallas_call | solution.py:349
  (18 shorter events, 0.4 us)
Async XLA Ops:
  1.8 30.8 %collective-permute-start = (bf16[24,3072]{1,0:T(8,128)(2,1)S(1)}, bf16[24,3072]{1,0:T(8,128)(2,1)S(1)}, u32[]{:S(2)}, u32[]{:S(2)}) collective-permute-start(bf16[24,3072]{1,0:T(8,128)(2,1)S(1)} %shard_map.50.refs_1_.own_ref), channel_id=1, source_target_pairs={{0,4},{1,5},{2,6},{3,7},{4,8},{5,9},{6,10},{7,11},{8,0},{9,1},{10,... | collective-permute-start | bytes 442376 | tf_op jit(solution)/shard_map/ppermute | solution.py:273
  13.3 19.4 %collective-permute-start.1 = (bf16[24,3072]{1,0:T(8,128)(2,1)S(1)}, bf16[24,3072]{1,0:T(8,128)(2,1)S(1)}, u32[]{:S(2)}, u32[]{:S(2)}) collective-permute-start(bf16[24,3072]{1,0:T(8,128)(2,1)S(1)} %shard_map.50.refs_1_.own_ref), channel_id=1, source_target_pairs={{0,8},{1,9},{2,10},{3,11},{4,0},{5,1},{6,2},{7,3},{8,4},{9,5},{10,... | collective-permute-start | bytes 442376 | tf_op jit(solution)/shard_map/ppermute | solution.py:273
  20.0 24.9 %collective-permute-start.2 = (bf16[24,3072]{1,0:T(8,128)(2,1)S(1)}, bf16[24,3072]{1,0:T(8,128)(2,1)S(1)}, u32[]{:S(2)}, u32[]{:S(2)}) collective-permute-start(bf16[24,3072]{1,0:T(8,128)(2,1)S(1)} %shard_map.51.refs_6_), channel_id=1, source_target_pairs={{0,10},{1,11},{2,0},{3,1},{4,2},{5,3},{6,4},{7,5},{8,6},{9,7},{10,... | collective-permute-start | bytes 442376 | tf_op jit(solution)/shard_map/ppermute | solution.py:273
  27.3 17.6 %collective-permute-start.3 = (bf16[24,3072]{1,0:T(8,128)(2,1)S(1)}, bf16[24,3072]{1,0:T(8,128)(2,1)S(1)}, u32[]{:S(2)}, u32[]{:S(2)}) collective-permute-start(bf16[24,3072]{1,0:T(8,128)(2,1)S(1)} %shard_map.51.refs_6_), channel_id=1, source_target_pairs={{0,11},{1,0},{2,1},{3,2},{4,3},{5,4},{6,5},{7,6},{8,7},{9,8},{10,9... | collective-permute-start | bytes 442376 | tf_op jit(solution)/shard_map/ppermute | solution.py:273
  29.5 15.4 %collective-permute-start.4 = (bf16[24,3072]{1,0:T(8,128)(2,1)S(1)}, bf16[24,3072]{1,0:T(8,128)(2,1)S(1)}, u32[]{:S(2)}, u32[]{:S(2)}) collective-permute-start(bf16[24,3072]{1,0:T(8,128)(2,1)S(1)} %shard_map.51.refs_6_), channel_id=1, source_target_pairs={{0,1},{1,2},{2,3},{3,4},{4,5},{5,6},{6,7},{7,8},{8,9},{9,10},{10,1... | collective-permute-start | bytes 442376 | tf_op jit(solution)/shard_map/ppermute | solution.py:273
  33.0 14.7 %collective-permute-start.5 = (bf16[72,128]{1,0:T(8,128)(2,1)S(1)}, bf16[72,128]{1,0:T(8,128)(2,1)S(1)}, u32[]{:S(2)}, u32[]{:S(2)}) collective-permute-start(bf16[72,128]{1,0:T(8,128)(2,1)S(1)} %shard_map.54), channel_id=1, source_target_pairs={{0,12},{12,24},{24,36},{36,48},{48,60},{60,72},{72,84},{84,96},{96... | collective-permute-start | bytes 55304 | tf_op jit(solution)/shard_map/ppermute | solution.py:290
  40.7 7.0 %collective-permute-start.6 = (bf16[72,128]{1,0:T(8,128)(2,1)S(1)}, bf16[72,128]{1,0:T(8,128)(2,1)S(1)}, u32[]{:S(2)}, u32[]{:S(2)}) collective-permute-start(bf16[72,128]{1,0:T(8,128)(2,1)S(1)} %shard_map.54), channel_id=1, source_target_pairs={{12,0},{24,12},{36,24},{48,36},{60,48},{72,60},{84,72},{96,84},{10... | collective-permute-start | bytes 55304 | tf_op jit(solution)/shard_map/ppermute | solution.py:291
  45.0 0.9 copy-start
  47.7 9.6 %copy-start.1 = (bf16[3,96,216]{2,1,0:T(8,128)(2,1)S(1)}, bf16[3,96,216]{2,1,0:T(8,128)(2,1)}, u32[]{:S(2)}) copy-start(bf16[3,96,216]{2,1,0:T(8,128)(2,1)} %shard_map.52.refs_7_.filters_ref) | copy-start | bytes 373252
  50.4 13.8 %all-to-all-start = ((f32[8,72,128]{2,1,0:T(8,128)}), f32[8,72,128]{2,1,0:T(8,128)S(1)}, u32[]{:S(2)}, u32[]{:S(2)}) async-start(f32[8,72,128]{2,1,0:T(8,128)} %get-tuple-element.19), calls=%async_computation | async-start | bytes 589824 | tf_op jit(solution)/shard_map/all_to_all | solution.py:276
  59.2 0.7 copy-start.2
  64.2 4.7 %collective-permute-start.10 = (f32[1,72,128]{2,1,0:T(8,128)S(1)}, f32[1,72,128]{2,1,0:T(8,128)S(1)}, u32[]{:S(2)}, u32[]{:S(2)}) collective-permute-start(f32[1,72,128]{2,1,0:T(8,128)S(1)} %shard_map.56), channel_id=1, source_target_pairs={{0,11},{1,0},{2,1},{3,2},{4,3},{5,4},{6,5},{7,6},{8,7},{9,8},{10,9... | collective-permute-start | bytes 110600 | tf_op jit(solution)/shard_map/ppermute | solution.py:336
  69.6 15.9 %all-to-all-start.1 = ((f32[8,72,128]{2,1,0:T(8,128)}), f32[8,72,128]{2,1,0:T(8,128)S(1)}, u32[]{:S(2)}, u32[]{:S(2)}) async-start(f32[8,72,128]{2,1,0:T(8,128)} %shard_map.59), calls=%async_computation.1 | async-start | bytes 589824 | tf_op jit(solution)/shard_map/all_to_all | solution.py:276
  75.5 18.8 %collective-permute-start.7 = (f32[24,3072]{1,0:T(8,128)}, f32[24,3072]{1,0:T(8,128)S(1)}, u32[]{:S(2)}, u32[]{:S(2)}) collective-permute-start(f32[24,3072]{1,0:T(8,128)} %copy-done.2), channel_id=1, source_target_pairs={{0,2},{1,3},{2,4},{3,5},{4,6},{5,7},{6,8},{7,9},{8,10},{9,11},{10,... | collective-permute-start | bytes 884744 | tf_op jit(solution)/shard_map/ppermute | solution.py:343
  78.8 15.6 %collective-permute-start.8 = (f32[24,3072]{1,0:T(8,128)S(1)}, f32[24,3072]{1,0:T(8,128)S(1)}, u32[]{:S(2)}, u32[]{:S(2)}) collective-permute-start(f32[24,3072]{1,0:T(8,128)S(1)} %get-tuple-element.27), channel_id=1, source_target_pairs={{0,11},{1,0},{2,1},{3,2},{4,3},{5,4},{6,5},{7,6},{8,7},{9,8},{10,9... | collective-permute-start | bytes 884744 | tf_op jit(solution)/shard_map/ppermute | solution.py:273
  81.8 14.2 %collective-permute-start.9 = (f32[24,3072]{1,0:T(8,128)S(1)}, f32[24,3072]{1,0:T(8,128)S(1)}, u32[]{:S(2)}, u32[]{:S(2)}) collective-permute-start(f32[24,3072]{1,0:T(8,128)S(1)} %get-tuple-element.28), channel_id=1, source_target_pairs={{0,1},{1,2},{2,3},{3,4},{4,5},{5,6},{6,7},{7,8},{8,9},{9,10},{10,1... | collective-permute-start | bytes 884744 | tf_op jit(solution)/shard_map/ppermute | solution.py:273
  86.2 15.0 %all-to-all-start.2 = ((f32[8,72,128]{2,1,0:T(8,128)}), f32[8,72,128]{2,1,0:T(8,128)S(1)}, u32[]{:S(2)}, u32[]{:S(2)}) async-start(f32[8,72,128]{2,1,0:T(8,128)} %shard_map.60), calls=%async_computation.2 | async-start | bytes 589824 | tf_op jit(solution)/shard_map/all_to_all | solution.py:276

commit v8 on v7

--- a/solution.py
+++ b/solution.py
@@ -29,8 +29,15 @@
 
 
 def pack_kernel(cells_ref, dense_ref):
-    for start in range(0, cells_ref.shape[0], 4):
-        store_dense(dense_ref, start, [cells_ref[start + i].astype(jnp.float32) for i in range(4)])
+    chans, rows, width = cells_ref.shape
+    for start in range(0, rows, 8):
+        block = cells_ref[:, start : start + 8, :].astype(jnp.float32)
+        block = jnp.concatenate(
+            [block, jnp.zeros((chans, 8, LANES - width), jnp.float32)], axis=2
+        )
+        block = jnp.swapaxes(block, 0, 1)
+        for half in (0, 4):
+            store_dense(dense_ref, start + half, [block[half + i] for i in range(4)])
 
 
 def edges_kernel(near_ref, own_ref, far_ref, edges_ref):
@@ -77,7 +84,7 @@
     return (layer + step) % 12
 
 
-def filters_kernel(code_ref, w0, w1, w2, w3, own_ref):
+def filters_kernel(code_ref, w0, w1, w2, w3, own_ref, token_ref):
     chans = w0.shape[1]
     outs = (12 * chans, 3 * chans)
     column = lax.broadcasted_iota(jnp.int32, outs, 1)
@@ -85,6 +92,7 @@
     wanted = column + 3 * chans * third + chans * ((code_ref[0] // 2) % 4)
     chosen = (lax.broadcasted_iota(jnp.int32, outs, 0) == wanted).astype(jnp.float32)
     chosen = chosen.astype(own_ref.dtype)
+    token_ref[...] = jnp.zeros(token_ref.shape, token_ref.dtype)
     picked = []
     for w in (w0, w1, w2, w3):
         flat = w[...].reshape(9 * chans, 12 * chans)
@@ -279,7 +287,7 @@
         return call(copies_kernel, shape(copies, *parts.shape[1:], dtype=wide), 1)(parts)
 
     def by_row(cells):
-        return jnp.pad(cells.transpose(2, 0, 1), ((0, 0), (0, 0), (0, LANES - width)))
+        return cells.transpose(0, 2, 1)
 
     cells = rows * width
     dense = call(pack_kernel, shape(chan_dev, cells), 1)(by_row(grad_out))
@@ -291,9 +299,9 @@
     right = lax.ppermute(edges, "space", [(i + 1, i) for i in range(spaces - 1)])
 
     code = (2 * layer + lax.axis_index("space") % NCORE)[None]
-    own = pl.pallas_call(
+    own, token = pl.pallas_call(
         filters_kernel,
-        out_shape=shape(3, 4 * chan_dev, 9 * chan_dev),
+        out_shape=(shape(3, 4 * chan_dev, 9 * chan_dev), shape(8, LANES, dtype=wide)),
         grid_spec=pltpu.PrefetchScalarGridSpec(
             num_scalar_prefetch=1,
             grid=(1,),
@@ -301,7 +309,10 @@
                 pl.BlockSpec((9, chan_dev, 12 * chan_dev), lambda i, at, j=j: (0, window_block(j, at[0]), 0))
                 for j in range(4)
             ],
-            out_specs=pl.BlockSpec((3, 4 * chan_dev, 9 * chan_dev), lambda i, at: (0, 0, 0)),
+            out_specs=(
+                pl.BlockSpec((3, 4 * chan_dev, 9 * chan_dev), lambda i, at: (0, 0, 0)),
+                pl.BlockSpec((8, LANES), lambda i, at: (0, 0)),
+            ),
         ),
     )(code, filters, filters, filters, filters)
 
@@ -315,7 +326,7 @@
         ),
         9,
         1,
-    )(third, *grads, sources[3], sources[2], sources[0], sources[1], own)
+    )(third, *grads, sources[3], sources[2], sources[0], sources[1], token)
     parts, borders = call(
         weights_kernel,
         (shape(8, 3 * chan_dev, LANES, dtype=wide), shape(3, 9 * chan_dev, LANES)),

time: 103 us -> 103 us (level)
    unnamed x8 -> x12, local copies, waits for them, and re-layouts: 3.63 us -> 3.95 us
  transfers between devices with their start and end apart: 14 -> 14, of which waited for: 5 -> 5; matrix products, arithmetic and copies ran while one was open for 1% -> 0% of each run, Pallas kernels for 8% -> 8%
where the time goes in v8:
time: 103 us; the launch traced here: 102 us
  starting transfers between devices  72.8 us (71%)
  Pallas kernels  12.9 us (13%)
  waiting for transfers between devices  11.4 us (11%)
  local copies, waits for them, and re-layouts  3.95 us (4%)
    ppermute x7, starting transfers between devices, move(): lax.ppermute(cells, 'chan', [(i, (i + step) % chans) for i in range(chans)])  35.7 us
    all_to_all x3, starting transfers between devices, exchange(): lax.all_to_all(parts, 'space', 0, 0, axis_index_groups=groups, tiled=True)  21 us
    all_to_all x3, waiting for transfers between devices, exchange(): lax.all_to_all(parts, 'space', 0, 0, axis_index_groups=groups, tiled=True)  8.18 us
    ppermute x1, starting transfers between devices, per_device(): left = lax.ppermute(edges, 'space', [(i, i + 1) for i in range(spaces - 1)])  7.77 us
    unnamed x12, local copies, waits for them, and re-layouts  3.95 us
    ppermute x1, starting transfers between devices, per_device(): lax.ppermute(blocks[3], ('space', 'chan'), apart)  3.2 us
    ppermute x1, starting transfers between devices, per_device(): piece = lax.ppermute(piece, ('space', 'chan'), home)  3.13 us
    pallas_call x1, Pallas kernels, per_device(): call(weights_kernel, (shape(8, 3 * chan_dev, LANES, dtype=wide), shape(3,...  2.63 us
  transfers between devices with their start and end apart: 14, of which 5 were waited for; matrix products, arithmetic and copies ran while one was open for 0% of the time, Pallas kernels for 8%

profile of v8, /device:TPU:1, one launch (start us, length us, event | category | flops | bytes accessed | tf_op | source)
XLA Modules:
  0.0 101.9 jit_solution(5367934301639929695)
XLA Ops:
  0.6 0.9 copy-done
  1.7 11.5 %collective-permute-start = (bf16[24,3072]{1,0:T(8,128)(2,1)S(1)}, bf16[24,3072]{1,0:T(8,128)(2,1)S(1)}, u32[]{:S(2)}, u32[]{:S(2)}) collective-permute-start(bf16[24,3072]{1,0:T(8,128)(2,1)S(1)} %shard_map.50.refs_1_.own_ref), channel_id=1, source_target_pairs={{0,4},{1,5},{2,6},{3,7},{4,8},{5,9},{6,10},{7,11},{8,0},{9,1},{10,... | collective-permute-start | bytes 442376 | tf_op jit(solution)/shard_map/ppermute | solution.py:281
  13.2 5.6 %collective-permute-start.1 = (bf16[24,3072]{1,0:T(8,128)(2,1)S(1)}, bf16[24,3072]{1,0:T(8,128)(2,1)S(1)}, u32[]{:S(2)}, u32[]{:S(2)}) collective-permute-start(bf16[24,3072]{1,0:T(8,128)(2,1)S(1)} %shard_map.50.refs_1_.own_ref), channel_id=1, source_target_pairs={{0,8},{1,9},{2,10},{3,11},{4,0},{5,1},{6,2},{7,3},{8,4},{9,5},{10,... | collective-permute-start | bytes 442376 | tf_op jit(solution)/shard_map/ppermute | solution.py:281
  18.8 0.9 copy-done.1
  19.9 7.3 %collective-permute-start.2 = (bf16[24,3072]{1,0:T(8,128)(2,1)S(1)}, bf16[24,3072]{1,0:T(8,128)(2,1)S(1)}, u32[]{:S(2)}, u32[]{:S(2)}) collective-permute-start(bf16[24,3072]{1,0:T(8,128)(2,1)S(1)} %shard_map.51.refs_6_), channel_id=1, source_target_pairs={{0,10},{1,11},{2,0},{3,1},{4,2},{5,3},{6,4},{7,5},{8,6},{9,7},{10,... | collective-permute-start | bytes 442376 | tf_op jit(solution)/shard_map/ppermute | solution.py:281
  27.2 2.2 %collective-permute-start.3 = (bf16[24,3072]{1,0:T(8,128)(2,1)S(1)}, bf16[24,3072]{1,0:T(8,128)(2,1)S(1)}, u32[]{:S(2)}, u32[]{:S(2)}) collective-permute-start(bf16[24,3072]{1,0:T(8,128)(2,1)S(1)} %shard_map.51.refs_6_), channel_id=1, source_target_pairs={{0,11},{1,0},{2,1},{3,2},{4,3},{5,4},{6,5},{7,6},{8,7},{9,8},{10,9... | collective-permute-start | bytes 442376 | tf_op jit(solution)/shard_map/ppermute | solution.py:281
  29.4 3.1 %collective-permute-start.4 = (bf16[24,3072]{1,0:T(8,128)(2,1)S(1)}, bf16[24,3072]{1,0:T(8,128)(2,1)S(1)}, u32[]{:S(2)}, u32[]{:S(2)}) collective-permute-start(bf16[24,3072]{1,0:T(8,128)(2,1)S(1)} %shard_map.51.refs_6_), channel_id=1, source_target_pairs={{0,1},{1,2},{2,3},{3,4},{4,5},{5,6},{6,7},{7,8},{8,9},{9,10},{10,1... | collective-permute-start | bytes 442376 | tf_op jit(solution)/shard_map/ppermute | solution.py:281
  32.9 7.8 %collective-permute-start.5 = (bf16[72,128]{1,0:T(8,128)(2,1)S(1)}, bf16[72,128]{1,0:T(8,128)(2,1)S(1)}, u32[]{:S(2)}, u32[]{:S(2)}) collective-permute-start(bf16[72,128]{1,0:T(8,128)(2,1)S(1)} %shard_map.54), channel_id=1, source_target_pairs={{0,12},{12,24},{24,36},{36,48},{48,60},{60,72},{72,84},{84,96},{96... | collective-permute-start | bytes 55304 | tf_op jit(solution)/shard_map/ppermute | solution.py:298
  40.7 1.9 %collective-permute-start.6 = (bf16[72,128]{1,0:T(8,128)(2,1)S(1)}, bf16[72,128]{1,0:T(8,128)(2,1)S(1)}, u32[]{:S(2)}, u32[]{:S(2)}) collective-permute-start(bf16[72,128]{1,0:T(8,128)(2,1)S(1)} %shard_map.54), channel_id=1, source_target_pairs={{12,0},{24,12},{36,24},{48,36},{60,48},{72,60},{84,72},{96,84},{10... | collective-permute-start | bytes 55304 | tf_op jit(solution)/shard_map/ppermute | solution.py:299
  42.6 2.2 %shard_map.52 = (bf16[3,96,216]{2,1,0:T(8,128)(2,1)}, f32[8,128]{1,0:T(8,128)}) custom-call(s32[1]{0:T(128)} %bitcast.3.code_ref, bf16[9,288,288]{2,1,0:T(8,128)(2,1)} %w3.1, bf16[9,288,288]{2,1,0:T(8,128)(2,1)} %w3.1, bf16[9,288,288]{2,1,0:T(8,128)(2,1)} %w3.1, bf16[9,288,288]{2,1,0:T(8,128)(2,1)} %w3.1), custom_call_target="tpu_custom_call" | custom-call | tf_op jit(solution)/shard_map/pallas_call | solution.py:302
  44.9 0.7 copy-done.3
  45.6 1.8 %shard_map.53 = (bf16[216,4608]{1,0:T(8,128)(2,1)S(1)}, bf16[96,4096]{1,0:T(8,128)(2,1)S(1)}, bf16[96,128]{1,0:T(8,128)(2,1)S(1)}) custom-call(s32[1]{0:T(128)} %bitcast.third_ref, bf16[24,3072]{1,0:T(8,128)(2,1)S(1)} %collective-permute-done.refs_0_.near_ref, bf16[24,3072]{1,0:T(8,128)(2,1)S(1)} %shard_map.50.refs_1_.own_ref, ...), custom_call_target="tpu_custom_call" | custom-call | tf_op jit(solution)/shard_map/pallas_call | solution.py:320
  47.4 2.6 %shard_map.55 = (f32[8,72,128]{2,1,0:T(8,128)}, bf16[3,216,128]{2,1,0:T(8,128)(2,1)S(1)}) custom-call(s32[1]{0:T(128)} %bitcast.third_ref, bf16[216,4608]{1,0:T(8,128)(2,1)S(1)} %get-tuple-element.19.shifted_ref, bf16[96,4096]{1,0:T(8,128)(2,1)S(1)} %get-tuple-element.20.window_ref, bf16[96,128]{1,0:T(8,128)(2,1)S(1)} %get-tuple-element.21.ends_ref, ...), custom_call_target="tpu_custom_call" | custom-call | tf_op jit(solution)/shard_map/pallas_call | solution.py:330
  50.1 6.9 %all-to-all-start = ((f32[8,72,128]{2,1,0:T(8,128)}), f32[8,72,128]{2,1,0:T(8,128)S(1)}, u32[]{:S(2)}, u32[]{:S(2)}) async-start(f32[8,72,128]{2,1,0:T(8,128)} %get-tuple-element.22), calls=%async_computation | async-start | bytes 589824 | tf_op jit(solution)/shard_map/all_to_all | solution.py:284
  57.0 1.8 %shard_map.57 = (f32[24,3072]{1,0:T(8,128)S(1)}, f32[24,3072]{1,0:T(8,128)S(1)}, f32[24,3072]{1,0:T(8,128)S(1)}, f32[24,3072]{1,0:T(8,128)S(1)}) custom-call(bf16[216,4608]{1,0:T(8,128)(2,1)S(1)} %get-tuple-element.19.shifted_ref, bf16[3,96,216]{2,1,0:T(8,128)(2,1)S(1)} %copy-done.2, bf16[3,216,128]{2,1,0:T(8,128)(2,1)S(1)} %get-tuple-element.24.borders_ref), custom_call_target="tpu_custom_call" | custom-call | tf_op jit(solution)/shard_map/pallas_call | solution.py:336
  58.9 0.7 copy-done.4
  59.6 0.7 copy-done.5
  60.3 3.5 %all-to-all-done.in_ref = f32[8,72,128]{2,1,0:T(8,128)S(1)} async-done(((f32[8,72,128]{2,1,0:T(8,128)}), f32[8,72,128]{2,1,0:T(8,128)S(1)}, u32[]{:S(2)}, u32[]{:S(2)}) %all-to-all-start) | async-done | bytes 294944 | tf_op jit(solution)/shard_map/all_to_all | solution.py:284
  63.8 3.1 %collective-permute-start.10 = (f32[1,72,128]{2,1,0:T(8,128)S(1)}, f32[1,72,128]{2,1,0:T(8,128)S(1)}, u32[]{:S(2)}, u32[]{:S(2)}) collective-permute-start(f32[1,72,128]{2,1,0:T(8,128)S(1)} %shard_map.56), channel_id=1, source_target_pairs={{0,11},{1,0},{2,1},{3,2},{4,3},{5,4},{6,5},{7,6},{8,7},{9,8},{10,9... | collective-permute-start | bytes 110600 | tf_op jit(solution)/shard_map/ppermute | solution.py:347
  67.0 1.6 %collective-permute-done.10.in_ref = f32[1,72,128]{2,1,0:T(8,128)S(1)} collective-permute-done((f32[1,72,128]{2,1,0:T(8,128)S(1)}, f32[1,72,128]{2,1,0:T(8,128)S(1)}, u32[]{:S(2)}, u32[]{:S(2)}) %collective-permute-start.10) | collective-permute-done | bytes 36896 | tf_op jit(solution)/shard_map/ppermute | solution.py:347
  68.5 0.7 shard_map.59
  69.3 5.9 %all-to-all-start.1 = ((f32[8,72,128]{2,1,0:T(8,128)}), f32[8,72,128]{2,1,0:T(8,128)S(1)}, u32[]{:S(2)}, u32[]{:S(2)}) async-start(f32[8,72,128]{2,1,0:T(8,128)} %shard_map.59), calls=%async_computation.1 | async-start | bytes 589824 | tf_op jit(solution)/shard_map/all_to_all | solution.py:284
  75.2 3.2 %collective-permute-start.7 = (f32[24,3072]{1,0:T(8,128)}, f32[24,3072]{1,0:T(8,128)S(1)}, u32[]{:S(2)}, u32[]{:S(2)}) collective-permute-start(f32[24,3072]{1,0:T(8,128)} %copy-done.5), channel_id=1, source_target_pairs={{0,2},{1,3},{2,4},{3,5},{4,6},{5,7},{6,8},{7,9},{8,10},{9,11},{10,... | collective-permute-start | bytes 884744 | tf_op jit(solution)/shard_map/ppermute | solution.py:354
  78.4 3.0 %collective-permute-start.8 = (f32[24,3072]{1,0:T(8,128)}, f32[24,3072]{1,0:T(8,128)S(1)}, u32[]{:S(2)}, u32[]{:S(2)}) collective-permute-start(f32[24,3072]{1,0:T(8,128)} %copy-done.4), channel_id=1, source_target_pairs={{0,11},{1,0},{2,1},{3,2},{4,3},{5,4},{6,5},{7,6},{8,7},{9,8},{10,9... | collective-permute-start | bytes 884744 | tf_op jit(solution)/shard_map/ppermute | solution.py:281
  81.5 3.1 %collective-permute-start.9 = (f32[24,3072]{1,0:T(8,128)S(1)}, f32[24,3072]{1,0:T(8,128)S(1)}, u32[]{:S(2)}, u32[]{:S(2)}) collective-permute-start(f32[24,3072]{1,0:T(8,128)S(1)} %get-tuple-element.32), channel_id=1, source_target_pairs={{0,1},{1,2},{2,3},{3,4},{4,5},{5,6},{6,7},{7,8},{8,9},{9,10},{10,1... | collective-permute-start | bytes 884744 | tf_op jit(solution)/shard_map/ppermute | solution.py:281
  84.6 0.6 all-to-all-done.1.in_ref
  85.1 0.7 shard_map.60
  85.9 8.2 %all-to-all-start.2 = ((f32[8,72,128]{2,1,0:T(8,128)}), f32[8,72,128]{2,1,0:T(8,128)S(1)}, u32[]{:S(2)}, u32[]{:S(2)}) async-start(f32[8,72,128]{2,1,0:T(8,128)} %shard_map.60), calls=%async_computation.2 | async-start | bytes 589824 | tf_op jit(solution)/shard_map/all_to_all | solution.py:284
  94.0 1.6 %collective-permute-done.9.d_ref = f32[24,3072]{1,0:T(8,128)S(1)} collective-permute-done((f32[24,3072]{1,0:T(8,128)S(1)}, f32[24,3072]{1,0:T(8,128)S(1)}, u32[]{:S(2)}, u32[]{:S(2)}) %collective-permute-start.9) | collective-permute-done | bytes 294944 | tf_op jit(solution)/shard_map/ppermute | solution.py:281
  95.7 1.1 %shard_map.58 = f32[24,32,96]{2,1,0:T(8,128)} custom-call(f32[24,3072]{1,0:T(8,128)S(1)} %get-tuple-element.29.a_ref, f32[24,3072]{1,0:T(8,128)S(1)} %collective-permute-done.7.b_ref, f32[24,3072]{1,0:T(8,128)S(1)} %collective-permute-done.8.c_ref, f32[24,3072]{1,0:T(8,128)S(1)} %collective-permute-done.9.d_ref), custom_call_target="tpu_custom_call" | custom-call | tf_op jit(solution)/shard_map/pallas_call | solution.py:366
  96.8 4.1 %all-to-all-done.2.whole_ref = f32[8,72,128]{2,1,0:T(8,128)S(1)} async-done(((f32[8,72,128]{2,1,0:T(8,128)}), f32[8,72,128]{2,1,0:T(8,128)S(1)}, u32[]{:S(2)}, u32[]{:S(2)}) %all-to-all-start.2) | async-done | bytes 294944 | tf_op jit(solution)/shard_map/all_to_all | solution.py:284
  100.9 1.1 %shard_map.61 = f32[9,24,288]{2,1,0:T(8,128)} custom-call(s32[1]{0:T(128)} %bitcast.5.layer_ref, f32[8,72,128]{2,1,0:T(8,128)S(1)} %all-to-all-done.2.whole_ref), custom_call_target="tpu_custom_call" | custom-call | tf_op jit(solution)/shard_map/pallas_call | solution.py:360
  (20 shorter events, 0.8 us)
Async XLA Ops:
  0.6 0.9 copy-start
  1.7 30.7 %collective-permute-start = (bf16[24,3072]{1,0:T(8,128)(2,1)S(1)}, bf16[24,3072]{1,0:T(8,128)(2,1)S(1)}, u32[]{:S(2)}, u32[]{:S(2)}) collective-permute-start(bf16[24,3072]{1,0:T(8,128)(2,1)S(1)} %shard_map.50.refs_1_.own_ref), channel_id=1, source_target_pairs={{0,4},{1,5},{2,6},{3,7},{4,8},{5,9},{6,10},{7,11},{8,0},{9,1},{10,... | collective-permute-start | bytes 442376 | tf_op jit(solution)/shard_map/ppermute | solution.py:281
  13.2 19.3 %collective-permute-start.1 = (bf16[24,3072]{1,0:T(8,128)(2,1)S(1)}, bf16[24,3072]{1,0:T(8,128)(2,1)S(1)}, u32[]{:S(2)}, u32[]{:S(2)}) collective-permute-start(bf16[24,3072]{1,0:T(8,128)(2,1)S(1)} %shard_map.50.refs_1_.own_ref), channel_id=1, source_target_pairs={{0,8},{1,9},{2,10},{3,11},{4,0},{5,1},{6,2},{7,3},{8,4},{9,5},{10,... | collective-permute-start | bytes 442376 | tf_op jit(solution)/shard_map/ppermute | solution.py:281
  18.8 0.9 copy-start.1
  19.9 25.0 %collective-permute-start.2 = (bf16[24,3072]{1,0:T(8,128)(2,1)S(1)}, bf16[24,3072]{1,0:T(8,128)(2,1)S(1)}, u32[]{:S(2)}, u32[]{:S(2)}) collective-permute-start(bf16[24,3072]{1,0:T(8,128)(2,1)S(1)} %shard_map.51.refs_6_), channel_id=1, source_target_pairs={{0,10},{1,11},{2,0},{3,1},{4,2},{5,3},{6,4},{7,5},{8,6},{9,7},{10,... | collective-permute-start | bytes 442376 | tf_op jit(solution)/shard_map/ppermute | solution.py:281
  27.2 17.7 %collective-permute-start.3 = (bf16[24,3072]{1,0:T(8,128)(2,1)S(1)}, bf16[24,3072]{1,0:T(8,128)(2,1)S(1)}, u32[]{:S(2)}, u32[]{:S(2)}) collective-permute-start(bf16[24,3072]{1,0:T(8,128)(2,1)S(1)} %shard_map.51.refs_6_), channel_id=1, source_target_pairs={{0,11},{1,0},{2,1},{3,2},{4,3},{5,4},{6,5},{7,6},{8,7},{9,8},{10,9... | collective-permute-start | bytes 442376 | tf_op jit(solution)/shard_map/ppermute | solution.py:281
  29.4 15.5 %collective-permute-start.4 = (bf16[24,3072]{1,0:T(8,128)(2,1)S(1)}, bf16[24,3072]{1,0:T(8,128)(2,1)S(1)}, u32[]{:S(2)}, u32[]{:S(2)}) collective-permute-start(bf16[24,3072]{1,0:T(8,128)(2,1)S(1)} %shard_map.51.refs_6_), channel_id=1, source_target_pairs={{0,1},{1,2},{2,3},{3,4},{4,5},{5,6},{6,7},{7,8},{8,9},{9,10},{10,1... | collective-permute-start | bytes 442376 | tf_op jit(solution)/shard_map/ppermute | solution.py:281
  32.9 14.5 %collective-permute-start.5 = (bf16[72,128]{1,0:T(8,128)(2,1)S(1)}, bf16[72,128]{1,0:T(8,128)(2,1)S(1)}, u32[]{:S(2)}, u32[]{:S(2)}) collective-permute-start(bf16[72,128]{1,0:T(8,128)(2,1)S(1)} %shard_map.54), channel_id=1, source_target_pairs={{0,12},{12,24},{24,36},{36,48},{48,60},{60,72},{72,84},{84,96},{96... | collective-permute-start | bytes 55304 | tf_op jit(solution)/shard_map/ppermute | solution.py:298
  40.7 6.8 %collective-permute-start.6 = (bf16[72,128]{1,0:T(8,128)(2,1)S(1)}, bf16[72,128]{1,0:T(8,128)(2,1)S(1)}, u32[]{:S(2)}, u32[]{:S(2)}) collective-permute-start(bf16[72,128]{1,0:T(8,128)(2,1)S(1)} %shard_map.54), channel_id=1, source_target_pairs={{12,0},{24,12},{36,24},{48,36},{60,48},{72,60},{84,72},{96,84},{10... | collective-permute-start | bytes 55304 | tf_op jit(solution)/shard_map/ppermute | solution.py:299
  44.9 0.7 copy-start.3
  45.6 11.4 %copy-start.2 = (bf16[3,96,216]{2,1,0:T(8,128)(2,1)S(1)}, bf16[3,96,216]{2,1,0:T(8,128)(2,1)}, u32[]{:S(2)}) copy-start(bf16[3,96,216]{2,1,0:T(8,128)(2,1)} %get-tuple-element.23.filters_ref) | copy-start | bytes 373252
  50.1 13.8 %all-to-all-start = ((f32[8,72,128]{2,1,0:T(8,128)}), f32[8,72,128]{2,1,0:T(8,128)S(1)}, u32[]{:S(2)}, u32[]{:S(2)}) async-start(f32[8,72,128]{2,1,0:T(8,128)} %get-tuple-element.22), calls=%async_computation | async-start | bytes 589824 | tf_op jit(solution)/shard_map/all_to_all | solution.py:284
  58.9 0.7 copy-start.4
  59.6 0.7 copy-start.5
  63.8 4.7 %collective-permute-start.10 = (f32[1,72,128]{2,1,0:T(8,128)S(1)}, f32[1,72,128]{2,1,0:T(8,128)S(1)}, u32[]{:S(2)}, u32[]{:S(2)}) collective-permute-start(f32[1,72,128]{2,1,0:T(8,128)S(1)} %shard_map.56), channel_id=1, source_target_pairs={{0,11},{1,0},{2,1},{3,2},{4,3},{5,4},{6,5},{7,6},{8,7},{9,8},{10,9... | collective-permute-start | bytes 110600 | tf_op jit(solution)/shard_map/ppermute | solution.py:347
  69.3 15.9 %all-to-all-start.1 = ((f32[8,72,128]{2,1,0:T(8,128)}), f32[8,72,128]{2,1,0:T(8,128)S(1)}, u32[]{:S(2)}, u32[]{:S(2)}) async-start(f32[8,72,128]{2,1,0:T(8,128)} %shard_map.59), calls=%async_computation.1 | async-start | bytes 589824 | tf_op jit(solution)/shard_map/all_to_all | solution.py:284
  75.2 18.8 %collective-permute-start.7 = (f32[24,3072]{1,0:T(8,128)}, f32[24,3072]{1,0:T(8,128)S(1)}, u32[]{:S(2)}, u32[]{:S(2)}) collective-permute-start(f32[24,3072]{1,0:T(8,128)} %copy-done.5), channel_id=1, source_target_pairs={{0,2},{1,3},{2,4},{3,5},{4,6},{5,7},{6,8},{7,9},{8,10},{9,11},{10,... | collective-permute-start | bytes 884744 | tf_op jit(solution)/shard_map/ppermute | solution.py:354
  78.4 15.6 %collective-permute-start.8 = (f32[24,3072]{1,0:T(8,128)}, f32[24,3072]{1,0:T(8,128)S(1)}, u32[]{:S(2)}, u32[]{:S(2)}) collective-permute-start(f32[24,3072]{1,0:T(8,128)} %copy-done.4), channel_id=1, source_target_pairs={{0,11},{1,0},{2,1},{3,2},{4,3},{5,4},{6,5},{7,6},{8,7},{9,8},{10,9... | collective-permute-start | bytes 884744 | tf_op jit(solution)/shard_map/ppermute | solution.py:281
  81.5 14.2 %collective-permute-start.9 = (f32[24,3072]{1,0:T(8,128)S(1)}, f32[24,3072]{1,0:T(8,128)S(1)}, u32[]{:S(2)}, u32[]{:S(2)}) collective-permute-start(f32[24,3072]{1,0:T(8,128)S(1)} %get-tuple-element.32), channel_id=1, source_target_pairs={{0,1},{1,2},{2,3},{3,4},{4,5},{5,6},{6,7},{7,8},{8,9},{9,10},{10,1... | collective-permute-start | bytes 884744 | tf_op jit(solution)/shard_map/ppermute | solution.py:281
  85.9 15.0 %all-to-all-start.2 = ((f32[8,72,128]{2,1,0:T(8,128)}), f32[8,72,128]{2,1,0:T(8,128)S(1)}, u32[]{:S(2)}, u32[]{:S(2)}) async-start(f32[8,72,128]{2,1,0:T(8,128)} %shard_map.60), calls=%async_computation.2 | async-start | bytes 589824 | tf_op jit(solution)/shard_map/all_to_all | solution.py:284

commit v9 on v7

--- a/solution.py
+++ b/solution.py
@@ -29,20 +29,32 @@
 
 
 def pack_kernel(cells_ref, dense_ref):
-    for start in range(0, cells_ref.shape[0], 4):
-        store_dense(dense_ref, start, [cells_ref[start + i].astype(jnp.float32) for i in range(4)])
-
-
-def edges_kernel(near_ref, own_ref, far_ref, edges_ref):
-    refs = (near_ref, own_ref, far_ref)
-    rows = near_ref.shape[1] // WIDTH
-    lane = lane_index(3 * near_ref.shape[0])
+    chans, rows, width = cells_ref.shape
+    blank = jnp.zeros((chans, 8, LANES - width), jnp.float32)
+    for start in range(0, rows, 8):
+        block = cells_ref[:, start : start + 8, :].astype(jnp.float32)
+        block = jnp.swapaxes(jnp.concatenate([block, blank], axis=2), 0, 1)
+        for half in (0, 4):
+            store_dense(dense_ref, start + half, [block[half + i] for i in range(4)])
+
+
+def sorted_blocks(code, first, own, second):
+    even = code % 2 == 0
+    return jnp.where(even, first, second), own, jnp.where(even, second, first)
+
+
+def edges_kernel(code_ref, first_ref, own_ref, second_ref, edges_ref):
+    refs = (first_ref, own_ref, second_ref)
+    code = code_ref[0]
+    rows = own_ref.shape[1] // WIDTH
+    lane = lane_index(3 * own_ref.shape[0])
     packed = jnp.zeros(edges_ref.shape, jnp.float32)
     for r in range(rows):
         for column, to in ((TAIL, 4 * r), (0, (4 * r + TAIL) % LANES)):
             tile, at = divmod(r * WIDTH + column, LANES)
             cut = slice(tile * LANES, (tile + 1) * LANES)
-            block = jnp.concatenate([ref[:, cut].astype(jnp.float32) for ref in refs], axis=0)
+            block = [ref[:, cut].astype(jnp.float32) for ref in refs]
+            block = jnp.concatenate(sorted_blocks(code, *block), axis=0)
             turn = (to - at) % LANES
             block = pltpu.roll(block, turn, 1) if turn else block
             packed = jnp.where((lane >= to) & (lane < to + 2), block, packed)
@@ -97,7 +109,8 @@
         own_ref[b] = jnp.concatenate(taps, axis=1).astype(own_ref.dtype)
 
 
-def ordered(third, near, own, far):
+def ordered(code, near, own, far):
+    third = code // 8
     orders = ((own, far, near), (near, own, far), (far, near, own))
     return jnp.concatenate(
         [jnp.where(third == 0, a, jnp.where(third == 1, b, c)) for a, b, c in zip(*orders)],
@@ -105,12 +118,12 @@
     )
 
 
-def build_kernel(third_ref, *refs):
-    g_refs, (x3, x2, x0, x1), (shifted_ref, window_ref, ends_ref) = refs[:3], refs[3:7], refs[8:]
+def build_kernel(code_ref, *refs):
+    g_refs, (x3, x2, x0, x1), (shifted_ref, window_ref, ends_ref) = refs[:3], refs[3:7], refs[7:]
     x_refs = (x0, x1, x2, x3)
     chans = g_refs[0].shape[0]
     rows = g_refs[0].shape[1] // WIDTH
-    third = third_ref[0]
+    code = code_ref[0]
     kind = shifted_ref.dtype
     blank = jnp.zeros((9 * chans, 2 * LANES), kind)
     shifted_ref[:, : 2 * LANES] = blank
@@ -119,7 +132,8 @@
     ends = jnp.zeros((4 * chans, LANES), jnp.float32)
     for start in range(0, rows, 4):
         cuts = [pl.ds((3 * start // 4 + i) * LANES, LANES) for i in range(3)]
-        tiles = [ordered(third, *[g[:, cut].astype(jnp.float32) for g in g_refs]) for cut in cuts]
+        tiles = [[g[:, cut].astype(jnp.float32) for g in g_refs] for cut in cuts]
+        tiles = [ordered(code, *sorted_blocks(code, *blocks)) for blocks in tiles]
         for i, row in enumerate(load_rows(tiles, 2)):
             row = jnp.where((lane >= 2) & (lane < WIDTH + 2), row, 0.0)
             taps = [pltpu.roll(row, LANES - 4, 1), pltpu.roll(row, LANES - 2, 1), row]
@@ -142,7 +156,7 @@
 
 
 def weights_kernel(
-    third_ref, shifted_ref, window_ref, ends_ref, left_ref, right_ref, parts_ref, borders_ref
+    code_ref, shifted_ref, window_ref, ends_ref, left_ref, right_ref, parts_ref, borders_ref
 ):
     chans = left_ref.shape[0] // 3
     rows = window_ref.shape[1] // LANES
@@ -150,7 +164,7 @@
     at_head = lane % 4 < 2
     row_of = jnp.where(at_head, lane, (lane + LANES - TAIL) % LANES) // 4
     sides = [
-        ordered(third_ref[0], *[ref[m * chans : (m + 1) * chans].astype(jnp.float32) for m in range(3)])
+        ordered(code_ref[0], *[ref[m * chans : (m + 1) * chans].astype(jnp.float32) for m in range(3)])
         for ref in (left_ref, right_ref)
     ]
     contract = (((1,), (1,)), ((), ()))
@@ -279,18 +293,27 @@
         return call(copies_kernel, shape(copies, *parts.shape[1:], dtype=wide), 1)(parts)
 
     def by_row(cells):
-        return jnp.pad(cells.transpose(2, 0, 1), ((0, 0), (0, 0), (0, LANES - width)))
+        return cells.transpose(0, 2, 1)
 
     cells = rows * width
+    code = (2 * layer + lax.axis_index("space") % NCORE)[None]
     dense = call(pack_kernel, shape(chan_dev, cells), 1)(by_row(grad_out))
-    grads = [move(dense, 4), dense, move(dense, -4)]
     source = call(pack_kernel, shape(chan_dev, cells), 1)(by_row(field))
+
+    def apart(cells, even, odd):
+        pairs = [
+            (s * chans + c, s * chans + (c + (odd if s % NCORE else even)) % chans)
+            for s in range(spaces)
+            for c in range(chans)
+        ]
+        return lax.ppermute(cells, ("space", "chan"), pairs)
+
+    grads = [apart(dense, 4, -4), dense, apart(dense, -4, 4)]
     sources = [move(source, 1), source, move(source, -1), move(source, -2)]
-    edges = call(edges_kernel, shape(3 * chan_dev, LANES), 3)(*grads)
+    edges = call(edges_kernel, shape(3 * chan_dev, LANES), 4, 1)(code, *grads)
     left = lax.ppermute(edges, "space", [(i, i + 1) for i in range(spaces - 1)])
     right = lax.ppermute(edges, "space", [(i + 1, i) for i in range(spaces - 1)])
 
-    code = (2 * layer + lax.axis_index("space") % NCORE)[None]
     own = pl.pallas_call(
         filters_kernel,
         out_shape=shape(3, 4 * chan_dev, 9 * chan_dev),
@@ -305,7 +328,6 @@
         ),
     )(code, filters, filters, filters, filters)
 
-    third = (layer // 4)[None]
     shifted, window, ends = call(
         build_kernel,
         (
@@ -313,15 +335,15 @@
             shape(4 * chan_dev, rows * LANES),
             shape(4 * chan_dev, LANES),
         ),
-        9,
+        8,
         1,
-    )(third, *grads, sources[3], sources[2], sources[0], sources[1], own)
+    )(code, *grads, sources[3], sources[2], sources[0], sources[1])
     parts, borders = call(
         weights_kernel,
         (shape(8, 3 * chan_dev, LANES, dtype=wide), shape(3, 9 * chan_dev, LANES)),
         6,
         1,
-    )(third, shifted, window, ends, left, right)
+    )(code, shifted, window, ends, left, right)
     blocks = call(inputs_kernel, (shape(chan_dev, cells, dtype=wide),) * 4, 3)(
         shifted, own, borders
     )
@@ -334,16 +356,7 @@
         for c in range(chans)
     ]
     piece = lax.ppermute(piece, ("space", "chan"), home)
-    apart = [
-        (s * chans + c, s * chans + (c + (-2 if s % NCORE else 2)) % chans)
-        for s in range(spaces)
-        for c in range(chans)
-    ]
-    others = [
-        lax.ppermute(blocks[3], ("space", "chan"), apart),
-        move(blocks[0], -1),
-        move(blocks[2], 1),
-    ]
+    others = [apart(blocks[3], 2, -2), move(blocks[0], -1), move(blocks[2], 1)]
     piece = added(exchange(added(piece, 8), along), 8)
     whole = exchange(piece, across)
     grad_filters = call(

time: 103 us -> 97.6 us (0.948)
  starting transfers between devices: 72.7 us -> 70 us
  waiting for transfers between devices: 12.1 us -> 9.7 us
    ppermute x1 -> x3, starting transfers between devices: 3.25 us -> 21.1 us  [apart(): return lax.ppermute(cells, ('space', 'chan'), pairs)]
    ppermute x7 -> x5, starting transfers between devices: 35.7 us -> 18.3 us  [move(): lax.ppermute(cells, 'chan', [(i, (i + step) % chans) for i in range(chans)])]
    all_to_all x3, waiting for transfers between devices: 8.9 us -> 6.21 us  [exchange(): lax.all_to_all(parts, 'space', 0, 0, axis_index_groups=groups, tiled=True)]
    ppermute x1, starting transfers between devices: 7.7 us -> 5.17 us  [per_device(): left = lax.ppermute(edges, 'space', [(i, i + 1) for i in range(spaces - 1)])]
    ppermute x1, waiting for transfers between devices: 0.01 us -> 1.27 us  [per_device(): lax.ppermute(edges, 'space', [(i + 1, i) for i in range(spaces - 1)])]
  transfers between devices with their start and end apart: 14 -> 14, of which waited for: 5 -> 6; matrix products, arithmetic and copies ran while one was open for 1% -> 0% of each run, Pallas kernels for 8% -> 9%
where the time goes in v9:
time: 97.6 us; the launch traced here: 96.8 us
  starting transfers between devices  70 us (72%)
  Pallas kernels  12.8 us (13%)
  waiting for transfers between devices  9.7 us (10%)
  local copies, waits for them, and re-layouts  3.46 us (4%)
    ppermute x3, starting transfers between devices, apart(): return lax.ppermute(cells, ('space', 'chan'), pairs)  21.1 us
    all_to_all x3, starting transfers between devices, exchange(): lax.all_to_all(parts, 'space', 0, 0, axis_index_groups=groups, tiled=True)  20.4 us
    ppermute x5, starting transfers between devices, move(): lax.ppermute(cells, 'chan', [(i, (i + step) % chans) for i in range(chans)])  18.3 us
    all_to_all x3, waiting for transfers between devices, exchange(): lax.all_to_all(parts, 'space', 0, 0, axis_index_groups=groups, tiled=True)  6.21 us
    ppermute x1, starting transfers between devices, per_device(): left = lax.ppermute(edges, 'space', [(i, i + 1) for i in range(spaces - 1)])  5.17 us
    unnamed x8, local copies, waits for them, and re-layouts  3.46 us
    ppermute x1, starting transfers between devices, per_device(): piece = lax.ppermute(piece, ('space', 'chan'), home)  3.08 us
    pallas_call x1, Pallas kernels, per_device(): call(weights_kernel, (shape(8, 3 * chan_dev, LANES, dtype=wide), shape(3,...  2.47 us
  transfers between devices with their start and end apart: 14, of which 6 were waited for; matrix products, arithmetic and copies ran while one was open for 0% of the time, Pallas kernels for 9%

profile of v9, /device:TPU:1, one launch (start us, length us, event | category | flops | bytes accessed | tf_op | source)
XLA Modules:
  0.0 96.8 jit_solution(18323672855089776143)
XLA Ops:
  0.6 0.9 copy-done.1
  1.7 15.1 %collective-permute-start = (bf16[24,3072]{1,0:T(8,128)(2,1)S(1)}, bf16[24,3072]{1,0:T(8,128)(2,1)S(1)}, u32[]{:S(2)}, u32[]{:S(2)}) collective-permute-start(bf16[24,3072]{1,0:T(8,128)(2,1)S(1)} %shard_map.50.refs_1_.own_ref), channel_id=1, source_target_pairs={{0,4},{1,5},{2,6},{3,7},{4,8},{5,9},{6,10},{7,11},{8,0},{9,1},{10,... | collective-permute-start | bytes 442376 | tf_op jit(solution)/shard_map/ppermute | solution.py:309
  16.8 1.9 %collective-permute-start.1 = (bf16[24,3072]{1,0:T(8,128)(2,1)S(1)}, bf16[24,3072]{1,0:T(8,128)(2,1)S(1)}, u32[]{:S(2)}, u32[]{:S(2)}) collective-permute-start(bf16[24,3072]{1,0:T(8,128)(2,1)S(1)} %shard_map.50.refs_1_.own_ref), channel_id=1, source_target_pairs={{0,8},{1,9},{2,10},{3,11},{4,0},{5,1},{6,2},{7,3},{8,4},{9,5},{10,... | collective-permute-start | bytes 442376 | tf_op jit(solution)/shard_map/ppermute | solution.py:309
  18.8 0.9 copy-done.2
  19.9 7.3 %collective-permute-start.2 = (bf16[24,3072]{1,0:T(8,128)(2,1)S(1)}, bf16[24,3072]{1,0:T(8,128)(2,1)S(1)}, u32[]{:S(2)}, u32[]{:S(2)}) collective-permute-start(bf16[24,3072]{1,0:T(8,128)(2,1)S(1)} %shard_map.51.refs_6_), channel_id=1, source_target_pairs={{0,10},{1,11},{2,0},{3,1},{4,2},{5,3},{6,4},{7,5},{8,6},{9,7},{10,... | collective-permute-start | bytes 442376 | tf_op jit(solution)/shard_map/ppermute | solution.py:287
  27.2 2.2 %collective-permute-start.3 = (bf16[24,3072]{1,0:T(8,128)(2,1)S(1)}, bf16[24,3072]{1,0:T(8,128)(2,1)S(1)}, u32[]{:S(2)}, u32[]{:S(2)}) collective-permute-start(bf16[24,3072]{1,0:T(8,128)(2,1)S(1)} %shard_map.51.refs_6_), channel_id=1, source_target_pairs={{0,11},{1,0},{2,1},{3,2},{4,3},{5,4},{6,5},{7,6},{8,7},{9,8},{10,9... | collective-permute-start | bytes 442376 | tf_op jit(solution)/shard_map/ppermute | solution.py:287
  29.4 3.1 %collective-permute-start.4 = (bf16[24,3072]{1,0:T(8,128)(2,1)S(1)}, bf16[24,3072]{1,0:T(8,128)(2,1)S(1)}, u32[]{:S(2)}, u32[]{:S(2)}) collective-permute-start(bf16[24,3072]{1,0:T(8,128)(2,1)S(1)} %shard_map.51.refs_6_), channel_id=1, source_target_pairs={{0,1},{1,2},{2,3},{3,4},{4,5},{5,6},{6,7},{7,8},{8,9},{9,10},{10,1... | collective-permute-start | bytes 442376 | tf_op jit(solution)/shard_map/ppermute | solution.py:287
  32.5 0.4 shard_map.53
  32.9 5.2 %collective-permute-start.5 = (bf16[72,128]{1,0:T(8,128)(2,1)S(1)}, bf16[72,128]{1,0:T(8,128)(2,1)S(1)}, u32[]{:S(2)}, u32[]{:S(2)}) collective-permute-start(bf16[72,128]{1,0:T(8,128)(2,1)S(1)} %shard_map.53), channel_id=1, source_target_pairs={{0,12},{12,24},{24,36},{36,48},{48,60},{60,72},{72,84},{84,96},{96... | collective-permute-start | bytes 55304 | tf_op jit(solution)/shard_map/ppermute | solution.py:314
  38.1 1.9 %collective-permute-start.6 = (bf16[72,128]{1,0:T(8,128)(2,1)S(1)}, bf16[72,128]{1,0:T(8,128)(2,1)S(1)}, u32[]{:S(2)}, u32[]{:S(2)}) collective-permute-start(bf16[72,128]{1,0:T(8,128)(2,1)S(1)} %shard_map.53), channel_id=1, source_target_pairs={{12,0},{24,12},{36,24},{48,36},{60,48},{72,60},{84,72},{96,84},{10... | collective-permute-start | bytes 55304 | tf_op jit(solution)/shard_map/ppermute | solution.py:315
  40.0 1.8 %shard_map.52 = (bf16[216,4608]{1,0:T(8,128)(2,1)S(1)}, bf16[96,4096]{1,0:T(8,128)(2,1)S(1)}, bf16[96,128]{1,0:T(8,128)(2,1)S(1)}) custom-call(s32[1]{0:T(128)} %bitcast.code_ref, bf16[24,3072]{1,0:T(8,128)(2,1)S(1)} %collective-permute-done.refs_0_.first_ref, bf16[24,3072]{1,0:T(8,128)(2,1)S(1)} %shard_map.50.refs_1_.own_ref, ...), custom_call_target="tpu_custom_call" | custom-call | tf_op jit(solution)/shard_map/pallas_call | solution.py:331
  41.9 1.3 %collective-permute-done.6.right_ref = bf16[72,128]{1,0:T(8,128)(2,1)S(1)} collective-permute-done((bf16[72,128]{1,0:T(8,128)(2,1)S(1)}, bf16[72,128]{1,0:T(8,128)(2,1)S(1)}, u32[]{:S(2)}, u32[]{:S(2)}) %collective-permute-start.6) | collective-permute-done | bytes 18464 | tf_op jit(solution)/shard_map/ppermute | solution.py:315
  43.2 2.5 %shard_map.54 = (f32[8,72,128]{2,1,0:T(8,128)}, bf16[3,216,128]{2,1,0:T(8,128)(2,1)S(1)}) custom-call(s32[1]{0:T(128)} %bitcast.code_ref, bf16[216,4608]{1,0:T(8,128)(2,1)S(1)} %get-tuple-element.16.shifted_ref, bf16[96,4096]{1,0:T(8,128)(2,1)S(1)} %get-tuple-element.17.window_ref, bf16[96,128]{1,0:T(8,128)(2,1)S(1)} %get-tuple-element.18.ends_ref, ...), custom_call_target="tpu_custom_call" | custom-call | tf_op jit(solution)/shard_map/pallas_call | solution.py:341
  45.6 6.5 %all-to-all-start = ((f32[8,72,128]{2,1,0:T(8,128)}), f32[8,72,128]{2,1,0:T(8,128)S(1)}, u32[]{:S(2)}, u32[]{:S(2)}) async-start(f32[8,72,128]{2,1,0:T(8,128)} %get-tuple-element.19), calls=%async_computation | async-start | bytes 589824 | tf_op jit(solution)/shard_map/all_to_all | solution.py:290
  52.2 2.2 %shard_map.56.filters_ref = bf16[3,96,216]{2,1,0:T(8,128)(2,1)} custom-call(s32[1]{0:T(128)} %bitcast.code_ref, bf16[9,288,288]{2,1,0:T(8,128)(2,1)} %w3.1, bf16[9,288,288]{2,1,0:T(8,128)(2,1)} %w3.1, bf16[9,288,288]{2,1,0:T(8,128)(2,1)} %w3.1, bf16[9,288,288]{2,1,0:T(8,128)(2,1)} %w3.1), custom_call_target="tpu_custom_call" | custom-call | tf_op jit(solution)/shard_map/pallas_call | solution.py:317
  54.4 0.9 copy-done
  55.3 1.8 %shard_map.57 = (f32[24,3072]{1,0:T(8,128)S(1)}, f32[24,3072]{1,0:T(8,128)S(1)}, f32[24,3072]{1,0:T(8,128)S(1)}, f32[24,3072]{1,0:T(8,128)S(1)}) custom-call(bf16[216,4608]{1,0:T(8,128)(2,1)S(1)} %get-tuple-element.16.shifted_ref, bf16[3,96,216]{2,1,0:T(8,128)(2,1)S(1)} %copy-done, bf16[3,216,128]{2,1,0:T(8,128)(2,1)S(1)} %get-tuple-element.20.borders_ref), custom_call_target="tpu_custom_call" | custom-call | tf_op jit(solution)/shard_map/pallas_call | solution.py:347
  57.1 0.7 copy-done.3
  57.8 1.1 %all-to-all-done.in_ref = f32[8,72,128]{2,1,0:T(8,128)S(1)} async-done(((f32[8,72,128]{2,1,0:T(8,128)}), f32[8,72,128]{2,1,0:T(8,128)S(1)}, u32[]{:S(2)}, u32[]{:S(2)}) %all-to-all-start) | async-done | bytes 294944 | tf_op jit(solution)/shard_map/all_to_all | solution.py:290
  59.0 3.1 %collective-permute-start.10 = (f32[1,72,128]{2,1,0:T(8,128)S(1)}, f32[1,72,128]{2,1,0:T(8,128)S(1)}, u32[]{:S(2)}, u32[]{:S(2)}) collective-permute-start(f32[1,72,128]{2,1,0:T(8,128)S(1)} %shard_map.55), channel_id=1, source_target_pairs={{0,11},{1,0},{2,1},{3,2},{4,3},{5,4},{6,5},{7,6},{8,7},{9,8},{10,9... | collective-permute-start | bytes 110600 | tf_op jit(solution)/shard_map/ppermute | solution.py:358
  62.1 1.6 %collective-permute-done.10.in_ref = f32[1,72,128]{2,1,0:T(8,128)S(1)} collective-permute-done((f32[1,72,128]{2,1,0:T(8,128)S(1)}, f32[1,72,128]{2,1,0:T(8,128)S(1)}, u32[]{:S(2)}, u32[]{:S(2)}) %collective-permute-start.10) | collective-permute-done | bytes 36896 | tf_op jit(solution)/shard_map/ppermute | solution.py:358
  63.7 0.7 shard_map.59
  64.4 5.3 %all-to-all-start.1 = ((f32[8,72,128]{2,1,0:T(8,128)}), f32[8,72,128]{2,1,0:T(8,128)S(1)}, u32[]{:S(2)}, u32[]{:S(2)}) async-start(f32[8,72,128]{2,1,0:T(8,128)} %shard_map.59), calls=%async_computation.1 | async-start | bytes 589824 | tf_op jit(solution)/shard_map/all_to_all | solution.py:290
  69.8 4.1 %collective-permute-start.7 = (f32[24,3072]{1,0:T(8,128)}, f32[24,3072]{1,0:T(8,128)S(1)}, u32[]{:S(2)}, u32[]{:S(2)}) collective-permute-start(f32[24,3072]{1,0:T(8,128)} %copy-done.3), channel_id=1, source_target_pairs={{0,2},{1,3},{2,4},{3,5},{4,6},{5,7},{6,8},{7,9},{8,10},{9,11},{10,... | collective-permute-start | bytes 884744 | tf_op jit(solution)/shard_map/ppermute | solution.py:309
  73.9 3.4 %collective-permute-start.8 = (f32[24,3072]{1,0:T(8,128)S(1)}, f32[24,3072]{1,0:T(8,128)S(1)}, u32[]{:S(2)}, u32[]{:S(2)}) collective-permute-start(f32[24,3072]{1,0:T(8,128)S(1)} %get-tuple-element.27), channel_id=1, source_target_pairs={{0,11},{1,0},{2,1},{3,2},{4,3},{5,4},{6,5},{7,6},{8,7},{9,8},{10,9... | collective-permute-start | bytes 884744 | tf_op jit(solution)/shard_map/ppermute | solution.py:287
  77.4 2.3 %collective-permute-start.9 = (f32[24,3072]{1,0:T(8,128)S(1)}, f32[24,3072]{1,0:T(8,128)S(1)}, u32[]{:S(2)}, u32[]{:S(2)}) collective-permute-start(f32[24,3072]{1,0:T(8,128)S(1)} %get-tuple-element.28), channel_id=1, source_target_pairs={{0,1},{1,2},{2,3},{3,4},{4,5},{5,6},{6,7},{7,8},{8,9},{9,10},{10,1... | collective-permute-start | bytes 884744 | tf_op jit(solution)/shard_map/ppermute | solution.py:287
  79.7 0.7 shard_map.60
  80.4 8.5 %all-to-all-start.2 = ((f32[8,72,128]{2,1,0:T(8,128)}), f32[8,72,128]{2,1,0:T(8,128)S(1)}, u32[]{:S(2)}, u32[]{:S(2)}) async-start(f32[8,72,128]{2,1,0:T(8,128)} %shard_map.60), calls=%async_computation.2 | async-start | bytes 589824 | tf_op jit(solution)/shard_map/all_to_all | solution.py:290
  89.2 0.4 collective-permute-done.9.d_ref
  89.6 1.1 %shard_map.58 = f32[24,32,96]{2,1,0:T(8,128)} custom-call(f32[24,3072]{1,0:T(8,128)S(1)} %get-tuple-element.25.a_ref, f32[24,3072]{1,0:T(8,128)S(1)} %collective-permute-done.7.b_ref, f32[24,3072]{1,0:T(8,128)S(1)} %collective-permute-done.8.c_ref, f32[24,3072]{1,0:T(8,128)S(1)} %collective-permute-done.9.d_ref), custom_call_target="tpu_custom_call" | custom-call | tf_op jit(solution)/shard_map/pallas_call | solution.py:368
  90.7 5.1 %all-to-all-done.2.whole_ref = f32[8,72,128]{2,1,0:T(8,128)S(1)} async-done(((f32[8,72,128]{2,1,0:T(8,128)}), f32[8,72,128]{2,1,0:T(8,128)S(1)}, u32[]{:S(2)}, u32[]{:S(2)}) %all-to-all-start.2) | async-done | bytes 294944 | tf_op jit(solution)/shard_map/all_to_all | solution.py:290
  95.8 1.1 %shard_map.61 = f32[9,24,288]{2,1,0:T(8,128)} custom-call(s32[1]{0:T(128)} %bitcast.4.layer_ref, f32[8,72,128]{2,1,0:T(8,128)S(1)} %all-to-all-done.2.whole_ref), custom_call_target="tpu_custom_call" | custom-call | tf_op jit(solution)/shard_map/pallas_call | solution.py:362
  (16 shorter events, 0.6 us)
Async XLA Ops:
  0.6 0.9 copy-start.1
  1.7 30.8 %collective-permute-start = (bf16[24,3072]{1,0:T(8,128)(2,1)S(1)}, bf16[24,3072]{1,0:T(8,128)(2,1)S(1)}, u32[]{:S(2)}, u32[]{:S(2)}) collective-permute-start(bf16[24,3072]{1,0:T(8,128)(2,1)S(1)} %shard_map.50.refs_1_.own_ref), channel_id=1, source_target_pairs={{0,4},{1,5},{2,6},{3,7},{4,8},{5,9},{6,10},{7,11},{8,0},{9,1},{10,... | collective-permute-start | bytes 442376 | tf_op jit(solution)/shard_map/ppermute | solution.py:309
  16.8 15.7 %collective-permute-start.1 = (bf16[24,3072]{1,0:T(8,128)(2,1)S(1)}, bf16[24,3072]{1,0:T(8,128)(2,1)S(1)}, u32[]{:S(2)}, u32[]{:S(2)}) collective-permute-start(bf16[24,3072]{1,0:T(8,128)(2,1)S(1)} %shard_map.50.refs_1_.own_ref), channel_id=1, source_target_pairs={{0,8},{1,9},{2,10},{3,11},{4,0},{5,1},{6,2},{7,3},{8,4},{9,5},{10,... | collective-permute-start | bytes 442376 | tf_op jit(solution)/shard_map/ppermute | solution.py:309
  18.8 0.9 copy-start.2
  19.9 20.1 %collective-permute-start.2 = (bf16[24,3072]{1,0:T(8,128)(2,1)S(1)}, bf16[24,3072]{1,0:T(8,128)(2,1)S(1)}, u32[]{:S(2)}, u32[]{:S(2)}) collective-permute-start(bf16[24,3072]{1,0:T(8,128)(2,1)S(1)} %shard_map.51.refs_6_), channel_id=1, source_target_pairs={{0,10},{1,11},{2,0},{3,1},{4,2},{5,3},{6,4},{7,5},{8,6},{9,7},{10,... | collective-permute-start | bytes 442376 | tf_op jit(solution)/shard_map/ppermute | solution.py:287
  27.2 12.9 %collective-permute-start.3 = (bf16[24,3072]{1,0:T(8,128)(2,1)S(1)}, bf16[24,3072]{1,0:T(8,128)(2,1)S(1)}, u32[]{:S(2)}, u32[]{:S(2)}) collective-permute-start(bf16[24,3072]{1,0:T(8,128)(2,1)S(1)} %shard_map.51.refs_6_), channel_id=1, source_target_pairs={{0,11},{1,0},{2,1},{3,2},{4,3},{5,4},{6,5},{7,6},{8,7},{9,8},{10,9... | collective-permute-start | bytes 442376 | tf_op jit(solution)/shard_map/ppermute | solution.py:287
  29.4 10.7 %collective-permute-start.4 = (bf16[24,3072]{1,0:T(8,128)(2,1)S(1)}, bf16[24,3072]{1,0:T(8,128)(2,1)S(1)}, u32[]{:S(2)}, u32[]{:S(2)}) collective-permute-start(bf16[24,3072]{1,0:T(8,128)(2,1)S(1)} %shard_map.51.refs_6_), channel_id=1, source_target_pairs={{0,1},{1,2},{2,3},{3,4},{4,5},{5,6},{6,7},{7,8},{8,9},{9,10},{10,1... | collective-permute-start | bytes 442376 | tf_op jit(solution)/shard_map/ppermute | solution.py:287
  32.9 9.0 %collective-permute-start.5 = (bf16[72,128]{1,0:T(8,128)(2,1)S(1)}, bf16[72,128]{1,0:T(8,128)(2,1)S(1)}, u32[]{:S(2)}, u32[]{:S(2)}) collective-permute-start(bf16[72,128]{1,0:T(8,128)(2,1)S(1)} %shard_map.53), channel_id=1, source_target_pairs={{0,12},{12,24},{24,36},{36,48},{48,60},{60,72},{72,84},{84,96},{96... | collective-permute-start | bytes 55304 | tf_op jit(solution)/shard_map/ppermute | solution.py:314
  38.1 5.1 %collective-permute-start.6 = (bf16[72,128]{1,0:T(8,128)(2,1)S(1)}, bf16[72,128]{1,0:T(8,128)(2,1)S(1)}, u32[]{:S(2)}, u32[]{:S(2)}) collective-permute-start(bf16[72,128]{1,0:T(8,128)(2,1)S(1)} %shard_map.53), channel_id=1, source_target_pairs={{12,0},{24,12},{36,24},{48,36},{60,48},{72,60},{84,72},{96,84},{10... | collective-permute-start | bytes 55304 | tf_op jit(solution)/shard_map/ppermute | solution.py:315
  45.6 13.3 %all-to-all-start = ((f32[8,72,128]{2,1,0:T(8,128)}), f32[8,72,128]{2,1,0:T(8,128)S(1)}, u32[]{:S(2)}, u32[]{:S(2)}) async-start(f32[8,72,128]{2,1,0:T(8,128)} %get-tuple-element.19), calls=%async_computation | async-start | bytes 589824 | tf_op jit(solution)/shard_map/all_to_all | solution.py:290
  54.4 0.9 copy-start
  57.1 0.7 copy-start.3
  59.0 4.7 %collective-permute-start.10 = (f32[1,72,128]{2,1,0:T(8,128)S(1)}, f32[1,72,128]{2,1,0:T(8,128)S(1)}, u32[]{:S(2)}, u32[]{:S(2)}) collective-permute-start(f32[1,72,128]{2,1,0:T(8,128)S(1)} %shard_map.55), channel_id=1, source_target_pairs={{0,11},{1,0},{2,1},{3,2},{4,3},{5,4},{6,5},{7,6},{8,7},{9,8},{10,9... | collective-permute-start | bytes 110600 | tf_op jit(solution)/shard_map/ppermute | solution.py:358
  64.4 15.2 %all-to-all-start.1 = ((f32[8,72,128]{2,1,0:T(8,128)}), f32[8,72,128]{2,1,0:T(8,128)S(1)}, u32[]{:S(2)}, u32[]{:S(2)}) async-start(f32[8,72,128]{2,1,0:T(8,128)} %shard_map.59), calls=%async_computation.1 | async-start | bytes 589824 | tf_op jit(solution)/shard_map/all_to_all | solution.py:290
  69.8 19.2 %collective-permute-start.7 = (f32[24,3072]{1,0:T(8,128)}, f32[24,3072]{1,0:T(8,128)S(1)}, u32[]{:S(2)}, u32[]{:S(2)}) collective-permute-start(f32[24,3072]{1,0:T(8,128)} %copy-done.3), channel_id=1, source_target_pairs={{0,2},{1,3},{2,4},{3,5},{4,6},{5,7},{6,8},{7,9},{8,10},{9,11},{10,... | collective-permute-start | bytes 884744 | tf_op jit(solution)/shard_map/ppermute | solution.py:309
  73.9 15.3 %collective-permute-start.8 = (f32[24,3072]{1,0:T(8,128)S(1)}, f32[24,3072]{1,0:T(8,128)S(1)}, u32[]{:S(2)}, u32[]{:S(2)}) collective-permute-start(f32[24,3072]{1,0:T(8,128)S(1)} %get-tuple-element.27), channel_id=1, source_target_pairs={{0,11},{1,0},{2,1},{3,2},{4,3},{5,4},{6,5},{7,6},{8,7},{9,8},{10,9... | collective-permute-start | bytes 884744 | tf_op jit(solution)/shard_map/ppermute | solution.py:287
  77.4 12.2 %collective-permute-start.9 = (f32[24,3072]{1,0:T(8,128)S(1)}, f32[24,3072]{1,0:T(8,128)S(1)}, u32[]{:S(2)}, u32[]{:S(2)}) collective-permute-start(f32[24,3072]{1,0:T(8,128)S(1)} %get-tuple-element.28), channel_id=1, source_target_pairs={{0,1},{1,2},{2,3},{3,4},{4,5},{5,6},{6,7},{7,8},{8,9},{9,10},{10,1... | collective-permute-start | bytes 884744 | tf_op jit(solution)/shard_map/ppermute | solution.py:287
  80.4 15.3 %all-to-all-start.2 = ((f32[8,72,128]{2,1,0:T(8,128)}), f32[8,72,128]{2,1,0:T(8,128)S(1)}, u32[]{:S(2)}, u32[]{:S(2)}) async-start(f32[8,72,128]{2,1,0:T(8,128)} %shard_map.60), calls=%async_computation.2 | async-start | bytes 589824 | tf_op jit(solution)/shard_map/all_to_all | solution.py:290

commit v10 on v9

--- a/solution.py
+++ b/solution.py
@@ -119,8 +119,7 @@
 
 
 def build_kernel(code_ref, *refs):
-    g_refs, (x3, x2, x0, x1), (shifted_ref, window_ref, ends_ref) = refs[:3], refs[3:7], refs[7:]
-    x_refs = (x0, x1, x2, x3)
+    g_refs, x_refs, (shifted_ref, window_ref, ends_ref) = refs[:3], refs[3:7], refs[7:]
     chans = g_refs[0].shape[0]
     rows = g_refs[0].shape[1] // WIDTH
     code = code_ref[0]
@@ -139,10 +138,11 @@
             taps = [pltpu.roll(row, LANES - 4, 1), pltpu.roll(row, LANES - 2, 1), row]
             at = (start + i + 2) * LANES
             shifted_ref[:, at : at + LANES] = jnp.concatenate(taps, axis=0).astype(kind)
-        tiles = [
-            jnp.concatenate([x[:, cut].astype(jnp.float32) for x in x_refs], axis=0)
-            for cut in cuts
-        ]
+        tiles = []
+        for cut in cuts:
+            outer, second, first, own = [x[:, cut].astype(jnp.float32) for x in x_refs]
+            near = sorted_blocks(code, first, own, second)
+            tiles.append(jnp.concatenate([*near, outer], axis=0))
         for i, row in enumerate(load_rows(tiles, 0)):
             r = start + i
             row = jnp.where(lane_x < WIDTH, row, 0.0)
@@ -196,7 +196,7 @@
                 ]
 
 
-def inputs_kernel(shifted_ref, filters_ref, borders_ref, *out_refs):
+def inputs_kernel(code_ref, shifted_ref, filters_ref, borders_ref, *out_refs):
     chans = out_refs[0].shape[0]
     rows = out_refs[0].shape[1] // WIDTH
     lane = lane_index(4 * chans)
@@ -217,9 +217,10 @@
         for r in range(start, start + 4):
             rim = pltpu.roll(edge, LANES - 4 * r, 1) if r else edge
             group.append(total[:, r * LANES : (r + 1) * LANES] + jnp.where(on_rim, rim, 0.0))
+        blocks = [[row[j * chans : (j + 1) * chans] for j in range(4)] for row in group]
+        blocks = [[*sorted_blocks(code_ref[0], *row[:3]), row[3]] for row in blocks]
         for j in range(4):
-            cut = slice(j * chans, (j + 1) * chans)
-            store_dense(out_refs[j], start, [row[cut] for row in group])
+            store_dense(out_refs[j], start, [row[j] for row in blocks])
 
 
 def total_kernel(a_ref, b_ref, c_ref, d_ref, out_ref):
@@ -309,7 +310,7 @@
         return lax.ppermute(cells, ("space", "chan"), pairs)
 
     grads = [apart(dense, 4, -4), dense, apart(dense, -4, 4)]
-    sources = [move(source, 1), source, move(source, -1), move(source, -2)]
+    sources = [move(source, -2), apart(source, -1, 1), apart(source, 1, -1), source]
     edges = call(edges_kernel, shape(3 * chan_dev, LANES), 4, 1)(code, *grads)
     left = lax.ppermute(edges, "space", [(i, i + 1) for i in range(spaces - 1)])
     right = lax.ppermute(edges, "space", [(i + 1, i) for i in range(spaces - 1)])
@@ -337,15 +338,15 @@
         ),
         8,
         1,
-    )(code, *grads, sources[3], sources[2], sources[0], sources[1])
+    )(code, *grads, *sources)
     parts, borders = call(
         weights_kernel,
         (shape(8, 3 * chan_dev, LANES, dtype=wide), shape(3, 9 * chan_dev, LANES)),
         6,
         1,
     )(code, shifted, window, ends, left, right)
-    blocks = call(inputs_kernel, (shape(chan_dev, cells, dtype=wide),) * 4, 3)(
-        shifted, own, borders
+    blocks = call(inputs_kernel, (shape(chan_dev, cells, dtype=wide),) * 4, 4, 1)(
+        code, shifted, own, borders
     )
 
     piece = added(exchange(parts, across), 1)
@@ -356,7 +357,7 @@
         for c in range(chans)
     ]
     piece = lax.ppermute(piece, ("space", "chan"), home)
-    others = [apart(blocks[3], 2, -2), move(blocks[0], -1), move(blocks[2], 1)]
+    others = [apart(blocks[3], 2, -2), apart(blocks[0], -1, 1), apart(blocks[2], 1, -1)]
     piece = added(exchange(added(piece, 8), along), 8)
     whole = exchange(piece, across)
     grad_filters = call(

time: 97.6 us -> 97.6 us (level)
    ppermute x3 -> x7, starting transfers between devices: 21.1 us -> 34.2 us  [apart(): return lax.ppermute(cells, ('space', 'chan'), pairs)]
    ppermute x5 -> x1, starting transfers between devices: 18.3 us -> 7.29 us  [move(): lax.ppermute(cells, 'chan', [(i, (i + step) % chans) for i in range(chans)])]
    ppermute x1, starting transfers between devices: 5.17 us -> 3.95 us  [per_device(): left = lax.ppermute(edges, 'space', [(i, i + 1) for i in range(spaces - 1)])]
  transfers between devices with their start and end apart: 14 -> 14, of which waited for: 6 -> 5; matrix products, arithmetic and copies ran while one was open for 0% -> 0% of each run, Pallas kernels for 9% -> 9%
where the time goes in v10:
time: 97.6 us; the launch traced here: 96.8 us
  starting transfers between devices  70.1 us (72%)
  Pallas kernels  12.8 us (13%)
  waiting for transfers between devices  9.65 us (10%)
  local copies, waits for them, and re-layouts  3.46 us (4%)
    ppermute x7, starting transfers between devices, apart(): return lax.ppermute(cells, ('space', 'chan'), pairs)  34.2 us
    all_to_all x3, starting transfers between devices, exchange(): lax.all_to_all(parts, 'space', 0, 0, axis_index_groups=groups, tiled=True)  19.6 us
    ppermute x1, starting transfers between devices, move(): lax.ppermute(cells, 'chan', [(i, (i + step) % chans) for i in range(chans)])  7.29 us
    all_to_all x3, waiting for transfers between devices, exchange(): lax.all_to_all(parts, 'space', 0, 0, axis_index_groups=groups, tiled=True)  6.65 us
    ppermute x1, starting transfers between devices, per_device(): left = lax.ppermute(edges, 'space', [(i, i + 1) for i in range(spaces - 1)])  3.95 us
    unnamed x8, local copies, waits for them, and re-layouts  3.46 us
    ppermute x1, starting transfers between devices, per_device(): piece = lax.ppermute(piece, ('space', 'chan'), home)  3.14 us
    pallas_call x1, Pallas kernels, per_device(): call(weights_kernel, (shape(8, 3 * chan_dev, LANES, dtype=wide), shape(3,...  2.47 us
  transfers between devices with their start and end apart: 14, of which 5 were waited for; matrix products, arithmetic and copies ran while one was open for 0% of the time, Pallas kernels for 9%

profile of v10, /device:TPU:1, one launch (start us, length us, event | category | flops | bytes accessed | tf_op | source)
XLA Modules:
  0.0 96.8 jit_solution(6303629698092033704)
XLA Ops:
  0.6 0.9 copy-done.1
  1.6 0.2 shard_map.50.refs_1_.own_ref
  1.7 15.1 %collective-permute-start = (bf16[24,3072]{1,0:T(8,128)(2,1)S(1)}, bf16[24,3072]{1,0:T(8,128)(2,1)S(1)}, u32[]{:S(2)}, u32[]{:S(2)}) collective-permute-start(bf16[24,3072]{1,0:T(8,128)(2,1)S(1)} %shard_map.50.refs_1_.own_ref), channel_id=1, source_target_pairs={{0,4},{1,5},{2,6},{3,7},{4,8},{5,9},{6,10},{7,11},{8,0},{9,1},{10,... | collective-permute-start | bytes 442376 | tf_op jit(solution)/shard_map/ppermute | solution.py:310
  16.8 1.9 %collective-permute-start.1 = (bf16[24,3072]{1,0:T(8,128)(2,1)S(1)}, bf16[24,3072]{1,0:T(8,128)(2,1)S(1)}, u32[]{:S(2)}, u32[]{:S(2)}) collective-permute-start(bf16[24,3072]{1,0:T(8,128)(2,1)S(1)} %shard_map.50.refs_1_.own_ref), channel_id=1, source_target_pairs={{0,8},{1,9},{2,10},{3,11},{4,0},{5,1},{6,2},{7,3},{8,4},{9,5},{10,... | collective-permute-start | bytes 442376 | tf_op jit(solution)/shard_map/ppermute | solution.py:310
  18.8 0.9 copy-done.2
  19.9 7.3 %collective-permute-start.2 = (bf16[24,3072]{1,0:T(8,128)(2,1)S(1)}, bf16[24,3072]{1,0:T(8,128)(2,1)S(1)}, u32[]{:S(2)}, u32[]{:S(2)}) collective-permute-start(bf16[24,3072]{1,0:T(8,128)(2,1)S(1)} %shard_map.51.refs_6_), channel_id=1, source_target_pairs={{0,10},{1,11},{2,0},{3,1},{4,2},{5,3},{6,4},{7,5},{8,6},{9,7},{10,... | collective-permute-start | bytes 442376 | tf_op jit(solution)/shard_map/ppermute | solution.py:288
  27.2 3.1 %collective-permute-start.3 = (bf16[24,3072]{1,0:T(8,128)(2,1)S(1)}, bf16[24,3072]{1,0:T(8,128)(2,1)S(1)}, u32[]{:S(2)}, u32[]{:S(2)}) collective-permute-start(bf16[24,3072]{1,0:T(8,128)(2,1)S(1)} %shard_map.51.refs_6_), channel_id=1, source_target_pairs={{0,11},{1,0},{2,1},{3,2},{4,3},{5,4},{6,5},{7,6},{8,7},{9,8},{10,9... | collective-permute-start | bytes 442376 | tf_op jit(solution)/shard_map/ppermute | solution.py:310
  30.3 3.4 %collective-permute-start.4 = (bf16[24,3072]{1,0:T(8,128)(2,1)S(1)}, bf16[24,3072]{1,0:T(8,128)(2,1)S(1)}, u32[]{:S(2)}, u32[]{:S(2)}) collective-permute-start(bf16[24,3072]{1,0:T(8,128)(2,1)S(1)} %shard_map.51.refs_6_), channel_id=1, source_target_pairs={{0,1},{1,2},{2,3},{3,4},{4,5},{5,6},{6,7},{7,8},{8,9},{9,10},{10,1... | collective-permute-start | bytes 442376 | tf_op jit(solution)/shard_map/ppermute | solution.py:310
  33.7 0.4 shard_map.53
  34.1 4.0 %collective-permute-start.5 = (bf16[72,128]{1,0:T(8,128)(2,1)S(1)}, bf16[72,128]{1,0:T(8,128)(2,1)S(1)}, u32[]{:S(2)}, u32[]{:S(2)}) collective-permute-start(bf16[72,128]{1,0:T(8,128)(2,1)S(1)} %shard_map.53), channel_id=1, source_target_pairs={{0,12},{12,24},{24,36},{36,48},{48,60},{60,72},{72,84},{84,96},{96... | collective-permute-start | bytes 55304 | tf_op jit(solution)/shard_map/ppermute | solution.py:315
  38.1 1.9 %collective-permute-start.6 = (bf16[72,128]{1,0:T(8,128)(2,1)S(1)}, bf16[72,128]{1,0:T(8,128)(2,1)S(1)}, u32[]{:S(2)}, u32[]{:S(2)}) collective-permute-start(bf16[72,128]{1,0:T(8,128)(2,1)S(1)} %shard_map.53), channel_id=1, source_target_pairs={{12,0},{24,12},{36,24},{48,36},{60,48},{72,60},{84,72},{96,84},{10... | collective-permute-start | bytes 55304 | tf_op jit(solution)/shard_map/ppermute | solution.py:316
  40.0 1.8 %shard_map.52 = (bf16[216,4608]{1,0:T(8,128)(2,1)S(1)}, bf16[96,4096]{1,0:T(8,128)(2,1)S(1)}, bf16[96,128]{1,0:T(8,128)(2,1)S(1)}) custom-call(s32[1]{0:T(128)} %bitcast.code_ref, bf16[24,3072]{1,0:T(8,128)(2,1)S(1)} %collective-permute-done.refs_0_.first_ref, bf16[24,3072]{1,0:T(8,128)(2,1)S(1)} %shard_map.50.refs_1_.own_ref, ...), custom_call_target="tpu_custom_call" | custom-call | tf_op jit(solution)/shard_map/pallas_call | solution.py:332
  41.9 1.3 %collective-permute-done.6.right_ref = bf16[72,128]{1,0:T(8,128)(2,1)S(1)} collective-permute-done((bf16[72,128]{1,0:T(8,128)(2,1)S(1)}, bf16[72,128]{1,0:T(8,128)(2,1)S(1)}, u32[]{:S(2)}, u32[]{:S(2)}) %collective-permute-start.6) | collective-permute-done | bytes 18464 | tf_op jit(solution)/shard_map/ppermute | solution.py:316
  43.2 2.5 %shard_map.54 = (f32[8,72,128]{2,1,0:T(8,128)}, bf16[3,216,128]{2,1,0:T(8,128)(2,1)S(1)}) custom-call(s32[1]{0:T(128)} %bitcast.code_ref, bf16[216,4608]{1,0:T(8,128)(2,1)S(1)} %get-tuple-element.16.shifted_ref, bf16[96,4096]{1,0:T(8,128)(2,1)S(1)} %get-tuple-element.17.window_ref, bf16[96,128]{1,0:T(8,128)(2,1)S(1)} %get-tuple-element.18.ends_ref, ...), custom_call_target="tpu_custom_call" | custom-call | tf_op jit(solution)/shard_map/pallas_call | solution.py:342
  45.6 6.5 %all-to-all-start = ((f32[8,72,128]{2,1,0:T(8,128)}), f32[8,72,128]{2,1,0:T(8,128)S(1)}, u32[]{:S(2)}, u32[]{:S(2)}) async-start(f32[8,72,128]{2,1,0:T(8,128)} %get-tuple-element.19), calls=%async_computation | async-start | bytes 589824 | tf_op jit(solution)/shard_map/all_to_all | solution.py:291
  52.1 2.2 %shard_map.56.filters_ref = bf16[3,96,216]{2,1,0:T(8,128)(2,1)} custom-call(s32[1]{0:T(128)} %bitcast.code_ref, bf16[9,288,288]{2,1,0:T(8,128)(2,1)} %w3.1, bf16[9,288,288]{2,1,0:T(8,128)(2,1)} %w3.1, bf16[9,288,288]{2,1,0:T(8,128)(2,1)} %w3.1, bf16[9,288,288]{2,1,0:T(8,128)(2,1)} %w3.1), custom_call_target="tpu_custom_call" | custom-call | tf_op jit(solution)/shard_map/pallas_call | solution.py:318
  54.3 0.9 copy-done
  55.2 1.8 %shard_map.57 = (f32[24,3072]{1,0:T(8,128)S(1)}, f32[24,3072]{1,0:T(8,128)S(1)}, f32[24,3072]{1,0:T(8,128)S(1)}, f32[24,3072]{1,0:T(8,128)S(1)}) custom-call(s32[1]{0:T(128)} %bitcast.code_ref, bf16[216,4608]{1,0:T(8,128)(2,1)S(1)} %get-tuple-element.16.shifted_ref, bf16[3,96,216]{2,1,0:T(8,128)(2,1)S(1)} %copy-done, ...), custom_call_target="tpu_custom_call" | custom-call | tf_op jit(solution)/shard_map/pallas_call | solution.py:348
  57.1 0.7 copy-done.3
  57.8 1.1 %all-to-all-done.in_ref = f32[8,72,128]{2,1,0:T(8,128)S(1)} async-done(((f32[8,72,128]{2,1,0:T(8,128)}), f32[8,72,128]{2,1,0:T(8,128)S(1)}, u32[]{:S(2)}, u32[]{:S(2)}) %all-to-all-start) | async-done | bytes 294944 | tf_op jit(solution)/shard_map/all_to_all | solution.py:291
  58.9 3.1 %collective-permute-start.10 = (f32[1,72,128]{2,1,0:T(8,128)S(1)}, f32[1,72,128]{2,1,0:T(8,128)S(1)}, u32[]{:S(2)}, u32[]{:S(2)}) collective-permute-start(f32[1,72,128]{2,1,0:T(8,128)S(1)} %shard_map.55), channel_id=1, source_target_pairs={{0,11},{1,0},{2,1},{3,2},{4,3},{5,4},{6,5},{7,6},{8,7},{9,8},{10,9... | collective-permute-start | bytes 110600 | tf_op jit(solution)/shard_map/ppermute | solution.py:359
  62.1 1.6 %collective-permute-done.10.in_ref = f32[1,72,128]{2,1,0:T(8,128)S(1)} collective-permute-done((f32[1,72,128]{2,1,0:T(8,128)S(1)}, f32[1,72,128]{2,1,0:T(8,128)S(1)}, u32[]{:S(2)}, u32[]{:S(2)}) %collective-permute-start.10) | collective-permute-done | bytes 36896 | tf_op jit(solution)/shard_map/ppermute | solution.py:359
  63.6 0.7 shard_map.59
  64.4 5.4 %all-to-all-start.1 = ((f32[8,72,128]{2,1,0:T(8,128)}), f32[8,72,128]{2,1,0:T(8,128)S(1)}, u32[]{:S(2)}, u32[]{:S(2)}) async-start(f32[8,72,128]{2,1,0:T(8,128)} %shard_map.59), calls=%async_computation.1 | async-start | bytes 589824 | tf_op jit(solution)/shard_map/all_to_all | solution.py:291
  69.8 4.2 %collective-permute-start.7 = (f32[24,3072]{1,0:T(8,128)}, f32[24,3072]{1,0:T(8,128)S(1)}, u32[]{:S(2)}, u32[]{:S(2)}) collective-permute-start(f32[24,3072]{1,0:T(8,128)} %copy-done.3), channel_id=1, source_target_pairs={{0,2},{1,3},{2,4},{3,5},{4,6},{5,7},{6,8},{7,9},{8,10},{9,11},{10,... | collective-permute-start | bytes 884744 | tf_op jit(solution)/shard_map/ppermute | solution.py:310
  74.0 3.8 %collective-permute-start.8 = (f32[24,3072]{1,0:T(8,128)S(1)}, f32[24,3072]{1,0:T(8,128)S(1)}, u32[]{:S(2)}, u32[]{:S(2)}) collective-permute-start(f32[24,3072]{1,0:T(8,128)S(1)} %get-tuple-element.27), channel_id=1, source_target_pairs={{0,11},{1,0},{2,1},{3,2},{4,3},{5,4},{6,5},{7,6},{8,7},{9,8},{10,9... | collective-permute-start | bytes 884744 | tf_op jit(solution)/shard_map/ppermute | solution.py:310
  77.7 2.7 %collective-permute-start.9 = (f32[24,3072]{1,0:T(8,128)S(1)}, f32[24,3072]{1,0:T(8,128)S(1)}, u32[]{:S(2)}, u32[]{:S(2)}) collective-permute-start(f32[24,3072]{1,0:T(8,128)S(1)} %get-tuple-element.28), channel_id=1, source_target_pairs={{0,1},{1,2},{2,3},{3,4},{4,5},{5,6},{6,7},{7,8},{8,9},{9,10},{10,1... | collective-permute-start | bytes 884744 | tf_op jit(solution)/shard_map/ppermute | solution.py:310
  80.5 0.7 shard_map.60
  81.2 7.7 %all-to-all-start.2 = ((f32[8,72,128]{2,1,0:T(8,128)}), f32[8,72,128]{2,1,0:T(8,128)S(1)}, u32[]{:S(2)}, u32[]{:S(2)}) async-start(f32[8,72,128]{2,1,0:T(8,128)} %shard_map.60), calls=%async_computation.2 | async-start | bytes 589824 | tf_op jit(solution)/shard_map/all_to_all | solution.py:291
  89.1 1.1 %shard_map.58 = f32[24,32,96]{2,1,0:T(8,128)} custom-call(f32[24,3072]{1,0:T(8,128)S(1)} %get-tuple-element.25.a_ref, f32[24,3072]{1,0:T(8,128)S(1)} %collective-permute-done.7.b_ref, f32[24,3072]{1,0:T(8,128)S(1)} %collective-permute-done.8.c_ref, f32[24,3072]{1,0:T(8,128)S(1)} %collective-permute-done.9.d_ref), custom_call_target="tpu_custom_call" | custom-call | tf_op jit(solution)/shard_map/pallas_call | solution.py:369
  90.3 5.5 %all-to-all-done.2.whole_ref = f32[8,72,128]{2,1,0:T(8,128)S(1)} async-done(((f32[8,72,128]{2,1,0:T(8,128)}), f32[8,72,128]{2,1,0:T(8,128)S(1)}, u32[]{:S(2)}, u32[]{:S(2)}) %all-to-all-start.2) | async-done | bytes 294944 | tf_op jit(solution)/shard_map/all_to_all | solution.py:291
  95.8 1.1 %shard_map.61 = f32[9,24,288]{2,1,0:T(8,128)} custom-call(s32[1]{0:T(128)} %bitcast.4.layer_ref, f32[8,72,128]{2,1,0:T(8,128)S(1)} %all-to-all-done.2.whole_ref), custom_call_target="tpu_custom_call" | custom-call | tf_op jit(solution)/shard_map/pallas_call | solution.py:363
  (16 shorter events, 0.4 us)
Async XLA Ops:
  0.6 0.9 copy-start.1
  1.7 32.0 %collective-permute-start = (bf16[24,3072]{1,0:T(8,128)(2,1)S(1)}, bf16[24,3072]{1,0:T(8,128)(2,1)S(1)}, u32[]{:S(2)}, u32[]{:S(2)}) collective-permute-start(bf16[24,3072]{1,0:T(8,128)(2,1)S(1)} %shard_map.50.refs_1_.own_ref), channel_id=1, source_target_pairs={{0,4},{1,5},{2,6},{3,7},{4,8},{5,9},{6,10},{7,11},{8,0},{9,1},{10,... | collective-permute-start | bytes 442376 | tf_op jit(solution)/shard_map/ppermute | solution.py:310
  16.8 16.9 %collective-permute-start.1 = (bf16[24,3072]{1,0:T(8,128)(2,1)S(1)}, bf16[24,3072]{1,0:T(8,128)(2,1)S(1)}, u32[]{:S(2)}, u32[]{:S(2)}) collective-permute-start(bf16[24,3072]{1,0:T(8,128)(2,1)S(1)} %shard_map.50.refs_1_.own_ref), channel_id=1, source_target_pairs={{0,8},{1,9},{2,10},{3,11},{4,0},{5,1},{6,2},{7,3},{8,4},{9,5},{10,... | collective-permute-start | bytes 442376 | tf_op jit(solution)/shard_map/ppermute | solution.py:310
  18.8 0.9 copy-start.2
  19.9 20.1 %collective-permute-start.2 = (bf16[24,3072]{1,0:T(8,128)(2,1)S(1)}, bf16[24,3072]{1,0:T(8,128)(2,1)S(1)}, u32[]{:S(2)}, u32[]{:S(2)}) collective-permute-start(bf16[24,3072]{1,0:T(8,128)(2,1)S(1)} %shard_map.51.refs_6_), channel_id=1, source_target_pairs={{0,10},{1,11},{2,0},{3,1},{4,2},{5,3},{6,4},{7,5},{8,6},{9,7},{10,... | collective-permute-start | bytes 442376 | tf_op jit(solution)/shard_map/ppermute | solution.py:288
  27.2 12.9 %collective-permute-start.3 = (bf16[24,3072]{1,0:T(8,128)(2,1)S(1)}, bf16[24,3072]{1,0:T(8,128)(2,1)S(1)}, u32[]{:S(2)}, u32[]{:S(2)}) collective-permute-start(bf16[24,3072]{1,0:T(8,128)(2,1)S(1)} %shard_map.51.refs_6_), channel_id=1, source_target_pairs={{0,11},{1,0},{2,1},{3,2},{4,3},{5,4},{6,5},{7,6},{8,7},{9,8},{10,9... | collective-permute-start | bytes 442376 | tf_op jit(solution)/shard_map/ppermute | solution.py:310
  30.3 9.8 %collective-permute-start.4 = (bf16[24,3072]{1,0:T(8,128)(2,1)S(1)}, bf16[24,3072]{1,0:T(8,128)(2,1)S(1)}, u32[]{:S(2)}, u32[]{:S(2)}) collective-permute-start(bf16[24,3072]{1,0:T(8,128)(2,1)S(1)} %shard_map.51.refs_6_), channel_id=1, source_target_pairs={{0,1},{1,2},{2,3},{3,4},{4,5},{5,6},{6,7},{7,8},{8,9},{9,10},{10,1... | collective-permute-start | bytes 442376 | tf_op jit(solution)/shard_map/ppermute | solution.py:310
  34.1 7.8 %collective-permute-start.5 = (bf16[72,128]{1,0:T(8,128)(2,1)S(1)}, bf16[72,128]{1,0:T(8,128)(2,1)S(1)}, u32[]{:S(2)}, u32[]{:S(2)}) collective-permute-start(bf16[72,128]{1,0:T(8,128)(2,1)S(1)} %shard_map.53), channel_id=1, source_target_pairs={{0,12},{12,24},{24,36},{36,48},{48,60},{60,72},{72,84},{84,96},{96... | collective-permute-start | bytes 55304 | tf_op jit(solution)/shard_map/ppermute | solution.py:315
  38.1 5.1 %collective-permute-start.6 = (bf16[72,128]{1,0:T(8,128)(2,1)S(1)}, bf16[72,128]{1,0:T(8,128)(2,1)S(1)}, u32[]{:S(2)}, u32[]{:S(2)}) collective-permute-start(bf16[72,128]{1,0:T(8,128)(2,1)S(1)} %shard_map.53), channel_id=1, source_target_pairs={{12,0},{24,12},{36,24},{48,36},{60,48},{72,60},{84,72},{96,84},{10... | collective-permute-start | bytes 55304 | tf_op jit(solution)/shard_map/ppermute | solution.py:316
  45.6 13.3 %all-to-all-start = ((f32[8,72,128]{2,1,0:T(8,128)}), f32[8,72,128]{2,1,0:T(8,128)S(1)}, u32[]{:S(2)}, u32[]{:S(2)}) async-start(f32[8,72,128]{2,1,0:T(8,128)} %get-tuple-element.19), calls=%async_computation | async-start | bytes 589824 | tf_op jit(solution)/shard_map/all_to_all | solution.py:291
  54.3 0.9 copy-start
  57.1 0.7 copy-start.3
  58.9 4.7 %collective-permute-start.10 = (f32[1,72,128]{2,1,0:T(8,128)S(1)}, f32[1,72,128]{2,1,0:T(8,128)S(1)}, u32[]{:S(2)}, u32[]{:S(2)}) collective-permute-start(f32[1,72,128]{2,1,0:T(8,128)S(1)} %shard_map.55), channel_id=1, source_target_pairs={{0,11},{1,0},{2,1},{3,2},{4,3},{5,4},{6,5},{7,6},{8,7},{9,8},{10,9... | collective-permute-start | bytes 110600 | tf_op jit(solution)/shard_map/ppermute | solution.py:359
  64.4 16.1 %all-to-all-start.1 = ((f32[8,72,128]{2,1,0:T(8,128)}), f32[8,72,128]{2,1,0:T(8,128)S(1)}, u32[]{:S(2)}, u32[]{:S(2)}) async-start(f32[8,72,128]{2,1,0:T(8,128)} %shard_map.59), calls=%async_computation.1 | async-start | bytes 589824 | tf_op jit(solution)/shard_map/all_to_all | solution.py:291
  69.8 19.2 %collective-permute-start.7 = (f32[24,3072]{1,0:T(8,128)}, f32[24,3072]{1,0:T(8,128)S(1)}, u32[]{:S(2)}, u32[]{:S(2)}) collective-permute-start(f32[24,3072]{1,0:T(8,128)} %copy-done.3), channel_id=1, source_target_pairs={{0,2},{1,3},{2,4},{3,5},{4,6},{5,7},{6,8},{7,9},{8,10},{9,11},{10,... | collective-permute-start | bytes 884744 | tf_op jit(solution)/shard_map/ppermute | solution.py:310
  74.0 15.0 %collective-permute-start.8 = (f32[24,3072]{1,0:T(8,128)S(1)}, f32[24,3072]{1,0:T(8,128)S(1)}, u32[]{:S(2)}, u32[]{:S(2)}) collective-permute-start(f32[24,3072]{1,0:T(8,128)S(1)} %get-tuple-element.27), channel_id=1, source_target_pairs={{0,11},{1,0},{2,1},{3,2},{4,3},{5,4},{6,5},{7,6},{8,7},{9,8},{10,9... | collective-permute-start | bytes 884744 | tf_op jit(solution)/shard_map/ppermute | solution.py:310
  77.7 11.4 %collective-permute-start.9 = (f32[24,3072]{1,0:T(8,128)S(1)}, f32[24,3072]{1,0:T(8,128)S(1)}, u32[]{:S(2)}, u32[]{:S(2)}) collective-permute-start(f32[24,3072]{1,0:T(8,128)S(1)} %get-tuple-element.28), channel_id=1, source_target_pairs={{0,1},{1,2},{2,3},{3,4},{4,5},{5,6},{6,7},{7,8},{8,9},{9,10},{10,1... | collective-permute-start | bytes 884744 | tf_op jit(solution)/shard_map/ppermute | solution.py:310
  81.2 14.5 %all-to-all-start.2 = ((f32[8,72,128]{2,1,0:T(8,128)}), f32[8,72,128]{2,1,0:T(8,128)S(1)}, u32[]{:S(2)}, u32[]{:S(2)}) async-start(f32[8,72,128]{2,1,0:T(8,128)} %shard_map.60), calls=%async_computation.2 | async-start | bytes 589824 | tf_op jit(solution)/shard_map/all_to_all | solution.py:291

commit v11 on v10

--- a/solution.py
+++ b/solution.py
@@ -156,16 +156,18 @@
 
 
 def weights_kernel(
-    code_ref, shifted_ref, window_ref, ends_ref, left_ref, right_ref, parts_ref, borders_ref
+    code_ref, shifted_ref, window_ref, ends_ref, inner_ref, outer_ref, parts_ref, borders_ref
 ):
-    chans = left_ref.shape[0] // 3
+    chans = inner_ref.shape[0] // 3
     rows = window_ref.shape[1] // LANES
     lane = lane_index(3 * chans)
     at_head = lane % 4 < 2
     row_of = jnp.where(at_head, lane, (lane + LANES - TAIL) % LANES) // 4
+    inner, outer = inner_ref[...].astype(jnp.float32), outer_ref[...].astype(jnp.float32)
+    right, _, left = sorted_blocks(code_ref[0], inner, None, outer)
     sides = [
-        ordered(code_ref[0], *[ref[m * chans : (m + 1) * chans].astype(jnp.float32) for m in range(3)])
-        for ref in (left_ref, right_ref)
+        ordered(code_ref[0], *[side[m * chans : (m + 1) * chans] for m in range(3)])
+        for side in (left, right)
     ]
     contract = (((1,), (1,)), ((), ()))
     for b in range(3):
@@ -312,8 +314,10 @@
     grads = [apart(dense, 4, -4), dense, apart(dense, -4, 4)]
     sources = [move(source, -2), apart(source, -1, 1), apart(source, 1, -1), source]
     edges = call(edges_kernel, shape(3 * chan_dev, LANES), 4, 1)(code, *grads)
-    left = lax.ppermute(edges, "space", [(i, i + 1) for i in range(spaces - 1)])
-    right = lax.ppermute(edges, "space", [(i + 1, i) for i in range(spaces - 1)])
+    inner = lax.ppermute(edges, "space", [(i, i ^ 1) for i in range(spaces)])
+    across_chips = [(i, i - 1) for i in range(2, spaces, 2)]
+    across_chips += [(i, i + 1) for i in range(1, spaces - 1, 2)]
+    outer = lax.ppermute(edges, "space", across_chips)
 
     own = pl.pallas_call(
         filters_kernel,
@@ -344,7 +348,7 @@
         (shape(8, 3 * chan_dev, LANES, dtype=wide), shape(3, 9 * chan_dev, LANES)),
         6,
         1,
-    )(code, shifted, window, ends, left, right)
+    )(code, shifted, window, ends, inner, outer)
     blocks = call(inputs_kernel, (shape(chan_dev, cells, dtype=wide),) * 4, 4, 1)(
         code, shifted, own, borders
     )

time: 97.6 us -> 98.7 us (1.011)
  starting transfers between devices: 70.1 us -> 71.8 us
    all_to_all x3, starting transfers between devices: 19.6 us -> 21.2 us  [exchange(): lax.all_to_all(parts, 'space', 0, 0, axis_index_groups=groups, tiled=True)]
    ppermute x2, starting transfers between devices: 5.88 us -> 7.4 us  [the longest x1 4.63 us: per_device(): outer = lax.ppermute(edges, 'space', across_chips)]
    ppermute x2, waiting for transfers between devices: 1.27 us -> 0.01 us  [the longest x1 0.01 us: per_device(): outer = lax.ppermute(edges, 'space', across_chips)]
  transfers between devices with their start and end apart: 14 -> 14, of which waited for: 5 -> 4; matrix products, arithmetic and copies ran while one was open for 0% -> 0% of each run, Pallas kernels for 9% -> 8%
where the time goes in v11:
time: 98.7 us; the launch traced here: 97.9 us
  starting transfers between devices  71.8 us (73%)
  Pallas kernels  12.8 us (13%)
  waiting for transfers between devices  9.04 us (9%)
  local copies, waits for them, and re-layouts  3.46 us (4%)
    ppermute x7, starting transfers between devices, apart(): return lax.ppermute(cells, ('space', 'chan'), pairs)  33.3 us
    all_to_all x3, starting transfers between devices, exchange(): lax.all_to_all(parts, 'space', 0, 0, axis_index_groups=groups, tiled=True)  21.2 us
    ppermute x1, starting transfers between devices, move(): lax.ppermute(cells, 'chan', [(i, (i + step) % chans) for i in range(chans)])  7.29 us
    all_to_all x3, waiting for transfers between devices, exchange(): lax.all_to_all(parts, 'space', 0, 0, axis_index_groups=groups, tiled=True)  6.89 us
    ppermute x1, starting transfers between devices, per_device(): outer = lax.ppermute(edges, 'space', across_chips)  4.63 us
    unnamed x8, local copies, waits for them, and re-layouts  3.46 us
    ppermute x1, starting transfers between devices, per_device(): inner = lax.ppermute(edges, 'space', [(i, i ^ 1) for i in range(spaces)])  2.77 us
    ppermute x1, starting transfers between devices, per_device(): piece = lax.ppermute(piece, ('space', 'chan'), home)  2.57 us
  transfers between devices with their start and end apart: 14, of which 4 were waited for; matrix products, arithmetic and copies ran while one was open for 0% of the time, Pallas kernels for 8%

profile of v11, /device:TPU:1, one launch (start us, length us, event | category | flops | bytes accessed | tf_op | source)
XLA Modules:
  0.0 97.9 jit_solution(15969662243877552974)
XLA Ops:
  0.6 0.9 copy-done.1
  1.6 0.2 shard_map.50.refs_1_.own_ref
  1.7 15.1 %collective-permute-start = (bf16[24,3072]{1,0:T(8,128)(2,1)S(1)}, bf16[24,3072]{1,0:T(8,128)(2,1)S(1)}, u32[]{:S(2)}, u32[]{:S(2)}) collective-permute-start(bf16[24,3072]{1,0:T(8,128)(2,1)S(1)} %shard_map.50.refs_1_.own_ref), channel_id=1, source_target_pairs={{0,4},{1,5},{2,6},{3,7},{4,8},{5,9},{6,10},{7,11},{8,0},{9,1},{10,... | collective-permute-start | bytes 442376 | tf_op jit(solution)/shard_map/ppermute | solution.py:312
  16.8 1.9 %collective-permute-start.1 = (bf16[24,3072]{1,0:T(8,128)(2,1)S(1)}, bf16[24,3072]{1,0:T(8,128)(2,1)S(1)}, u32[]{:S(2)}, u32[]{:S(2)}) collective-permute-start(bf16[24,3072]{1,0:T(8,128)(2,1)S(1)} %shard_map.50.refs_1_.own_ref), channel_id=1, source_target_pairs={{0,8},{1,9},{2,10},{3,11},{4,0},{5,1},{6,2},{7,3},{8,4},{9,5},{10,... | collective-permute-start | bytes 442376 | tf_op jit(solution)/shard_map/ppermute | solution.py:312
  18.8 0.9 copy-done.2
  19.7 0.2 shard_map.51.refs_6_
  19.9 7.3 %collective-permute-start.2 = (bf16[24,3072]{1,0:T(8,128)(2,1)S(1)}, bf16[24,3072]{1,0:T(8,128)(2,1)S(1)}, u32[]{:S(2)}, u32[]{:S(2)}) collective-permute-start(bf16[24,3072]{1,0:T(8,128)(2,1)S(1)} %shard_map.51.refs_6_), channel_id=1, source_target_pairs={{0,10},{1,11},{2,0},{3,1},{4,2},{5,3},{6,4},{7,5},{8,6},{9,7},{10,... | collective-permute-start | bytes 442376 | tf_op jit(solution)/shard_map/ppermute | solution.py:290
  27.2 3.1 %collective-permute-start.3 = (bf16[24,3072]{1,0:T(8,128)(2,1)S(1)}, bf16[24,3072]{1,0:T(8,128)(2,1)S(1)}, u32[]{:S(2)}, u32[]{:S(2)}) collective-permute-start(bf16[24,3072]{1,0:T(8,128)(2,1)S(1)} %shard_map.51.refs_6_), channel_id=1, source_target_pairs={{0,11},{1,0},{2,1},{3,2},{4,3},{5,4},{6,5},{7,6},{8,7},{9,8},{10,9... | collective-permute-start | bytes 442376 | tf_op jit(solution)/shard_map/ppermute | solution.py:312
  30.3 3.4 %collective-permute-start.4 = (bf16[24,3072]{1,0:T(8,128)(2,1)S(1)}, bf16[24,3072]{1,0:T(8,128)(2,1)S(1)}, u32[]{:S(2)}, u32[]{:S(2)}) collective-permute-start(bf16[24,3072]{1,0:T(8,128)(2,1)S(1)} %shard_map.51.refs_6_), channel_id=1, source_target_pairs={{0,1},{1,2},{2,3},{3,4},{4,5},{5,6},{6,7},{7,8},{8,9},{9,10},{10,1... | collective-permute-start | bytes 442376 | tf_op jit(solution)/shard_map/ppermute | solution.py:312
  33.7 0.4 shard_map.53
  34.1 2.8 %collective-permute-start.5 = (bf16[72,128]{1,0:T(8,128)(2,1)S(1)}, bf16[72,128]{1,0:T(8,128)(2,1)S(1)}, u32[]{:S(2)}, u32[]{:S(2)}) collective-permute-start(bf16[72,128]{1,0:T(8,128)(2,1)S(1)} %shard_map.53), channel_id=1, source_target_pairs={{0,12},{12,0},{24,36},{36,24},{48,60},{60,48},{72,84},{84,72},{96,... | collective-permute-start | bytes 55304 | tf_op jit(solution)/shard_map/ppermute | solution.py:317
  36.9 4.6 %collective-permute-start.6 = (bf16[72,128]{1,0:T(8,128)(2,1)S(1)}, bf16[72,128]{1,0:T(8,128)(2,1)S(1)}, u32[]{:S(2)}, u32[]{:S(2)}) collective-permute-start(bf16[72,128]{1,0:T(8,128)(2,1)S(1)} %shard_map.53), channel_id=1, source_target_pairs={{24,12},{48,36},{72,60},{96,84},{120,108},{144,132},{168,156},{192... | collective-permute-start | bytes 55304 | tf_op jit(solution)/shard_map/ppermute | solution.py:320
  41.6 1.8 %shard_map.52 = (bf16[216,4608]{1,0:T(8,128)(2,1)S(1)}, bf16[96,4096]{1,0:T(8,128)(2,1)S(1)}, bf16[96,128]{1,0:T(8,128)(2,1)S(1)}) custom-call(s32[1]{0:T(128)} %bitcast.code_ref, bf16[24,3072]{1,0:T(8,128)(2,1)S(1)} %collective-permute-done.refs_0_.first_ref, bf16[24,3072]{1,0:T(8,128)(2,1)S(1)} %shard_map.50.refs_1_.own_ref, ...), custom_call_target="tpu_custom_call" | custom-call | tf_op jit(solution)/shard_map/pallas_call | solution.py:336
  43.4 2.5 %shard_map.54 = (f32[8,72,128]{2,1,0:T(8,128)}, bf16[3,216,128]{2,1,0:T(8,128)(2,1)S(1)}) custom-call(s32[1]{0:T(128)} %bitcast.code_ref, bf16[216,4608]{1,0:T(8,128)(2,1)S(1)} %get-tuple-element.16.shifted_ref, bf16[96,4096]{1,0:T(8,128)(2,1)S(1)} %get-tuple-element.17.window_ref, bf16[96,128]{1,0:T(8,128)(2,1)S(1)} %get-tuple-element.18.ends_ref, ...), custom_call_target="tpu_custom_call" | custom-call | tf_op jit(solution)/shard_map/pallas_call | solution.py:346
  45.9 6.5 %all-to-all-start = ((f32[8,72,128]{2,1,0:T(8,128)}), f32[8,72,128]{2,1,0:T(8,128)S(1)}, u32[]{:S(2)}, u32[]{:S(2)}) async-start(f32[8,72,128]{2,1,0:T(8,128)} %get-tuple-element.19), calls=%async_computation | async-start | bytes 589824 | tf_op jit(solution)/shard_map/all_to_all | solution.py:293
  52.4 2.2 %shard_map.56.filters_ref = bf16[3,96,216]{2,1,0:T(8,128)(2,1)} custom-call(s32[1]{0:T(128)} %bitcast.code_ref, bf16[9,288,288]{2,1,0:T(8,128)(2,1)} %w3.1, bf16[9,288,288]{2,1,0:T(8,128)(2,1)} %w3.1, bf16[9,288,288]{2,1,0:T(8,128)(2,1)} %w3.1, bf16[9,288,288]{2,1,0:T(8,128)(2,1)} %w3.1), custom_call_target="tpu_custom_call" | custom-call | tf_op jit(solution)/shard_map/pallas_call | solution.py:322
  54.6 0.9 copy-done
  55.5 1.8 %shard_map.57 = (f32[24,3072]{1,0:T(8,128)S(1)}, f32[24,3072]{1,0:T(8,128)S(1)}, f32[24,3072]{1,0:T(8,128)S(1)}, f32[24,3072]{1,0:T(8,128)S(1)}) custom-call(s32[1]{0:T(128)} %bitcast.code_ref, bf16[216,4608]{1,0:T(8,128)(2,1)S(1)} %get-tuple-element.16.shifted_ref, bf16[3,96,216]{2,1,0:T(8,128)(2,1)S(1)} %copy-done, ...), custom_call_target="tpu_custom_call" | custom-call | tf_op jit(solution)/shard_map/pallas_call | solution.py:352
  57.4 0.7 copy-done.3
  58.1 1.1 %all-to-all-done.in_ref = f32[8,72,128]{2,1,0:T(8,128)S(1)} async-done(((f32[8,72,128]{2,1,0:T(8,128)}), f32[8,72,128]{2,1,0:T(8,128)S(1)}, u32[]{:S(2)}, u32[]{:S(2)}) %all-to-all-start) | async-done | bytes 294944 | tf_op jit(solution)/shard_map/all_to_all | solution.py:293
  59.2 2.6 %collective-permute-start.10 = (f32[1,72,128]{2,1,0:T(8,128)S(1)}, f32[1,72,128]{2,1,0:T(8,128)S(1)}, u32[]{:S(2)}, u32[]{:S(2)}) collective-permute-start(f32[1,72,128]{2,1,0:T(8,128)S(1)} %shard_map.55), channel_id=1, source_target_pairs={{0,11},{1,0},{2,1},{3,2},{4,3},{5,4},{6,5},{7,6},{8,7},{9,8},{10,9... | collective-permute-start | bytes 110600 | tf_op jit(solution)/shard_map/ppermute | solution.py:363
  61.8 2.1 %collective-permute-done.10.in_ref = f32[1,72,128]{2,1,0:T(8,128)S(1)} collective-permute-done((f32[1,72,128]{2,1,0:T(8,128)S(1)}, f32[1,72,128]{2,1,0:T(8,128)S(1)}, u32[]{:S(2)}, u32[]{:S(2)}) %collective-permute-start.10) | collective-permute-done | bytes 36896 | tf_op jit(solution)/shard_map/ppermute | solution.py:363
  63.9 0.7 shard_map.59
  64.7 5.9 %all-to-all-start.1 = ((f32[8,72,128]{2,1,0:T(8,128)}), f32[8,72,128]{2,1,0:T(8,128)S(1)}, u32[]{:S(2)}, u32[]{:S(2)}) async-start(f32[8,72,128]{2,1,0:T(8,128)} %shard_map.59), calls=%async_computation.1 | async-start | bytes 589824 | tf_op jit(solution)/shard_map/all_to_all | solution.py:293
  70.6 3.3 %collective-permute-start.7 = (f32[24,3072]{1,0:T(8,128)}, f32[24,3072]{1,0:T(8,128)S(1)}, u32[]{:S(2)}, u32[]{:S(2)}) collective-permute-start(f32[24,3072]{1,0:T(8,128)} %copy-done.3), channel_id=1, source_target_pairs={{0,2},{1,3},{2,4},{3,5},{4,6},{5,7},{6,8},{7,9},{8,10},{9,11},{10,... | collective-permute-start | bytes 884744 | tf_op jit(solution)/shard_map/ppermute | solution.py:312
  73.9 3.4 %collective-permute-start.8 = (f32[24,3072]{1,0:T(8,128)S(1)}, f32[24,3072]{1,0:T(8,128)S(1)}, u32[]{:S(2)}, u32[]{:S(2)}) collective-permute-start(f32[24,3072]{1,0:T(8,128)S(1)} %get-tuple-element.27), channel_id=1, source_target_pairs={{0,11},{1,0},{2,1},{3,2},{4,3},{5,4},{6,5},{7,6},{8,7},{9,8},{10,9... | collective-permute-start | bytes 884744 | tf_op jit(solution)/shard_map/ppermute | solution.py:312
  77.3 3.1 %collective-permute-start.9 = (f32[24,3072]{1,0:T(8,128)S(1)}, f32[24,3072]{1,0:T(8,128)S(1)}, u32[]{:S(2)}, u32[]{:S(2)}) collective-permute-start(f32[24,3072]{1,0:T(8,128)S(1)} %get-tuple-element.28), channel_id=1, source_target_pairs={{0,1},{1,2},{2,3},{3,4},{4,5},{5,6},{6,7},{7,8},{8,9},{9,10},{10,1... | collective-permute-start | bytes 884744 | tf_op jit(solution)/shard_map/ppermute | solution.py:312
  80.5 0.7 shard_map.60
  81.3 8.8 %all-to-all-start.2 = ((f32[8,72,128]{2,1,0:T(8,128)}), f32[8,72,128]{2,1,0:T(8,128)S(1)}, u32[]{:S(2)}, u32[]{:S(2)}) async-start(f32[8,72,128]{2,1,0:T(8,128)} %shard_map.60), calls=%async_computation.2 | async-start | bytes 589824 | tf_op jit(solution)/shard_map/all_to_all | solution.py:293
  90.1 1.1 %shard_map.58 = f32[24,32,96]{2,1,0:T(8,128)} custom-call(f32[24,3072]{1,0:T(8,128)S(1)} %get-tuple-element.25.a_ref, f32[24,3072]{1,0:T(8,128)S(1)} %collective-permute-done.7.b_ref, f32[24,3072]{1,0:T(8,128)S(1)} %collective-permute-done.8.c_ref, f32[24,3072]{1,0:T(8,128)S(1)} %collective-permute-done.9.d_ref), custom_call_target="tpu_custom_call" | custom-call | tf_op jit(solution)/shard_map/pallas_call | solution.py:373
  91.2 5.6 %all-to-all-done.2.whole_ref = f32[8,72,128]{2,1,0:T(8,128)S(1)} async-done(((f32[8,72,128]{2,1,0:T(8,128)}), f32[8,72,128]{2,1,0:T(8,128)S(1)}, u32[]{:S(2)}, u32[]{:S(2)}) %all-to-all-start.2) | async-done | bytes 294944 | tf_op jit(solution)/shard_map/all_to_all | solution.py:293
  96.9 1.1 %shard_map.61 = f32[9,24,288]{2,1,0:T(8,128)} custom-call(s32[1]{0:T(128)} %bitcast.4.layer_ref, f32[8,72,128]{2,1,0:T(8,128)S(1)} %all-to-all-done.2.whole_ref), custom_call_target="tpu_custom_call" | custom-call | tf_op jit(solution)/shard_map/pallas_call | solution.py:367
  (16 shorter events, 0.2 us)
Async XLA Ops:
  0.6 0.9 copy-start.1
  1.7 32.0 %collective-permute-start = (bf16[24,3072]{1,0:T(8,128)(2,1)S(1)}, bf16[24,3072]{1,0:T(8,128)(2,1)S(1)}, u32[]{:S(2)}, u32[]{:S(2)}) collective-permute-start(bf16[24,3072]{1,0:T(8,128)(2,1)S(1)} %shard_map.50.refs_1_.own_ref), channel_id=1, source_target_pairs={{0,4},{1,5},{2,6},{3,7},{4,8},{5,9},{6,10},{7,11},{8,0},{9,1},{10,... | collective-permute-start | bytes 442376 | tf_op jit(solution)/shard_map/ppermute | solution.py:312
  16.8 16.9 %collective-permute-start.1 = (bf16[24,3072]{1,0:T(8,128)(2,1)S(1)}, bf16[24,3072]{1,0:T(8,128)(2,1)S(1)}, u32[]{:S(2)}, u32[]{:S(2)}) collective-permute-start(bf16[24,3072]{1,0:T(8,128)(2,1)S(1)} %shard_map.50.refs_1_.own_ref), channel_id=1, source_target_pairs={{0,8},{1,9},{2,10},{3,11},{4,0},{5,1},{6,2},{7,3},{8,4},{9,5},{10,... | collective-permute-start | bytes 442376 | tf_op jit(solution)/shard_map/ppermute | solution.py:312
  18.8 0.9 copy-start.2
  19.9 21.7 %collective-permute-start.2 = (bf16[24,3072]{1,0:T(8,128)(2,1)S(1)}, bf16[24,3072]{1,0:T(8,128)(2,1)S(1)}, u32[]{:S(2)}, u32[]{:S(2)}) collective-permute-start(bf16[24,3072]{1,0:T(8,128)(2,1)S(1)} %shard_map.51.refs_6_), channel_id=1, source_target_pairs={{0,10},{1,11},{2,0},{3,1},{4,2},{5,3},{6,4},{7,5},{8,6},{9,7},{10,... | collective-permute-start | bytes 442376 | tf_op jit(solution)/shard_map/ppermute | solution.py:290
  27.2 14.4 %collective-permute-start.3 = (bf16[24,3072]{1,0:T(8,128)(2,1)S(1)}, bf16[24,3072]{1,0:T(8,128)(2,1)S(1)}, u32[]{:S(2)}, u32[]{:S(2)}) collective-permute-start(bf16[24,3072]{1,0:T(8,128)(2,1)S(1)} %shard_map.51.refs_6_), channel_id=1, source_target_pairs={{0,11},{1,0},{2,1},{3,2},{4,3},{5,4},{6,5},{7,6},{8,7},{9,8},{10,9... | collective-permute-start | bytes 442376 | tf_op jit(solution)/shard_map/ppermute | solution.py:312
  30.3 11.3 %collective-permute-start.4 = (bf16[24,3072]{1,0:T(8,128)(2,1)S(1)}, bf16[24,3072]{1,0:T(8,128)(2,1)S(1)}, u32[]{:S(2)}, u32[]{:S(2)}) collective-permute-start(bf16[24,3072]{1,0:T(8,128)(2,1)S(1)} %shard_map.51.refs_6_), channel_id=1, source_target_pairs={{0,1},{1,2},{2,3},{3,4},{4,5},{5,6},{6,7},{7,8},{8,9},{9,10},{10,1... | collective-permute-start | bytes 442376 | tf_op jit(solution)/shard_map/ppermute | solution.py:312
  34.1 9.3 %collective-permute-start.5 = (bf16[72,128]{1,0:T(8,128)(2,1)S(1)}, bf16[72,128]{1,0:T(8,128)(2,1)S(1)}, u32[]{:S(2)}, u32[]{:S(2)}) collective-permute-start(bf16[72,128]{1,0:T(8,128)(2,1)S(1)} %shard_map.53), channel_id=1, source_target_pairs={{0,12},{12,0},{24,36},{36,24},{48,60},{60,48},{72,84},{84,72},{96,... | collective-permute-start | bytes 55304 | tf_op jit(solution)/shard_map/ppermute | solution.py:317
  36.9 6.5 %collective-permute-start.6 = (bf16[72,128]{1,0:T(8,128)(2,1)S(1)}, bf16[72,128]{1,0:T(8,128)(2,1)S(1)}, u32[]{:S(2)}, u32[]{:S(2)}) collective-permute-start(bf16[72,128]{1,0:T(8,128)(2,1)S(1)} %shard_map.53), channel_id=1, source_target_pairs={{24,12},{48,36},{72,60},{96,84},{120,108},{144,132},{168,156},{192... | collective-permute-start | bytes 55304 | tf_op jit(solution)/shard_map/ppermute | solution.py:320
  45.9 13.3 %all-to-all-start = ((f32[8,72,128]{2,1,0:T(8,128)}), f32[8,72,128]{2,1,0:T(8,128)S(1)}, u32[]{:S(2)}, u32[]{:S(2)}) async-start(f32[8,72,128]{2,1,0:T(8,128)} %get-tuple-element.19), calls=%async_computation | async-start | bytes 589824 | tf_op jit(solution)/shard_map/all_to_all | solution.py:293
  54.6 0.9 copy-start
  57.4 0.7 copy-start.3
  59.2 4.7 %collective-permute-start.10 = (f32[1,72,128]{2,1,0:T(8,128)S(1)}, f32[1,72,128]{2,1,0:T(8,128)S(1)}, u32[]{:S(2)}, u32[]{:S(2)}) collective-permute-start(f32[1,72,128]{2,1,0:T(8,128)S(1)} %shard_map.55), channel_id=1, source_target_pairs={{0,11},{1,0},{2,1},{3,2},{4,3},{5,4},{6,5},{7,6},{8,7},{9,8},{10,9... | collective-permute-start | bytes 110600 | tf_op jit(solution)/shard_map/ppermute | solution.py:363
  64.7 15.9 %all-to-all-start.1 = ((f32[8,72,128]{2,1,0:T(8,128)}), f32[8,72,128]{2,1,0:T(8,128)S(1)}, u32[]{:S(2)}, u32[]{:S(2)}) async-start(f32[8,72,128]{2,1,0:T(8,128)} %shard_map.59), calls=%async_computation.1 | async-start | bytes 589824 | tf_op jit(solution)/shard_map/all_to_all | solution.py:293
  70.6 19.5 %collective-permute-start.7 = (f32[24,3072]{1,0:T(8,128)}, f32[24,3072]{1,0:T(8,128)S(1)}, u32[]{:S(2)}, u32[]{:S(2)}) collective-permute-start(f32[24,3072]{1,0:T(8,128)} %copy-done.3), channel_id=1, source_target_pairs={{0,2},{1,3},{2,4},{3,5},{4,6},{5,7},{6,8},{7,9},{8,10},{9,11},{10,... | collective-permute-start | bytes 884744 | tf_op jit(solution)/shard_map/ppermute | solution.py:312
  73.9 16.1 %collective-permute-start.8 = (f32[24,3072]{1,0:T(8,128)S(1)}, f32[24,3072]{1,0:T(8,128)S(1)}, u32[]{:S(2)}, u32[]{:S(2)}) collective-permute-start(f32[24,3072]{1,0:T(8,128)S(1)} %get-tuple-element.27), channel_id=1, source_target_pairs={{0,11},{1,0},{2,1},{3,2},{4,3},{5,4},{6,5},{7,6},{8,7},{9,8},{10,9... | collective-permute-start | bytes 884744 | tf_op jit(solution)/shard_map/ppermute | solution.py:312
  77.3 12.8 %collective-permute-start.9 = (f32[24,3072]{1,0:T(8,128)S(1)}, f32[24,3072]{1,0:T(8,128)S(1)}, u32[]{:S(2)}, u32[]{:S(2)}) collective-permute-start(f32[24,3072]{1,0:T(8,128)S(1)} %get-tuple-element.28), channel_id=1, source_target_pairs={{0,1},{1,2},{2,3},{3,4},{4,5},{5,6},{6,7},{7,8},{8,9},{9,10},{10,1... | collective-permute-start | bytes 884744 | tf_op jit(solution)/shard_map/ppermute | solution.py:312
  81.3 15.6 %all-to-all-start.2 = ((f32[8,72,128]{2,1,0:T(8,128)}), f32[8,72,128]{2,1,0:T(8,128)S(1)}, u32[]{:S(2)}, u32[]{:S(2)}) async-start(f32[8,72,128]{2,1,0:T(8,128)} %shard_map.60), calls=%async_computation.2 | async-start | bytes 589824 | tf_op jit(solution)/shard_map/all_to_all | solution.py:293
